TPU v7x, 256 devices: a whole 4x4x8 slice. The times are simulated.
256 devices in a mesh: seq: 32 (over z, y), head: 2 (over core), dp: 4 (over x).
Axes of the slice: x: 4, y: 4, z: 8, core: 2. Of those that a mesh axis runs over, the one named last changes fastest.
Arguments:
- series: bfloat16 [4, 16384, 768], P('dp', 'seq'), may hold values from -6 to 6
- norm_attn: float32 [768], replicated, may hold values from 0.1 to 1.9
- qkv_weight: bfloat16 [768, 3, 768], P(None, None, 'head'), may hold values from -0.21875 to 0.21875
- out_weight: bfloat16 [768, 768], P('head'), may hold values from -0.21875 to 0.21875
- norm_moe: float32 [768], replicated, may hold values from 0.1 to 1.9
- router_weight: bfloat16 [768, 128], replicated, may hold values from -0.21875 to 0.21875
- expert_ids: int32 [4, 16384, 1], P('dp', ('seq', 'head')), may hold values from 0 to 127; in each aligned block of 256 rows (0 to 255, 256 to 511, ..., all dimensions but the last counted through in order) at most 4 rows name the same one
- gate_weight: bfloat16 [128, 768, 3072], P(('seq', 'dp'), None, 'head'), may hold values from -0.21875 to 0.21875
- up_weight: bfloat16 [128, 768, 3072], P(('seq', 'dp'), None, 'head'), may hold values from -0.21875 to 0.21875
- down_weight: bfloat16 [128, 3072, 768], P(('seq', 'dp'), 'head'), may hold values from -0.109375 to 0.109375
Outputs:
- layer_out: bfloat16 [4, 16384, 768], P('dp', ('seq', 'head'))
Inputs may be any that keep to these rules, and one draw needn't show every extreme that they name: `expert_ids`: among the rows of one device (aligned blocks of 256 positions, counted over series and positions in order) at most 4 name the same expert, and in every draw some expert is named by exactly 4 rows of some device.
All inputs are finite; a program needn't handle non-finite values.
Results may differ from a plain program's by a relative error of at most 0.0041.
Values may be sent and summed in bfloat16 or wider, within the bound.
No kernel may reach another device: no remote copies, remote signals or barrier semaphores. Data moves between devices by JAX's collectives and lax.ppermute only.
A program may use at most 128 MiB of HBM per device.

v0:
```python
import jax
import jax.numpy as jnp
from jax import lax
from jax.sharding import Mesh
from jax.sharding import PartitionSpec as P

HD = 128
BLOCK = 512
SEQ = ("seq_0", "seq_1")
SEQ_DP = ("seq_0", "seq_1", "dp")
SEQ_HEAD = ("seq_0", "seq_1", "head")


NORM_EPS = 1e-06


def sent_together(arrays, axis, dim, along):
    both = jnp.concatenate(arrays, axis=along)
    out, at, gathered = (lax.all_gather(both, axis, axis=dim, tiled=True), 0, [])
    for a in arrays:
        gathered.append(lax.slice_in_dim(out, at, at + a.shape[along], axis=along))
        at += a.shape[along]
    return tuple(gathered)


def nothing_yet(shard, identity):
    return jnp.zeros_like(shard) + jnp.asarray(identity, shard.dtype)


def prefix_by_axis(shard, axes, combine, identity):
    before = start = nothing_yet(shard, identity)
    so_far = shard
    for axis in reversed(axes):
        peers, mine = (lax.axis_size(axis), lax.axis_index(axis))
        pieces = lax.all_gather(so_far, axis)
        inside, so_far = (start, start)
        for k in range(peers):
            passed = k < mine
            so_far = combine(so_far, pieces[k])
            inside = jnp.where(passed, so_far, inside)
        before = combine(inside, before)
    return before


def split_up(shard, dim, peers):
    lengths = shard.shape
    pieces = shard.reshape(*lengths[:dim], peers, lengths[dim] // peers, *lengths[dim + 1 :])
    return jnp.moveaxis(pieces, dim, 0)


def sum_at_owner(shard, axis, dim):
    pieces = split_up(shard, dim, lax.axis_size(axis))
    arrived = lax.all_to_all(pieces, axis, split_axis=0, concat_axis=0, tiled=True)
    return arrived.sum(axis=0)


def rms_scale(values, gain):
    values = values.astype(jnp.float32)
    return values * lax.rsqrt(jnp.mean(values * values, axis=-1, keepdims=True) + NORM_EPS) * gain


def add_states(earlier_sum, later_sum):
    return earlier_sum + later_sum


def on_device(
    series,
    norm_attn,
    qkv_weight,
    out_weight,
    norm_moe,
    router_weight,
    expert_ids,
    gate_weight,
    up_weight,
    down_weight,
):
    gate_full, up_full = sent_together((gate_weight, up_weight), "head", 2, 0)
    down_full = lax.all_gather(down_weight, "head", axis=1, tiled=True)
    tokens_here = series.shape[1]
    model_width = series.shape[2]
    local_heads = qkv_weight.shape[2] // HD
    block_count = tokens_here // BLOCK
    normed_in = rms_scale(series[0], norm_attn).astype(jnp.bfloat16)
    projected = jnp.dot(
        normed_in,
        qkv_weight.reshape(model_width, 3 * local_heads * HD),
        preferred_element_type=jnp.float32,
    ).astype(jnp.bfloat16)
    projected = projected.reshape(block_count, BLOCK, 3, local_heads, HD)
    queries = projected[:, :, 0]
    key_rows = projected[:, :, 1]
    value_rows = projected[:, :, 2]
    block_states = jnp.einsum(
        "bkhd,bkhe->bhde", key_rows, value_rows, preferred_element_type=jnp.float32
    )
    own_state = jnp.sum(block_states, axis=0)
    before = prefix_by_axis(own_state, SEQ, add_states, jnp.zeros_like(own_state))
    earlier_blocks = jnp.concatenate(
        [jnp.zeros_like(block_states), jnp.cumsum(block_states, axis=0)[:-1]], axis=0
    )
    states = before[None] + earlier_blocks
    causal = jnp.arange(BLOCK)[:, None] >= jnp.arange(BLOCK)[None, :]
    scores = jnp.einsum("bqhd,bkhd->bhqk", queries, key_rows, preferred_element_type=jnp.float32)
    scores = jnp.where(causal, scores, 0.0).astype(jnp.bfloat16)
    inside = jnp.einsum("bhqk,bkhd->bqhd", scores, value_rows, preferred_element_type=jnp.float32)
    carried = jnp.einsum(
        "bqhd,bhde->bqhe", queries.astype(jnp.float32), states, precision=lax.Precision.HIGHEST
    )
    offset = lax.axis_index(SEQ) * tokens_here
    position = (offset + jnp.arange(tokens_here, dtype=jnp.int32) + 1).astype(jnp.float32)
    position_scale = (position * jnp.sqrt(jnp.float32(HD))).reshape(block_count, BLOCK, 1, 1)
    mixed_heads = (
        ((inside + carried) / position_scale)
        .astype(jnp.bfloat16)
        .reshape(tokens_here, local_heads * HD)
    )
    own_rows = tokens_here // lax.axis_size("head")
    head_rank = lax.axis_index("head")
    attention = sum_at_owner(
        jnp.dot(mixed_heads, out_weight, preferred_element_type=jnp.float32), "head", 0
    )
    own_series = lax.dynamic_slice_in_dim(series[0], head_rank * own_rows, own_rows, 0).astype(
        jnp.float32
    )
    residual = own_series + attention
    normed_moe = rms_scale(residual, norm_moe).astype(jnp.bfloat16)
    route_ids = expert_ids[0, :, 0]
    expert_count = router_weight.shape[1]
    capacity = 2 * own_rows // expert_count
    logits = jnp.dot(normed_moe, router_weight, preferred_element_type=jnp.float32)
    picked_expert = route_ids[:, None] == jnp.arange(expert_count, dtype=jnp.int32)[None, :]
    gate_value = jax.nn.sigmoid(
        jnp.sum(jnp.where(picked_expert, logits, 0.0), axis=1, keepdims=True)
    )
    earlier = jnp.arange(own_rows)[None, :] < jnp.arange(own_rows)[:, None]
    same_expert = route_ids[:, None] == route_ids[None, :]
    slot_rank = jnp.sum(jnp.logical_and(same_expert, earlier), axis=1)
    slot_index = route_ids * capacity + slot_rank
    routing = (
        slot_index[:, None] == jnp.arange(expert_count * capacity, dtype=jnp.int32)[None, :]
    ).astype(jnp.bfloat16)
    send_buffer = lax.dot_general(
        routing, normed_moe, (((0,), (0,)), ((), ())), preferred_element_type=jnp.float32
    )
    send_buffer = send_buffer.astype(jnp.bfloat16).reshape(expert_count, capacity, model_width)
    received = lax.all_to_all(send_buffer, SEQ_DP, split_axis=0, concat_axis=0, tiled=True)
    flat_rows = received.reshape(-1, model_width)
    gate_proj = jnp.dot(flat_rows, gate_full[0], preferred_element_type=jnp.float32)
    up_proj = jnp.dot(flat_rows, up_full[0], preferred_element_type=jnp.float32)
    hidden = (jax.nn.silu(gate_proj) * up_proj).astype(jnp.bfloat16)
    expert_out = jnp.dot(hidden, down_full[0], preferred_element_type=jnp.float32)
    returned = lax.all_to_all(
        expert_out.astype(jnp.bfloat16).reshape(received.shape),
        SEQ_DP,
        split_axis=0,
        concat_axis=0,
        tiled=True,
    )
    routed = jnp.dot(
        routing,
        returned.reshape(expert_count * capacity, model_width),
        preferred_element_type=jnp.float32,
    )
    layer_out = (residual + gate_value * routed).astype(jnp.bfloat16)
    return layer_out[None]


def solution(mesh):
    split = Mesh(
        mesh.devices.reshape(8, 4, mesh.shape["head"], mesh.shape["dp"]),
        ("seq_0", "seq_1", "head", "dp"),
    )
    placed = (
        P("dp", SEQ, None),
        P(),
        P(None, None, "head"),
        P("head", None),
        P(),
        P(),
        P("dp", SEQ_HEAD, None),
        P(SEQ_DP, None, "head"),
        P(SEQ_DP, None, "head"),
        P(SEQ_DP, "head", None),
    )
    return jax.shard_map(
        on_device, mesh=split, in_specs=placed, out_specs=P("dp", SEQ_HEAD, None), check_vma=False
    )
```

profile of v0, /device:TPU:32, one launch (start us, length us, event | category | flops | bytes accessed | tf_op | source)
XLA Modules:
  0.0 181.3 jit_solution(5469764930400631546)
XLA Ops:
  6.5 0.0 all-gather.5.cloned.1.call-start
  6.5 2.7 %copy.31 = bf16[768,3,384]{0,2,1:T(8,128)(2,1)S(1)} copy(bf16[768,3,384]{2,0,1:T(8,128)(2,1)} %param.12) | data formatting | bytes 3538944 | tf_op args[2]
  9.3 0.0 copy-done.1
  9.3 0.2 fusion.3
  9.5 2.3 %convolution_convert_fusion = bf16[512,1152]{1,0:T(8,128)(2,1)} fusion(bf16[768,1152]{0,1:T(8,128)(2,1)S(1)} %bitcast.81, bf16[1,512,768]{2,1,0:T(8,128)(2,1)S(1)} %copy-done.1, f32[768]{0:T(1024)S(1)} %copy-done.8, f32[512]{0:T(512)S(1)} %add_rsqrt_fusion), kind=kOutput, calls=%fused_computation.8 | convolution fusion | flops 908132352 | bytes 3740672 | tf_op jit(solution)/shard_map/dot_general | solution.py:85
  11.8 1.6 copy.32
  13.4 0.3 fusion.26
  13.7 13.8 %all-gather = f32[12,128,128]{2,1,0:T(8,128)S(1)} all-gather(f32[3,128,128]{2,1,0:T(8,128)S(1)} %fusion.26), channel_id=2, replica_groups=mesh['seq_0'=8,'seq_1'=4,'head'=2,'dp'=4] {'seq_1'}, dimensions={0}, use_global_device_ids=true | all-gather | bytes 983040 | tf_op jit(solution)/shard_map/all_gather | solution.py:35
  27.5 0.7 fusion.35
  28.2 0.0 all-gather.5.cloned.1.call-update
  28.2 0.0 all-gather.7.cloned.1.call-start
  28.3 4.9 %pad_maximum_fusion = bf16[2,768,1536]{2,1,0:T(8,128)(2,1)} fusion(bf16[1,768,1536]{2,1,0:T(8,128)(2,1)} %param.18, bf16[1,768,1536]{2,1,0:T(8,128)(2,1)} %param.17), kind=kLoop, calls=%fused_computation.4 | loop fusion | flops 2359296 | bytes 9437184 | tf_op jit(solution)/shard_map/concatenate | solution.py:18
  33.2 0.0 all-gather.7.cloned.1.call-update
  33.2 0.0 copy-start.5
  33.2 0.0 copy-start.3
  33.3 0.0 all-gather.9.cloned.1.call-start
  33.3 0.7 all-gather.9.cloned.1.call-update
  34.0 0.1 iota_compare_fusion
  34.1 0.0 copy-done.5
  34.1 0.2 convert_reduce_fusion
  34.3 35.9 %all-gather.5.cloned.1.call-done = f32[8,3,128,128]{3,2,1,0:T(8,128)} async-done(((f32[1,3,128,128]{3,2,1,0:T(8,128)}), f32[8,3,128,128]{3,2,1,0:T(8,128)}) %all-gather.5.cloned.1.call-update) | async-done | bytes 1572880 | tf_op jit(solution)/shard_map/all_gather | solution.py:35
  70.2 2.9 %fusion.27 = f32[3,128,512]{2,1,0:T(8,128)} fusion(bf16[1,512,3,3,128]{1,4,3,2,0:T(8,128)(2,1)S(1)} %bitcast.83, f32[8,3,128,128]{3,2,1,0:T(8,128)} %all-gather.5.cloned.1.call-done, f32[1,3,128,128]{3,2,1,0:T(8,128)S(1)} %copy-done.3, f32[12,128,128]{2,1,0:T(8,128)S(1)} %all-gather, pred[]{:T(512)S(6)} %gt.45, pred[]{:T(512)S(6)} %gt.46, pred[]{:T(512)S(6)} %gt.47, ...), kind=kOutput, calls=%fused_computation.43 | convolution fusion | flops 303071232 | bytes 3538956 | tf_op jit(solution)/shard_map/bqhd,bhde->bqhe/dot_general | solution.py:107
  73.1 2.2 %fusion.18 = bf16[1,512,3,128]{1,3,2,0:T(8,128)(2,1)S(1)} fusion(f32[3,128,512]{2,1,0:T(8,128)} %fusion.27, pred[512,512]{1,0:T(8,128)(4,1)S(1)} %iota_compare_fusion, f32[512]{0:T(512)S(1)} %convert_multiply_fusion.2, bf16[1,512,3,3,128]{1,4,3,2,0:T(8,128)(2,1)S(1)} %bitcast.84), kind=kOutput, calls=%fused_computation.28 | convolution fusion | flops 404815872 | bytes 2623488 | tf_op jit(solution)/shard_map/bhqk,bkhd->bqhd/dot_general | solution.py:106
  75.3 0.1 dot_general.46
  75.4 0.6 fusion.23
  76.0 5.0 %all_to_all.15 = f32[2,256,768]{2,1,0:T(8,128)S(1)} all-to-all(f32[2,256,768]{2,1,0:T(8,128)S(1)} %fusion.23), channel_id=1, replica_groups=mesh['seq_0'=8,'seq_1'=4,'head'=2,'dp'=4] {'head'}, dimensions={0} | all-to-all | bytes 3145728 | tf_op jit(solution)/shard_map/all_to_all | solution.py:53
  81.0 0.2 reduce_sum.50
  81.2 1.2 multiply_reduce_fusion
  82.4 1.2 multiply_convert_fusion.1
  83.6 0.6 convolution_convert_fusion.1
  84.2 0.2 reshape.127
  84.4 37.3 %all_to_all.16 = bf16[128,4,768]{2,1,0:T(4,128)(2,1)S(1)} all-to-all(bf16[128,4,768]{2,1,0:T(4,128)(2,1)S(1)} %reshape.127), channel_id=1, replica_groups=mesh['seq_0'=8,'seq_1'=4,'head'=2,'dp'=4] {'seq_0','seq_1','dp'}, dimensions={0} | all-to-all | bytes 1572864 | tf_op jit(solution)/shard_map/all_to_all | solution.py:147
  121.7 0.2 reshape.128
  121.9 0.0 all-gather.7.cloned.1.call-done
  121.9 0.0 copy-start.7
  121.9 4.6 %fusion = f32[512,3072]{1,0:T(8,128)S(1)} fusion(bf16[512,768]{1,0:T(8,128)(2,1)S(1)} %reshape.128, bf16[2,768,3072]{2,1,0:T(8,128)(2,1)} %all-gather.7.cloned.1.call-done), kind=kOutput, calls=%fused_computation.3 | convolution fusion | flops 2415919104 | bytes 11796480 | tf_op jit(solution)/shard_map/dot_general | solution.py:149
  126.6 0.5 copy-done.7
  127.0 4.5 %multiply_convert_fusion = bf16[512,3072]{1,0:T(8,128)(2,1)} fusion(f32[512,3072]{1,0:T(8,128)S(1)} %fusion, bf16[512,768]{1,0:T(8,128)(2,1)S(1)} %reshape.128, bf16[2,768,3072]{2,1,0:T(8,128)(2,1)S(1)} %copy-done.7), kind=kOutput, calls=%fused_computation | convolution fusion | flops 2425356288 | bytes 14942208 | tf_op jit(solution)/shard_map/dot_general | solution.py:150
  131.6 5.9 %fusion.7 = bf16[512,768]{1,0:T(8,128)(2,1)S(1)} fusion(bf16[512,3072]{1,0:T(8,128)(2,1)} %multiply_convert_fusion, bf16[1,3072,768]{2,1,0:T(8,128)(2,1)} %all-gather.9.cloned.1.call-done), kind=kOutput, calls=%fused_computation.15 | convolution fusion | flops 2416312320 | bytes 8650752 | tf_op jit(solution)/shard_map/dot_general | solution.py:152
  137.5 0.0 copy-start.4
  137.5 0.0 copy-start.2
  137.5 1.1 reshape.129
  138.6 7.2 %all-to-all-start.2 = ((bf16[128,4,768]{2,1,0:T(4,128)(2,1)}), bf16[128,4,768]{2,1,0:T(4,128)(2,1)S(1)}, u32[]{:S(2)}, u32[]{:S(2)}) async-start(bf16[128,4,768]{2,1,0:T(4,128)(2,1)} %reshape.129), calls=%async_computation.2 | async-start | bytes 1572864 | tf_op jit(solution)/shard_map/all_to_all | solution.py:153
  145.7 0.3 fusion.15
  146.1 25.3 %all-to-all-done.2 = bf16[128,4,768]{2,1,0:T(4,128)(2,1)S(1)} async-done(((bf16[128,4,768]{2,1,0:T(4,128)(2,1)}), bf16[128,4,768]{2,1,0:T(4,128)(2,1)S(1)}, u32[]{:S(2)}, u32[]{:S(2)}) %all-to-all-start.2) | async-done | bytes 786464 | tf_op jit(solution)/shard_map/all_to_all | solution.py:153
  171.4 1.1 reshape.130
  172.5 0.0 copy-done.2
  172.5 2.3 %fusion.14 = bf16[1,256,768]{2,1,0:T(8,128)(2,1)} fusion(bf16[512,768]{1,0:T(8,128)(2,1)} %reshape.130, f32[256]{0:T(256)S(1)} %add_divide_fusion, s32[256]{0:T(256)S(1)} %multiply_add_fusion, f32[256,768]{1,0:T(8,128)S(1)} %reduce_sum.50, bf16[1,512,768]{2,1,0:T(8,128)(2,1)S(1)} %copy-done.2, s32[]{:T(128)S(6)} %select_n.98), kind=kOutput, calls=%fused_computation.22 | convolution fusion | flops 202440704 | bytes 2361348 | tf_op jit(solution)/shard_map/dot_general | solution.py:160
  (15 shorter events, 0.1 us)
Async XLA Ops:
  6.5 68.9 %copy-start = (bf16[384,768]{1,0:T(8,128)(2,1)S(1)}, bf16[384,768]{1,0:T(8,128)(2,1)}, u32[]{:S(2)}) copy-start(bf16[384,768]{1,0:T(8,128)(2,1)} %param.13) | copy-start | bytes 1769476
  6.5 2.8 %copy-start.1 = (bf16[1,512,768]{2,1,0:T(8,128)(2,1)S(1)}, bf16[1,512,768]{2,1,0:T(8,128)(2,1)}, u32[]{:S(2)}) copy-start(bf16[1,512,768]{2,1,0:T(8,128)(2,1)} %param.10) | copy-start | bytes 2359300
  6.5 3.0 %copy-start.8 = (f32[768]{0:T(1024)S(1)}, f32[768]{0:T(1024)}, u32[]{:S(2)}) copy-start(f32[768]{0:T(1024)} %param.11) | copy-start | bytes 9220
  6.5 63.7 %all-gather.5.cloned.1.call-start = ((), (), s32[]{:S(2)}) async-start(), calls=%async_computation.3 | async-start | bytes 1769472 | tf_op jit(solution)/shard_map/all_gather | solution.py:35
  28.2 93.7 %all-gather.7.cloned.1.call-start = ((), (), s32[]{:S(2)}) async-start(), calls=%async_computation.4 | async-start | bytes 14155776 | tf_op jit(solution)/shard_map/all_gather | solution.py:19
  33.2 0.9 copy-start.5
  33.2 37.0 %copy-start.3 = (f32[1,3,128,128]{3,2,1,0:T(8,128)S(1)}, f32[1,3,128,128]{3,2,1,0:T(8,128)}, u32[]{:S(2)}) copy-start(f32[1,3,128,128]{3,2,1,0:T(8,128)} %fusion.35) | copy-start | bytes 589828
  33.3 98.3 %all-gather.9.cloned.1.call-start = ((), (), s32[]{:S(2)}) async-start(), calls=%async_computation.5 | async-start | bytes 7077888 | tf_op jit(solution)/shard_map/all_gather | solution.py:79
  81.0 1.4 copy-start.6
  121.9 5.1 %copy-start.7 = (bf16[2,768,3072]{2,1,0:T(8,128)(2,1)S(1)}, bf16[2,768,3072]{2,1,0:T(8,128)(2,1)}, u32[]{:S(2)}) copy-start(bf16[2,768,3072]{2,1,0:T(8,128)(2,1)} %all-gather.7.cloned.1.call-done) | copy-start | bytes 28311556
  137.5 8.3 %copy-start.4 = (bf16[768,128]{1,0:T(8,128)(2,1)S(1)}, bf16[768,128]{1,0:T(8,128)(2,1)}, u32[]{:S(2)}) copy-start(bf16[768,128]{1,0:T(8,128)(2,1)} %param.15) | copy-start | bytes 589828
  137.5 35.0 %copy-start.2 = (bf16[1,512,768]{2,1,0:T(8,128)(2,1)S(1)}, bf16[1,512,768]{2,1,0:T(8,128)(2,1)}, u32[]{:S(2)}) copy-start(bf16[1,512,768]{2,1,0:T(8,128)(2,1)} %param.10) | copy-start | bytes 2359300
  138.6 32.8 %all-to-all-start.2 = ((bf16[128,4,768]{2,1,0:T(4,128)(2,1)}), bf16[128,4,768]{2,1,0:T(4,128)(2,1)S(1)}, u32[]{:S(2)}, u32[]{:S(2)}) async-start(bf16[128,4,768]{2,1,0:T(4,128)(2,1)} %reshape.129), calls=%async_computation.2 | async-start | bytes 1572864 | tf_op jit(solution)/shard_map/all_to_all | solution.py:153
Sparse Core Ops, SparseCore 0:
  28.3 41.8 all-gather.4
  72.0 25.9 all-gather.6
  99.8 21.0 all-gather.8
where the time goes:
time: 182 us; the launch traced here: 181 us
  waiting for transfers between devices  61.9 us (34%)
  blocking collectives  56.2 us (31%)
  matrix products  26.4 us (15%)
  between operations  13.4 us (7%)
  other arithmetic  8.72 us (5%)
  local copies, waits for them, and re-layouts  7.4 us (4%)
  starting transfers between devices  7.25 us (4%)
    all_to_all x1, blocking collectives, on_device(): lax.all_to_all(send_buffer, SEQ_DP, split_axis=0, concat_axis=0, tiled=True)  37.3 us
    all_gather x1, waiting for transfers between devices, prefix_by_axis(): pieces = lax.all_gather(so_far, axis)  35.9 us
    all_to_all x1, waiting for transfers between devices, on_device(): lax.all_to_all(expert_out.astype(jnp.bfloat16).reshape(received.shape), S...  25.3 us
    all_gather x1, blocking collectives, prefix_by_axis(): pieces = lax.all_gather(so_far, axis)  13.8 us
    all_to_all x1, starting transfers between devices, on_device(): lax.all_to_all(expert_out.astype(jnp.bfloat16).reshape(received.shape), S...  7.17 us
    dot_general x1, matrix products, on_device(): jnp.dot(hidden, down_full[0], preferred_element_type=jnp.float32)  5.89 us
    all_to_all x1, blocking collectives, sum_at_owner(): lax.all_to_all(pieces, axis, split_axis=0, concat_axis=0, tiled=True)  5 us
    concatenate x1, other arithmetic, sent_together(): both = jnp.concatenate(arrays, axis=along)  4.93 us
  transfers between devices with their start and end apart: 4, of which 2 were waited for; matrix products, arithmetic and copies ran while one was open for 13% of the time, Pallas kernels for 0%

commit v1 on v0

v1 whole, which is shorter than its diff:
```python
import jax
import jax.numpy as jnp
from jax import lax
from jax.experimental import pallas as pl
from jax.experimental.pallas import tpu as pltpu
from jax.sharding import Mesh
from jax.sharding import PartitionSpec as P

HD = 128
BLOCK = 512
SEQ = ("seq_0", "seq_1")
SEQ_DP = ("seq_0", "seq_1", "dp")
SEQ_HEAD = ("seq_0", "seq_1", "head")
NORM_EPS = 1e-06
FF_BLOCK = 512


def rms_scale(values, gain):
    values = values.astype(jnp.float32)
    return values * lax.rsqrt(jnp.mean(values * values, axis=-1, keepdims=True) + NORM_EPS) * gain


def from_partner(shard):
    return lax.ppermute(shard, "head", [(0, 1), (1, 0)])


def exchange(pieces, axes):
    return lax.all_to_all(pieces, axes, split_axis=0, concat_axis=0, tiled=True)


def expert_kernel(blocks, rows, gate_a, up_a, down_a, gate_b, up_b, down_b, out, total):
    step = pl.program_id(0)

    def add_part(gate, up, down):
        x = rows[...]
        g = jnp.dot(x, gate[...], preferred_element_type=jnp.float32)
        u = jnp.dot(x, up[...], preferred_element_type=jnp.float32)
        hidden = (g / (1.0 + jnp.exp(-g)) * u).astype(jnp.bfloat16)
        return jnp.dot(hidden, down[...], preferred_element_type=jnp.float32)

    @pl.when(step == 0)
    def _():
        total[...] = add_part(gate_a, up_a, down_a)

    @pl.when(jnp.logical_and(step > 0, step < blocks))
    def _():
        total[...] += add_part(gate_a, up_a, down_a)

    @pl.when(step >= blocks)
    def _():
        total[...] += add_part(gate_b, up_b, down_b)

    @pl.when(step == 2 * blocks - 1)
    def _():
        out[...] = total[...].astype(out.dtype)


def expert_of(rows, own, partner):
    count, width = rows.shape
    units = own[0].shape[1]
    blocks = units // FF_BLOCK

    def first(step):
        return jnp.minimum(step, blocks - 1)

    def second(step):
        return jnp.maximum(step - blocks, 0)

    def specs(place):
        return [
            pl.BlockSpec((width, FF_BLOCK), lambda i: (0, place(i))),
            pl.BlockSpec((width, FF_BLOCK), lambda i: (0, place(i))),
            pl.BlockSpec((FF_BLOCK, width), lambda i: (place(i), 0)),
        ]

    return pl.pallas_call(
        lambda *refs: expert_kernel(blocks, *refs),
        grid=(2 * blocks,),
        in_specs=[pl.BlockSpec((count, width), lambda i: (0, 0))] + specs(first) + specs(second),
        out_specs=pl.BlockSpec((count, width), lambda i: (0, 0)),
        out_shape=jax.ShapeDtypeStruct((count, width), jnp.bfloat16),
        scratch_shapes=[pltpu.VMEM((count, width), jnp.float32)],
        compiler_params=pltpu.CompilerParams(
            dimension_semantics=("arbitrary",), vmem_limit_bytes=48 * 1024 * 1024
        ),
        cost_estimate=pl.CostEstimate(
            flops=2 * count * width * units * 6,
            bytes_accessed=12 * width * units,
            transcendentals=2 * count * units,
        ),
        name="expert_mlp",
    )(rows, *own, *partner)


def on_device(
    series,
    norm_attn,
    qkv_weight,
    out_weight,
    norm_moe,
    router_weight,
    expert_ids,
    gate_weight,
    up_weight,
    down_weight,
):
    rows_all = series.shape[1]
    width = series.shape[2]
    head_count = lax.axis_size("head")
    half = qkv_weight.shape[2]
    heads = half // HD
    own_rows = rows_all // head_count
    head_rank = lax.axis_index("head")
    seq_rank = lax.axis_index(SEQ)
    seq_size = lax.axis_size(SEQ)

    qkv_other = from_partner(qkv_weight)
    out_other = from_partner(out_weight)
    own_expert = (gate_weight[0], up_weight[0], down_weight[0])
    other_expert = tuple(from_partner(w) for w in own_expert)

    normed_in = rms_scale(series[0], norm_attn).astype(jnp.bfloat16)
    kv_own = jnp.dot(
        normed_in, qkv_weight[:, 1:].reshape(width, 2 * half), preferred_element_type=jnp.float32
    ).astype(jnp.bfloat16)
    keys_own, values_own = kv_own[:, :half], kv_own[:, half:]
    state = jnp.concatenate(
        [
            lax.dot_general(
                keys_own[:, n * HD : (n + 1) * HD],
                values_own[:, n * HD : (n + 1) * HD],
                (((0,), (0,)), ((), ())),
                preferred_element_type=jnp.float32,
            )
            for n in range(heads)
        ],
        axis=1,
    ).astype(jnp.bfloat16)
    lines = HD // seq_size
    pieces = exchange(state.reshape(seq_size, lines, half), SEQ)
    earlier = (jnp.arange(seq_size)[:, None] > jnp.arange(seq_size)[None, :]).astype(jnp.float32)
    before = lax.dot_general(
        earlier,
        pieces.astype(jnp.float32),
        (((1,), (0,)), ((), ())),
        precision=lax.Precision.HIGHEST,
        preferred_element_type=jnp.float32,
    ).astype(jnp.bfloat16)
    before = jnp.broadcast_to(before[:, None], (seq_size, head_count, lines, half))
    states = exchange(before.reshape(seq_size * head_count, lines, half), SEQ_HEAD)
    states = jnp.moveaxis(states.reshape(seq_size, head_count, lines, half), 1, 0)
    states = states.reshape(head_count, HD, half)
    state_own = jnp.where(head_rank == 0, states[0], states[1])
    state_other = jnp.where(head_rank == 0, states[1], states[0])

    first_row = head_rank * own_rows
    normed_own = lax.dynamic_slice_in_dim(normed_in, first_row, own_rows, 0)
    kv_other = jnp.dot(
        normed_in, qkv_other[:, 1:].reshape(width, 2 * half), preferred_element_type=jnp.float32
    ).astype(jnp.bfloat16)
    block_row = first_row + jnp.arange(own_rows)
    causal = block_row[:, None] >= jnp.arange(rows_all)[None, :]
    position = (seq_rank * rows_all + block_row + 1).astype(jnp.float32)
    scale = (position * jnp.sqrt(jnp.float32(HD)))[:, None]

    def attend(weight, kv, start_state):
        queries = jnp.dot(normed_own, weight[:, 0], preferred_element_type=jnp.float32).astype(
            jnp.bfloat16
        )
        mixed = []
        for n in range(heads):
            at = slice(n * HD, (n + 1) * HD)
            scores = lax.dot_general(
                queries[:, at],
                kv[:, :half][:, at],
                (((1,), (1,)), ((), ())),
                preferred_element_type=jnp.float32,
            )
            scores = jnp.where(causal, scores, 0.0).astype(jnp.bfloat16)
            inside = jnp.dot(scores, kv[:, half:][:, at], preferred_element_type=jnp.float32)
            carried = jnp.dot(
                queries[:, at], start_state[:, at], preferred_element_type=jnp.float32
            )
            mixed.append(((inside + carried) / scale).astype(jnp.bfloat16))
        return jnp.concatenate(mixed, axis=1)

    mixed_own = attend(qkv_weight, kv_own, state_own)
    mixed_other = attend(qkv_other, kv_other, state_other)
    attention = jnp.dot(mixed_own, out_weight, preferred_element_type=jnp.float32) + jnp.dot(
        mixed_other, out_other, preferred_element_type=jnp.float32
    )
    own_series = lax.dynamic_slice_in_dim(series[0], first_row, own_rows, 0).astype(jnp.float32)
    residual = own_series + attention
    normed_moe = rms_scale(residual, norm_moe).astype(jnp.bfloat16)

    route_ids = expert_ids[0, :, 0]
    expert_count = router_weight.shape[1]
    capacity = 2 * own_rows // expert_count
    logits = jnp.dot(normed_moe, router_weight, preferred_element_type=jnp.float32)
    picked_expert = route_ids[:, None] == jnp.arange(expert_count, dtype=jnp.int32)[None, :]
    gate_value = jax.nn.sigmoid(
        jnp.sum(jnp.where(picked_expert, logits, 0.0), axis=1, keepdims=True)
    )
    earlier_row = jnp.arange(own_rows)[None, :] < jnp.arange(own_rows)[:, None]
    same_expert = route_ids[:, None] == route_ids[None, :]
    slot_rank = jnp.sum(jnp.logical_and(same_expert, earlier_row), axis=1)
    slot_index = route_ids * capacity + slot_rank
    routing = (
        slot_index[:, None] == jnp.arange(expert_count * capacity, dtype=jnp.int32)[None, :]
    ).astype(jnp.bfloat16)
    send_buffer = lax.dot_general(
        routing, normed_moe, (((0,), (0,)), ((), ())), preferred_element_type=jnp.float32
    )
    send_buffer = send_buffer.astype(jnp.bfloat16).reshape(expert_count, capacity, width)
    received = exchange(send_buffer, SEQ_DP)
    expert_out = expert_of(received.reshape(-1, width), own_expert, other_expert)
    returned = exchange(expert_out.reshape(received.shape), SEQ_DP)
    routed = jnp.dot(
        routing,
        returned.reshape(expert_count * capacity, width),
        preferred_element_type=jnp.float32,
    )
    layer_out = (residual + gate_value * routed).astype(jnp.bfloat16)
    return layer_out[None]


def solution(mesh):
    split = Mesh(
        mesh.devices.reshape(8, 4, mesh.shape["head"], mesh.shape["dp"]),
        ("seq_0", "seq_1", "head", "dp"),
    )
    placed = (
        P("dp", SEQ, None),
        P(),
        P(None, None, "head"),
        P("head", None),
        P(),
        P(),
        P("dp", SEQ_HEAD, None),
        P(SEQ_DP, None, "head"),
        P(SEQ_DP, None, "head"),
        P(SEQ_DP, "head", None),
    )
    return jax.shard_map(
        on_device, mesh=split, in_specs=placed, out_specs=P("dp", SEQ_HEAD, None), check_vma=False
    )
```

time: 182 us -> 166 us (0.912)
  waiting for transfers between devices: 61.9 us -> 39.4 us
  blocking collectives: 56.2 us -> 34.6 us
  starting transfers between devices: 7.25 us -> 24.1 us
  between operations: 13.4 us -> 0.33 us
  Pallas kernels: 0 us -> 11.8 us
  local copies, waits for them, and re-layouts: 7.4 us -> 17.2 us
  matrix products: 26.4 us -> 33.3 us
  other arithmetic: 8.72 us -> 3.7 us
    all_gather x3 -> x0, waiting for transfers between devices: 35.9 us -> none  [the longest x1 35.9 us: prefix_by_axis(): pieces = lax.all_gather(so_far, axis)]
    all_to_all x1 -> x3, starting transfers between devices: 7.17 us -> 23 us  [exchange(): return lax.all_to_all(pieces, axes, split_axis=0, concat_axis=0, tiled=True)]
    all_to_all x1 -> x3, waiting for transfers between devices: 25.3 us -> 39.4 us  [exchange(): return lax.all_to_all(pieces, axes, split_axis=0, concat_axis=0, tiled=True)]
    all_gather x1 -> x0, blocking collectives: 13.8 us -> none  [prefix_by_axis(): pieces = lax.all_gather(so_far, axis)]
    pallas_call x0 -> x1, Pallas kernels: none -> 11.8 us  [expert_of(): pl.pallas_call(lambda *refs: expert_kernel(blocks, *refs), grid=(2 * bloc...]
    all_to_all x2 -> x1, blocking collectives: 42.3 us -> 34.6 us  [exchange(): return lax.all_to_all(pieces, axes, split_axis=0, concat_axis=0, tiled=True)]
    dot_general x9 -> x23, matrix products: 25.6 us -> 31.4 us  [the longest x6 10.6 us: attend(): jnp.dot(scores, kv[:, half:][:, at], preferred_element_type=jnp.float32)]
    concatenate x1, other arithmetic: 4.93 us -> 0.69 us  [on_device(): jnp.concatenate([lax.dot_general(keys_own[:, n * HD:(n + 1) * HD], values...]
  transfers between devices with their start and end apart: 4 -> 8, of which waited for: 2 -> 3; matrix products, arithmetic and copies ran while one was open for 13% -> 30% of each run, Pallas kernels for 0% -> 0%
where the time goes in v1:
time: 166 us; the launch traced here: 164 us
  waiting for transfers between devices  39.4 us (24%)
  blocking collectives  34.6 us (21%)
  matrix products  33.3 us (20%)
  starting transfers between devices  24.1 us (15%)
  local copies, waits for them, and re-layouts  17.2 us (10%)
  Pallas kernels  11.8 us (7%)
  other arithmetic  3.7 us (2%)
    all_to_all x3, waiting for transfers between devices, exchange(): return lax.all_to_all(pieces, axes, split_axis=0, concat_axis=0, tiled=True)  39.4 us
    all_to_all x1, blocking collectives, exchange(): return lax.all_to_all(pieces, axes, split_axis=0, concat_axis=0, tiled=True)  34.6 us
    all_to_all x3, starting transfers between devices, exchange(): return lax.all_to_all(pieces, axes, split_axis=0, concat_axis=0, tiled=True)  23 us
    pallas_call x1, Pallas kernels, expert_of(): pl.pallas_call(lambda *refs: expert_kernel(blocks, *refs), grid=(2 * bloc...  11.8 us
    dot_general x6, matrix products, attend(): jnp.dot(scores, kv[:, half:][:, at], preferred_element_type=jnp.float32)  10.6 us
    dot_general x6, matrix products, attend(): jnp.dot(queries[:, at], start_state[:, at], preferred_element_type=jnp.fl...  7.89 us
    unnamed x33, local copies, waits for them, and re-layouts  6.62 us
    dot_general x2, matrix products, attend(): jnp.dot(normed_own, weight[:, 0], preferred_element_type=jnp.float32)  3.89 us
  transfers between devices with their start and end apart: 8, of which 3 were waited for; matrix products, arithmetic and copies ran while one was open for 30% of the time, Pallas kernels for 0%

profile of v1, /device:TPU:32, one launch (start us, length us, event | category | flops | bytes accessed | tf_op | source)
XLA Modules:
  0.0 164.5 jit_solution(4352611403730971920)
XLA Ops:
  0.0 3.9 %copy.25 = bf16[768,3,384]{0,2,1:T(8,128)(2,1)} copy(bf16[768,3,384]{2,0,1:T(8,128)(2,1)} %param.12) | data formatting | bytes 3538944 | tf_op args[2]
  3.9 0.5 collective-permute-start
  4.4 1.3 slice.163
  5.7 0.2 multiply_reduce_fusion
  6.0 0.8 convolution_convert_fusion.1
  7.3 0.4 copy-done.15
  8.0 0.7 pad_maximum_fusion
  8.7 11.4 %all-to-all-start = ((bf16[32,4,384]{2,1,0:T(4,128)(2,1)}), bf16[32,4,384]{2,1,0:T(4,128)(2,1)S(1)}, u32[]{:S(2)}, u32[]{:S(2)}) async-start(bf16[32,4,384]{2,1,0:T(4,128)(2,1)} %pad_maximum_fusion), calls=%async_computation | async-start | bytes 196608 | tf_op jit(solution)/shard_map/all_to_all | solution.py:28
  20.1 0.5 collective-permute-start.3
  20.7 1.2 convert_bitcast_fusion
  22.2 7.2 %all-to-all-done = bf16[32,4,384]{2,1,0:T(4,128)(2,1)S(1)} async-done(((bf16[32,4,384]{2,1,0:T(4,128)(2,1)}), bf16[32,4,384]{2,1,0:T(4,128)(2,1)S(1)}, u32[]{:S(2)}, u32[]{:S(2)}) %all-to-all-start) | async-done | bytes 98336 | tf_op jit(solution)/shard_map/all_to_all | solution.py:28
  29.6 0.7 broadcast_in_dim.18
  30.3 5.2 %all-to-all-start.1 = ((bf16[64,4,384]{2,1,0:T(4,128)(2,1)}), bf16[64,4,384]{2,1,0:T(4,128)(2,1)S(1)}, u32[]{:S(2)}, u32[]{:S(2)}) async-start(bf16[64,4,384]{2,1,0:T(4,128)(2,1)} %bitcast.50), calls=%async_computation.1 | async-start | bytes 393216 | tf_op jit(solution)/shard_map/all_to_all | solution.py:28
  35.5 0.6 iota_add_fusion
  36.2 0.6 copy-done.10
  36.8 2.4 %convolution_convert_fusion.4 = bf16[256,384]{1,0:T(8,128)(2,1)} fusion(bf16[768,3,384]{2,0,1:T(8,128)(2,1)} %param.12, f32[512,768]{1,0:T(8,128)} %convert_bitcast_fusion, s32[]{:T(128)S(6)} %select_n.45, f32[768]{0:T(1024)} %param.11, f32[256]{0:T(256)S(1)} %dynamic-slice.1), kind=kOutput, calls=%fused_computation.27 | convolution fusion | flops 151683072 | bytes 1577988 | tf_op jit(solution)/shard_map/dot_general | solution.py:167
  39.2 7.8 %all-to-all-done.1 = bf16[64,4,384]{2,1,0:T(4,128)(2,1)S(1)} async-done(((bf16[64,4,384]{2,1,0:T(4,128)(2,1)}), bf16[64,4,384]{2,1,0:T(4,128)(2,1)S(1)}, u32[]{:S(2)}, u32[]{:S(2)}) %all-to-all-start.1) | async-done | bytes 196640 | tf_op jit(solution)/shard_map/all_to_all | solution.py:28
  47.0 0.7 broadcast_select_fusion
  47.8 0.9 select_n.54
  48.7 0.9 select_n.49
  49.6 1.7 %fusion.107 = f32[256,128]{0,1:T(8,128)} fusion(bf16[256,384]{1,0:T(8,128)(2,1)} %convolution_convert_fusion.4, bf16[128,384]{1,0:T(8,128)(2,1)S(1)} %select_n.49), kind=kOutput, calls=%fused_computation.129 | convolution fusion | flops 8388608 | bytes 229376 | tf_op jit(solution)/shard_map/dot_general | solution.py:181
  51.3 1.7 %fusion.111 = f32[256,128]{0,1:T(8,128)} fusion(bf16[256,384]{1,0:T(8,128)(2,1)} %convolution_convert_fusion.4, bf16[128,384]{1,0:T(8,128)(2,1)S(1)} %select_n.49), kind=kOutput, calls=%fused_computation.132 | convolution fusion | flops 8388608 | bytes 229376 | tf_op jit(solution)/shard_map/dot_general | solution.py:181
  53.0 1.7 %fusion.115 = f32[256,128]{0,1:T(8,128)} fusion(bf16[256,384]{1,0:T(8,128)(2,1)} %convolution_convert_fusion.4, bf16[128,384]{1,0:T(8,128)(2,1)S(1)} %select_n.49), kind=kOutput, calls=%fused_computation.135 | convolution fusion | flops 8388608 | bytes 229376 | tf_op jit(solution)/shard_map/dot_general | solution.py:181
  54.7 1.5 fusion.32
  56.2 2.1 %fusion.31 = bf16[256,128]{0,1:T(8,128)(2,1)} fusion(f32[256,128]{0,1:T(8,128)} %fusion.111, s32[256]{0:T(256)} %iota_add_fusion, bf16[512,768]{1,0:T(8,128)(2,1)} %copy-done.15, f32[256]{0:T(256)S(1)} %convert_multiply_fusion.1, bf16[256,384]{1,0:T(8,128)(2,1)} %convolution_convert_fusion.4), kind=kOutput, calls=%fused_computation.49 | convolution fusion | flops 67600384 | bytes 526336 | tf_op jit(solution)/shard_map/dot_general | solution.py:180
  58.3 2.1 %fusion.30 = bf16[256,128]{0,1:T(8,128)(2,1)} fusion(f32[256,128]{0,1:T(8,128)} %fusion.115, s32[256]{0:T(256)} %iota_add_fusion, bf16[512,768]{1,0:T(8,128)(2,1)} %copy-done.15, f32[256]{0:T(256)S(1)} %convert_multiply_fusion.1, bf16[256,384]{1,0:T(8,128)(2,1)} %convolution_convert_fusion.4), kind=kOutput, calls=%fused_computation.48 | convolution fusion | flops 67600384 | bytes 526336 | tf_op jit(solution)/shard_map/dot_general | solution.py:180
  60.4 2.5 %fusion.59 = f32[256,768]{1,0:T(8,128)} fusion(bf16[384,768]{1,0:T(8,128)(2,1)} %param.13, bf16[256,128]{0,1:T(8,128)(2,1)S(1)} %fusion.32, bf16[256,128]{0,1:T(8,128)(2,1)} %fusion.31, bf16[256,128]{0,1:T(8,128)(2,1)} %fusion.30), kind=kOutput, calls=%fused_computation.86 | convolution fusion | flops 151584768 | bytes 1572864 | tf_op jit(solution)/shard_map/dot_general | solution.py:189
  63.0 1.5 convolution_convert_fusion.3
  64.5 0.9 fusion.103
  65.3 0.9 fusion.99
  66.2 1.3 slice.179
  67.6 1.7 %convolution_convert_fusion = bf16[512,768]{1,0:T(8,128)(2,1)} fusion(bf16[768,768]{0,1:T(8,128)(2,1)S(1)} %bitcast.48, bf16[1,512,768]{2,1,0:T(8,128)(2,1)S(1)} %copy-done.5, f32[768]{0:T(1024)S(1)} %copy-done.13, f32[512]{0:T(512)S(1)} %add_rsqrt_fusion), kind=kOutput, calls=%fused_computation.5 | convolution fusion | flops 605945856 | bytes 2757632 | tf_op jit(solution)/shard_map/dot_general | solution.py:158
  69.3 1.5 fusion.33
  70.8 1.1 fusion.95
  71.8 1.5 fusion.34
  73.3 2.0 %fusion.35 = bf16[256,128]{0,1:T(8,128)(2,1)} fusion(f32[256,128]{0,1:T(8,128)S(1)} %fusion.95, s32[256]{0:T(256)S(1)} %copy-done.14, bf16[512,768]{1,0:T(8,128)(2,1)} %convolution_convert_fusion, f32[256]{0:T(256)S(1)} %convert_multiply_fusion.1, bf16[256,384]{1,0:T(8,128)(2,1)} %copy-done.7), kind=kOutput, calls=%fused_computation.53 | convolution fusion | flops 67600384 | bytes 526336 | tf_op jit(solution)/shard_map/dot_general | solution.py:180
  75.3 1.9 %multiply_reduce_fusion.1 = (f32[256]{0:T(256)S(1)}, f32[256,768]{1,0:T(8,128)S(1)}) fusion(f32[256,768]{1,0:T(8,128)} %fusion.59, bf16[384,768]{1,0:T(8,128)(2,1)} %collective-permute-done.1, bf16[256,128]{0,1:T(8,128)(2,1)} %fusion.35, bf16[256,128]{0,1:T(8,128)(2,1)S(1)} %fusion.34, bf16[256,128]{0,1:T(8,128)(2,1)S(1)} %fusion.33, ...), kind=kOutput, calls=%fused_computation.63 | convolution fusion | flops 152567552 | bytes 2753540 | tf_op jit(solution)/shard_map/dot_general | solution.py:189
  77.3 1.5 convolution_convert_fusion.2
  78.8 2.4 %reshape.124 = bf16[128,4,768]{2,1,0:T(4,128)(2,1)} reshape(bf16[512,768]{1,0:T(8,128)(2,1)} %convolution_convert_fusion.2) | data formatting | bytes 1572864 | tf_op jit(solution)/shard_map/reshape | solution.py:214
  81.2 34.6 %all_to_all.20 = bf16[128,4,768]{2,1,0:T(4,128)(2,1)} all-to-all(bf16[128,4,768]{2,1,0:T(4,128)(2,1)} %reshape.124), channel_id=1, replica_groups=mesh['seq_0'=8,'seq_1'=4,'head'=2,'dp'=4] {'seq_0','seq_1','dp'}, dimensions={0} | all-to-all | bytes 1572864 | tf_op jit(solution)/shard_map/all_to_all | solution.py:28
  115.9 1.6 reshape.125.refs_0_
  117.5 1.7 %copy-done.2 = bf16[1,768,1536]{2,1,0:T(8,128)(2,1)S(1)} copy-done((bf16[1,768,1536]{2,1,0:T(8,128)(2,1)S(1)}, bf16[1,768,1536]{2,1,0:T(8,128)(2,1)}, u32[]{:S(2)}) %copy-start.2) | copy-done | bytes 2359320
  119.1 11.8 %expert_mlp.1 = bf16[512,768]{1,0:T(8,128)(2,1)S(1)} custom-call(bf16[512,768]{1,0:T(8,128)(2,1)S(1)} %reshape.125.refs_0_, bf16[768,1536]{1,0:T(8,128)(2,1)S(1)} %bitcast.46, bf16[768,1536]{1,0:T(8,128)(2,1)} %bitcast.58, bf16[1536,768]{1,0:T(8,128)(2,1)} %bitcast.60, bf16[768,1536]{1,0:T(8,128)(2,1)} %collective-permute-done.2.refs_4_, ...), custom_call_target="tpu_custom_call" | custom-call | flops 7247757312 | bytes 14155776 | tf_op jit(solution)/shard_map/expert_mlp/pallas_call | solution.py:76
  130.9 1.1 reshape.126
  132.0 6.4 %all-to-all-start.3 = ((bf16[128,4,768]{2,1,0:T(4,128)(2,1)}), bf16[128,4,768]{2,1,0:T(4,128)(2,1)S(1)}, u32[]{:S(2)}, u32[]{:S(2)}) async-start(bf16[128,4,768]{2,1,0:T(4,128)(2,1)} %reshape.126), calls=%async_computation.3 | async-start | bytes 1572864 | tf_op jit(solution)/shard_map/all_to_all | solution.py:28
  138.4 0.4 fusion.36
  138.8 24.3 %all-to-all-done.3 = bf16[128,4,768]{2,1,0:T(4,128)(2,1)S(1)} async-done(((bf16[128,4,768]{2,1,0:T(4,128)(2,1)}), bf16[128,4,768]{2,1,0:T(4,128)(2,1)S(1)}, u32[]{:S(2)}, u32[]{:S(2)}) %all-to-all-start.3) | async-done | bytes 786464 | tf_op jit(solution)/shard_map/all_to_all | solution.py:28
  163.3 1.2 fusion.5
  (50 shorter events, 1.6 us)
Async XLA Ops:
  0.0 138.4 %copy-start = (bf16[768,128]{1,0:T(8,128)(2,1)S(1)}, bf16[768,128]{1,0:T(8,128)(2,1)}, u32[]{:S(2)}) copy-start(bf16[768,128]{1,0:T(8,128)(2,1)} %param.15) | copy-start | bytes 589828
  0.0 75.3 %collective-permute-start.1 = (bf16[384,768]{1,0:T(8,128)(2,1)}, bf16[384,768]{1,0:T(8,128)(2,1)}, u32[]{:S(2)}, u32[]{:S(2)}) collective-permute-start(bf16[384,768]{1,0:T(8,128)(2,1)} %param.13), channel_id=1, source_target_pairs={{0,4},{4,0},{1,5},{5,1},{2,6},{6,2},{3,7},{7,3},{8,12},{12,8},{9,1... | collective-permute-start | bytes 1769480 | tf_op jit(solution)/shard_map/ppermute | solution.py:24
  3.9 1.8 %copy-start.5 = (bf16[1,512,768]{2,1,0:T(8,128)(2,1)S(1)}, bf16[1,512,768]{2,1,0:T(8,128)(2,1)}, u32[]{:S(2)}) copy-start(bf16[1,512,768]{2,1,0:T(8,128)(2,1)} %param.10) | copy-start | bytes 2359300
  3.9 2.1 %copy-start.12 = (f32[768]{0:T(1024)S(1)}, f32[768]{0:T(1024)}, u32[]{:S(2)}) copy-start(f32[768]{0:T(1024)} %param.11) | copy-start | bytes 9220
  3.9 59.0 %collective-permute-start = (bf16[768,3,384]{0,2,1:T(8,128)(2,1)}, bf16[768,3,384]{0,2,1:T(8,128)(2,1)}, u32[]{:S(2)}, u32[]{:S(2)}) collective-permute-start(bf16[768,3,384]{0,2,1:T(8,128)(2,1)} %copy.25), channel_id=1, source_target_pairs={{0,4},{4,0},{1,5},{5,1},{2,6},{6,2},{3,7},{7,3},{8,12},{12,8},{9,1... | collective-permute-start | bytes 5308424 | tf_op jit(solution)/shard_map/ppermute | solution.py:24
  6.0 14.1 %copy-start.1 = (bf16[1,768,1536]{2,1,0:T(8,128)(2,1)S(1)}, bf16[1,768,1536]{2,1,0:T(8,128)(2,1)}, u32[]{:S(2)}) copy-start(bf16[1,768,1536]{2,1,0:T(8,128)(2,1)} %param.17) | copy-start | bytes 7077892
  6.8 0.9 copy-start.15
  7.7 14.2 %copy-start.9 = (s32[1,256,1]{1,2,0:T(1,128)S(1)}, s32[1,256,1]{1,2,0:T(1,128)}, u32[]{:S(2)}) copy-start(s32[1,256,1]{1,2,0:T(1,128)} %param.16) | copy-start | bytes 3076
  8.7 20.7 %all-to-all-start = ((bf16[32,4,384]{2,1,0:T(4,128)(2,1)}), bf16[32,4,384]{2,1,0:T(4,128)(2,1)S(1)}, u32[]{:S(2)}, u32[]{:S(2)}) async-start(bf16[32,4,384]{2,1,0:T(4,128)(2,1)} %pad_maximum_fusion), calls=%async_computation | async-start | bytes 196608 | tf_op jit(solution)/shard_map/all_to_all | solution.py:28
  20.0 97.4 %collective-permute-start.2 = (bf16[768,1536]{1,0:T(8,128)(2,1)S(1)}, bf16[768,1536]{1,0:T(8,128)(2,1)}, u32[]{:S(2)}, u32[]{:S(2)}) collective-permute-start(bf16[768,1536]{1,0:T(8,128)(2,1)S(1)} %bitcast.45), channel_id=1, source_target_pairs={{0,4},{4,0},{1,5},{5,1},{2,6},{6,2},{3,7},{7,3},{8,12},{12,8},{9,1... | collective-permute-start | bytes 7077896 | tf_op jit(solution)/shard_map/ppermute | solution.py:24
  20.1 97.3 %collective-permute-start.3 = (bf16[768,1536]{1,0:T(8,128)(2,1)}, bf16[768,1536]{1,0:T(8,128)(2,1)}, u32[]{:S(2)}, u32[]{:S(2)}) collective-permute-start(bf16[768,1536]{1,0:T(8,128)(2,1)} %bitcast.57), channel_id=1, source_target_pairs={{0,4},{4,0},{1,5},{5,1},{2,6},{6,2},{3,7},{7,3},{8,12},{12,8},{9,1... | collective-permute-start | bytes 7077896 | tf_op jit(solution)/shard_map/ppermute | solution.py:24
  20.6 96.8 %collective-permute-start.4 = (bf16[1536,768]{1,0:T(8,128)(2,1)}, bf16[1536,768]{1,0:T(8,128)(2,1)}, u32[]{:S(2)}, u32[]{:S(2)}) collective-permute-start(bf16[1536,768]{1,0:T(8,128)(2,1)} %bitcast.59), channel_id=1, source_target_pairs={{0,4},{4,0},{1,5},{5,1},{2,6},{6,2},{3,7},{7,3},{8,12},{12,8},{9,1... | collective-permute-start | bytes 7077896 | tf_op jit(solution)/shard_map/ppermute | solution.py:24
  30.3 16.7 %all-to-all-start.1 = ((bf16[64,4,384]{2,1,0:T(4,128)(2,1)}), bf16[64,4,384]{2,1,0:T(4,128)(2,1)S(1)}, u32[]{:S(2)}, u32[]{:S(2)}) async-start(bf16[64,4,384]{2,1,0:T(4,128)(2,1)} %bitcast.50), calls=%async_computation.1 | async-start | bytes 393216 | tf_op jit(solution)/shard_map/all_to_all | solution.py:28
  36.2 0.6 copy-start.10
  58.3 4.7 %copy-start.11 = (f32[256]{0:T(256)S(1)}, f32[256]{0:T(256)}, u32[]{:S(2)}) copy-start(f32[256]{0:T(256)} %copy-done.10) | copy-start | bytes 3076
  58.3 4.7 %copy-start.13 = (f32[768]{0:T(1024)S(1)}, f32[768]{0:T(1024)}, u32[]{:S(2)}) copy-start(f32[768]{0:T(1024)} %param.11) | copy-start | bytes 9220
  60.4 2.6 %copy-start.6 = (f32[512,768]{1,0:T(8,128)S(1)}, f32[512,768]{1,0:T(8,128)}, u32[]{:S(2)}) copy-start(f32[512,768]{1,0:T(8,128)} %convert_bitcast_fusion) | copy-start | bytes 4718596
  64.5 0.9 copy-start.7
  67.6 1.7 %copy-start.14 = (s32[256]{0:T(256)S(1)}, s32[256]{0:T(256)}, u32[]{:S(2)}) copy-start(s32[256]{0:T(256)} %iota_add_fusion) | copy-start | bytes 3076
  75.3 2.0 %copy-start.8 = (f32[768]{0:T(1024)S(1)}, f32[768]{0:T(1024)}, u32[]{:S(2)}) copy-start(f32[768]{0:T(1024)} %param.14) | copy-start | bytes 9220
  77.3 4.0 %copy-start.3 = (f32[256,768]{1,0:T(8,128)}, f32[256,768]{1,0:T(8,128)S(1)}, u32[]{:S(2)}) copy-start(f32[256,768]{1,0:T(8,128)S(1)} %get-tuple-element.8) | copy-start | bytes 2359300
  117.5 1.7 %copy-start.2 = (bf16[1,768,1536]{2,1,0:T(8,128)(2,1)S(1)}, bf16[1,768,1536]{2,1,0:T(8,128)(2,1)}, u32[]{:S(2)}) copy-start(bf16[1,768,1536]{2,1,0:T(8,128)(2,1)} %param.17) | copy-start | bytes 7077892
  130.9 7.5 %copy-start.4 = (f32[256,768]{1,0:T(8,128)S(1)}, f32[256,768]{1,0:T(8,128)}, u32[]{:S(2)}) copy-start(f32[256,768]{1,0:T(8,128)} %copy-done.3) | copy-start | bytes 2359300
  132.0 31.1 %all-to-all-start.3 = ((bf16[128,4,768]{2,1,0:T(4,128)(2,1)}), bf16[128,4,768]{2,1,0:T(4,128)(2,1)S(1)}, u32[]{:S(2)}, u32[]{:S(2)}) async-start(bf16[128,4,768]{2,1,0:T(4,128)(2,1)} %reshape.126), calls=%async_computation.3 | async-start | bytes 1572864 | tf_op jit(solution)/shard_map/all_to_all | solution.py:28

commit v2 on v1

v2 whole, which is shorter than its diff:
```python
import math

import jax
import jax.numpy as jnp
from jax import lax
from jax.experimental import pallas as pl
from jax.experimental.pallas import tpu as pltpu
from jax.sharding import Mesh
from jax.sharding import PartitionSpec as P

HD = 128
BLOCK = 512
SEQ = ("seq_0", "seq_1")
SEQ_DP = ("seq_0", "seq_1", "dp")
SEQ_HEAD = ("seq_0", "seq_1", "head")
NORM_EPS = 1e-06
FF_BLOCK = 512
MIB = 1024 * 1024


def from_partner(shard):
    return lax.ppermute(shard, "head", [(0, 1), (1, 0)])


def exchange(pieces, axes):
    return lax.all_to_all(pieces, axes, split_axis=0, concat_axis=0, tiled=True)


def expert_kernel(blocks, rows, gate_a, up_a, down_a, gate_b, up_b, down_b, out, total):
    step = pl.program_id(0)

    def add_part(gate, up, down):
        x = rows[...]
        g = jnp.dot(x, gate[...], preferred_element_type=jnp.float32)
        u = jnp.dot(x, up[...], preferred_element_type=jnp.float32)
        hidden = (g * (0.5 + 0.5 * jnp.tanh(0.5 * g)) * u).astype(jnp.bfloat16)
        return jnp.dot(hidden, down[...], preferred_element_type=jnp.float32)

    @pl.when(step == 0)
    def _():
        total[...] = add_part(gate_a, up_a, down_a)

    @pl.when(jnp.logical_and(step > 0, step < blocks))
    def _():
        total[...] += add_part(gate_a, up_a, down_a)

    @pl.when(step >= blocks)
    def _():
        total[...] += add_part(gate_b, up_b, down_b)

    @pl.when(step == 2 * blocks - 1)
    def _():
        out[...] = total[...].astype(out.dtype)


def expert_of(rows, own, partner):
    count, width = rows.shape
    units = own[0].shape[1]
    blocks = units // FF_BLOCK

    def first(step):
        return jnp.minimum(step, blocks - 1)

    def second(step):
        return jnp.maximum(step - blocks, 0)

    def specs(place):
        return [
            pl.BlockSpec((width, FF_BLOCK), lambda i: (0, place(i))),
            pl.BlockSpec((width, FF_BLOCK), lambda i: (0, place(i))),
            pl.BlockSpec((FF_BLOCK, width), lambda i: (place(i), 0)),
        ]

    return pl.pallas_call(
        lambda *refs: expert_kernel(blocks, *refs),
        grid=(2 * blocks,),
        in_specs=[pl.BlockSpec((count, width), lambda i: (0, 0))] + specs(first) + specs(second),
        out_specs=pl.BlockSpec((count, width), lambda i: (0, 0)),
        out_shape=jax.ShapeDtypeStruct((count, width), jnp.bfloat16),
        scratch_shapes=[pltpu.VMEM((count, width), jnp.float32)],
        compiler_params=pltpu.CompilerParams(
            dimension_semantics=("arbitrary",), vmem_limit_bytes=32 * MIB
        ),
        cost_estimate=pl.CostEstimate(
            flops=2 * count * width * units * 6,
            bytes_accessed=12 * width * units,
            transcendentals=2 * count * units,
        ),
        name="expert_mlp",
    )(rows, *(in_hbm(w) for w in own), *(in_hbm(w) for w in partner))


def in_hbm(array):
    return pltpu.with_memory_space_constraint(array, pltpu.HBM)


def normed_rows(rows, gain):
    x = rows.astype(jnp.float32)
    mean = jnp.sum(x * x, axis=-1, keepdims=True) * (1.0 / x.shape[1])
    return x * lax.rsqrt(mean + NORM_EPS) * gain


def state_kernel(series, weight, gain, state_out, rows, table, sems):
    half = table.shape[2]
    fetch_rows = pltpu.make_async_copy(series, rows, sems.at[0])
    fetch_keys = pltpu.make_async_copy(weight.at[1], table.at[0], sems.at[1])
    fetch_values = pltpu.make_async_copy(weight.at[2], table.at[1], sems.at[2])
    fetch_rows.start()
    fetch_keys.start()
    fetch_values.start()
    fetch_rows.wait()
    normed = normed_rows(rows[...], gain[...]).astype(jnp.bfloat16)
    fetch_keys.wait()
    keys = jnp.dot(normed, table[0], preferred_element_type=jnp.float32).astype(jnp.bfloat16)
    fetch_values.wait()
    values = jnp.dot(normed, table[1], preferred_element_type=jnp.float32).astype(jnp.bfloat16)
    heads = half // HD
    for n in range(heads):
        at = slice(n * HD, (n + 1) * HD)
        state_out[at, :] = lax.dot_general(
            keys[:, at], values[:, at], (((0,), (0,)), ((), ())), preferred_element_type=jnp.float32
        ).astype(jnp.bfloat16)
    state_out[heads * HD :, :] = jnp.zeros((HD, HD), jnp.bfloat16)


def block_state(series, weight, gain):
    count, width = series.shape
    half = weight.shape[2]
    return pl.pallas_call(
        state_kernel,
        in_specs=[
            pl.BlockSpec(memory_space=pl.ANY),
            pl.BlockSpec(memory_space=pl.ANY),
            pl.BlockSpec(memory_space=pltpu.VMEM),
        ],
        out_specs=pl.BlockSpec(memory_space=pltpu.VMEM),
        out_shape=jax.ShapeDtypeStruct((half + HD, HD), jnp.bfloat16),
        scratch_shapes=[
            pltpu.VMEM((count, width), jnp.bfloat16),
            pltpu.VMEM((2, width, half), jnp.bfloat16),
            pltpu.SemaphoreType.DMA((3,)),
        ],
        compiler_params=pltpu.CompilerParams(vmem_limit_bytes=24 * MIB),
        cost_estimate=pl.CostEstimate(
            flops=4 * count * width * half, bytes_accessed=4 * count * width, transcendentals=count
        ),
        name="block_state",
    )(in_hbm(series), in_hbm(weight), gain)


def prefix_kernel(pieces, out):
    total = jnp.zeros(pieces.shape[1:], jnp.float32)
    for k in range(pieces.shape[0]):
        rounded = total.astype(jnp.bfloat16)
        out[k, 0] = rounded
        out[k, 1] = rounded
        total = total + pieces[k].astype(jnp.float32)


def prefix(pieces):
    count, lines, lanes = pieces.shape
    return pl.pallas_call(
        prefix_kernel,
        in_specs=[pl.BlockSpec(memory_space=pltpu.VMEM)],
        out_specs=pl.BlockSpec(memory_space=pltpu.VMEM),
        out_shape=jax.ShapeDtypeStruct((count, 2, lines, lanes), jnp.bfloat16),
        compiler_params=pltpu.CompilerParams(vmem_limit_bytes=4 * MIB),
        cost_estimate=pl.CostEstimate(
            flops=count * lines * lanes, bytes_accessed=6 * count * lines * lanes, transcendentals=0
        ),
        name="prefix",
    )(pieces)


def inside_kernel(series, gain, w_own, w_other, queries_out, inside_out):
    count, _ = series.shape
    own_rows = queries_out.shape[0]
    half = w_own.shape[2]
    heads = half // HD
    first_row = pl.multiple_of(lax.axis_index("head") * own_rows, own_rows)
    mine = normed_rows(series[pl.ds(first_row, own_rows), :], gain[...]).astype(jnp.bfloat16)
    normed = normed_rows(series[...], gain[...]).astype(jnp.bfloat16)
    row = lax.broadcasted_iota(jnp.int32, (own_rows, count), 0) + first_row
    causal = row >= lax.broadcasted_iota(jnp.int32, (own_rows, count), 1)
    for part, weight in ((0, w_own), (1, w_other)):
        queries, keys, values = (
            jnp.dot(rows, weight[k], preferred_element_type=jnp.float32).astype(jnp.bfloat16)
            for k, rows in ((0, mine), (1, normed), (2, normed))
        )
        queries_out[:, part * half : (part + 1) * half] = queries
        for n in range(heads):
            at = slice(n * HD, (n + 1) * HD)
            scores = lax.dot_general(
                queries[:, at],
                keys[:, at],
                (((1,), (1,)), ((), ())),
                preferred_element_type=jnp.float32,
            )
            scores = jnp.where(causal, scores, 0.0).astype(jnp.bfloat16)
            lanes = slice(part * half + n * HD, part * half + (n + 1) * HD)
            inside_out[:, lanes] = jnp.dot(
                scores, values[:, at], preferred_element_type=jnp.float32
            )


def inside_block(series, gain, w_own, w_other, own_rows):
    count, width = series.shape
    half = w_own.shape[2]
    return pl.pallas_call(
        inside_kernel,
        in_specs=[pl.BlockSpec(memory_space=pltpu.VMEM)] * 4,
        out_specs=[pl.BlockSpec(memory_space=pltpu.VMEM)] * 2,
        out_shape=[
            jax.ShapeDtypeStruct((own_rows, 2 * half), jnp.bfloat16),
            jax.ShapeDtypeStruct((own_rows, 2 * half), jnp.float32),
        ],
        compiler_params=pltpu.CompilerParams(vmem_limit_bytes=24 * MIB),
        cost_estimate=pl.CostEstimate(
            flops=10 * count * width * half + 8 * own_rows * count * half,
            bytes_accessed=8 * count * width,
            transcendentals=0,
        ),
        name="inside_block",
    )(series, gain, w_own, w_other)


def mix_kernel(
    queries,
    inside,
    states,
    out_own,
    out_other,
    series,
    gain,
    slots,
    residual_out,
    normed_out,
    send_out,
    queries_in,
    inside_in,
    weights_in,
    rows_in,
    residual_held,
    normed_held,
    sems,
):
    own_rows, width = rows_in.shape
    half = out_own.shape[0]
    heads = half // HD
    head_rank = lax.axis_index("head")
    first_row = pl.multiple_of(head_rank * own_rows, own_rows)
    fetches = [
        pltpu.make_async_copy(queries, queries_in, sems.at[0]),
        pltpu.make_async_copy(inside, inside_in, sems.at[1]),
        pltpu.make_async_copy(out_own, weights_in.at[0], sems.at[2]),
        pltpu.make_async_copy(out_other, weights_in.at[1], sems.at[3]),
        pltpu.make_async_copy(series.at[pl.ds(first_row, own_rows)], rows_in, sems.at[4]),
    ]
    for fetch in fetches:
        fetch.start()
    base = lax.axis_index(SEQ) * series.shape[0] + first_row + 1
    position = lax.broadcasted_iota(jnp.int32, (own_rows, HD), 0) + base
    unit = 1.0 / (position.astype(jnp.float32) * math.sqrt(HD))
    slot = lax.broadcasted_iota(jnp.int32, (send_out.shape[0], own_rows), 0)
    chosen = jnp.where(slot == slots[...], 1.0, 0.0).astype(jnp.bfloat16)
    per_head = HD // states.shape[2]
    fetches[0].wait()
    fetches[1].wait()
    mixed = []
    for part in range(2):
        rank = head_rank if part == 0 else 1 - head_rank
        for n in range(heads):
            lanes = slice(part * half + n * HD, part * half + (n + 1) * HD)
            start = states[n * per_head : (n + 1) * per_head, rank].reshape(HD, HD)
            carried = jnp.dot(queries_in[:, lanes], start, preferred_element_type=jnp.float32)
            mixed.append(((inside_in[:, lanes] + carried) * unit).astype(jnp.bfloat16))
    fetches[2].wait()
    total = jnp.dot(
        jnp.concatenate(mixed[:heads], axis=1), weights_in[0], preferred_element_type=jnp.float32
    )
    fetches[3].wait()
    total += jnp.dot(
        jnp.concatenate(mixed[heads:], axis=1), weights_in[1], preferred_element_type=jnp.float32
    )
    fetches[4].wait()
    total += rows_in[...].astype(jnp.float32)
    residual_held[...] = total
    keep_residual = pltpu.make_async_copy(residual_held, residual_out, sems.at[5])
    keep_residual.start()
    normed = normed_rows(total, gain[...]).astype(jnp.bfloat16)
    normed_held[...] = normed
    keep_normed = pltpu.make_async_copy(normed_held, normed_out, sems.at[6])
    keep_normed.start()
    send_out[...] = jnp.dot(chosen, normed, preferred_element_type=jnp.float32).astype(
        jnp.bfloat16
    )
    keep_residual.wait()
    keep_normed.wait()


def mix_heads(queries, inside, states, out_own, out_other, series, gain, slots, slot_count):
    own_rows, width = queries.shape
    half = out_own.shape[0]
    anywhere = pl.BlockSpec(memory_space=pl.ANY)
    local = pl.BlockSpec(memory_space=pltpu.VMEM)
    return pl.pallas_call(
        mix_kernel,
        in_specs=[anywhere, anywhere, local, anywhere, anywhere, anywhere, local, local],
        out_specs=[anywhere, anywhere, local],
        out_shape=[
            pltpu.HBM((own_rows, width), jnp.float32),
            pltpu.HBM((own_rows, width), jnp.bfloat16),
            jax.ShapeDtypeStruct((slot_count, width), jnp.bfloat16),
        ],
        scratch_shapes=[
            pltpu.VMEM((own_rows, width), jnp.bfloat16),
            pltpu.VMEM((own_rows, width), jnp.float32),
            pltpu.VMEM((2, half, width), jnp.bfloat16),
            pltpu.VMEM((own_rows, width), jnp.bfloat16),
            pltpu.VMEM((own_rows, width), jnp.float32),
            pltpu.VMEM((own_rows, width), jnp.bfloat16),
            pltpu.SemaphoreType.DMA((7,)),
        ],
        compiler_params=pltpu.CompilerParams(vmem_limit_bytes=24 * MIB),
        cost_estimate=pl.CostEstimate(
            flops=2 * own_rows * width * (width + HD + slot_count),
            bytes_accessed=12 * own_rows * width,
            transcendentals=own_rows,
        ),
        name="mix_heads",
    )(
        in_hbm(queries),
        in_hbm(inside),
        states,
        in_hbm(out_own),
        in_hbm(out_other),
        in_hbm(series),
        gain,
        slots,
    )


def on_device(
    series,
    norm_attn,
    qkv_weight,
    out_weight,
    norm_moe,
    router_weight,
    expert_ids,
    gate_weight,
    up_weight,
    down_weight,
):
    width = series.shape[2]
    head_count = lax.axis_size("head")
    seq_size = lax.axis_size(SEQ)
    own_rows = series.shape[1] // head_count

    qkv_own = jnp.moveaxis(qkv_weight, 1, 0)
    qkv_other = from_partner(qkv_own)
    out_other = from_partner(out_weight)
    own_expert = (gate_weight[0], up_weight[0], down_weight[0])
    other_expert = tuple(from_partner(w) for w in own_expert)

    state = block_state(series[0], qkv_own, norm_attn[None])
    pieces = exchange(state.reshape(seq_size, state.shape[0] // seq_size, HD), SEQ)
    before = prefix(pieces)
    states = exchange(before.reshape(seq_size * head_count, *before.shape[2:]), SEQ_HEAD)
    queries, inside = inside_block(series[0], norm_attn[None], qkv_own, qkv_other, own_rows)

    route_ids = expert_ids[0, :, 0]
    expert_count = router_weight.shape[1]
    capacity = 2 * own_rows // expert_count
    earlier_row = jnp.arange(own_rows)[None, :] < jnp.arange(own_rows)[:, None]
    same_expert = route_ids[:, None] == route_ids[None, :]
    slot_rank = jnp.sum(jnp.logical_and(same_expert, earlier_row), axis=1)
    slot_index = route_ids * capacity + slot_rank

    residual, normed_moe, send_buffer = mix_heads(
        queries,
        inside,
        states.reshape(before.shape),
        out_weight,
        out_other,
        series[0],
        norm_moe[None],
        slot_index[None, :],
        expert_count * capacity,
    )
    received = exchange(send_buffer.reshape(expert_count, capacity, width), SEQ_DP)

    logits = jnp.dot(normed_moe, router_weight, preferred_element_type=jnp.float32)
    picked_expert = route_ids[:, None] == jnp.arange(expert_count, dtype=jnp.int32)[None, :]
    gate_value = jax.nn.sigmoid(
        jnp.sum(jnp.where(picked_expert, logits, 0.0), axis=1, keepdims=True)
    )
    expert_out = expert_of(received.reshape(-1, width), own_expert, other_expert)
    returned = exchange(expert_out.reshape(received.shape), SEQ_DP)
    routing = (
        slot_index[:, None] == jnp.arange(expert_count * capacity, dtype=jnp.int32)[None, :]
    ).astype(jnp.bfloat16)
    routed = jnp.dot(
        routing,
        returned.reshape(expert_count * capacity, width),
        preferred_element_type=jnp.float32,
    )
    layer_out = (residual + gate_value * routed).astype(jnp.bfloat16)
    return layer_out[None]


def solution(mesh):
    split = Mesh(
        mesh.devices.reshape(8, 4, mesh.shape["head"], mesh.shape["dp"]),
        ("seq_0", "seq_1", "head", "dp"),
    )
    placed = (
        P("dp", SEQ, None),
        P(),
        P(None, None, "head"),
        P("head", None),
        P(),
        P(),
        P("dp", SEQ_HEAD, None),
        P(SEQ_DP, None, "head"),
        P(SEQ_DP, None, "head"),
        P(SEQ_DP, "head", None),
    )
    return jax.shard_map(
        on_device, mesh=split, in_specs=placed, out_specs=P("dp", SEQ_HEAD, None), check_vma=False
    )
```

time: 166 us -> 129 us (0.78)
  matrix products: 33.3 us -> 0.74 us
  local copies, waits for them, and re-layouts: 17.2 us -> 4.18 us
  Pallas kernels: 11.8 us -> 24.7 us
  other arithmetic: 3.7 us -> 1.02 us
    dot_general x23 -> x0, matrix products: 31.8 us -> none  [the longest x6 10.6 us: attend(): jnp.dot(scores, kv[:, half:][:, at], preferred_element_type=jnp.float32)]
    pallas_call x0 -> x4, Pallas kernels: none -> 12.8 us  [the longest x1 5.12 us: inside_block(): pl.pallas_call(inside_kernel, in_specs=[pl.BlockSpec(memory_space=pltpu.V...]
    unnamed x33 -> x18, local copies, waits for them, and re-layouts: 6.62 us -> 1.72 us
    slice x2 -> x0, local copies, waits for them, and re-layouts: 2.69 us -> none  [the longest x1 1.35 us: on_device(): qkv_other[:, 1:].reshape(width, 2 * half)]
    reshape x1, local copies, waits for them, and re-layouts: 2.41 us -> 0.18 us  [on_device(): send_buffer.reshape(expert_count, capacity, width)]
    select_n x2 -> x0, local copies, waits for them, and re-layouts: 1.84 us -> none  [the longest x1 0.92 us: on_device(): state_own = jnp.where(head_rank == 0, states[0], states[1])]
  transfers between devices with their start and end apart: 8 -> 8, of which waited for: 3 -> 3; matrix products, arithmetic and copies ran while one was open for 30% -> 1% of each run, Pallas kernels for 0% -> 10%
where the time goes in v2:
time: 129 us; the launch traced here: 128 us
  waiting for transfers between devices  38.7 us (30%)
  blocking collectives  34.6 us (27%)
  Pallas kernels  24.7 us (19%)
  starting transfers between devices  24.2 us (19%)
  local copies, waits for them, and re-layouts  4.18 us (3%)
    all_to_all x3, waiting for transfers between devices, exchange(): return lax.all_to_all(pieces, axes, split_axis=0, concat_axis=0, tiled=True)  38.7 us
    all_to_all x1, blocking collectives, exchange(): return lax.all_to_all(pieces, axes, split_axis=0, concat_axis=0, tiled=True)  34.6 us
    all_to_all x3, starting transfers between devices, exchange(): return lax.all_to_all(pieces, axes, split_axis=0, concat_axis=0, tiled=True)  23 us
    pallas_call x1, Pallas kernels, expert_of(): pl.pallas_call(lambda *refs: expert_kernel(blocks, *refs), grid=(2 * bloc...  12 us
    pallas_call x1, Pallas kernels, inside_block(): pl.pallas_call(inside_kernel, in_specs=[pl.BlockSpec(memory_space=pltpu.V...  5.12 us
    pallas_call x1, Pallas kernels, block_state(): pl.pallas_call(state_kernel, in_specs=[pl.BlockSpec(memory_space=pl.ANY),...  3.49 us
    pallas_call x1, Pallas kernels, mix_heads(): pl.pallas_call(mix_kernel, in_specs=[anywhere, anywhere, local, anywhere,...  3.4 us
  transfers between devices with their start and end apart: 8, of which 3 were waited for; matrix products, arithmetic and copies ran while one was open for 1% of the time, Pallas kernels for 10%

profile of v2, /device:TPU:32, one launch (start us, length us, event | category | flops | bytes accessed | tf_op | source)
XLA Modules:
  0.0 128.5 jit_solution(4434819718004961626)
XLA Ops:
  0.0 0.0 copy-start
  0.0 0.0 copy-start.2
  0.0 0.0 copy-start.1
  0.0 0.0 copy-start.8
  0.0 0.0 copy-start.7
  0.0 0.1 collective-permute-start
  0.1 0.8 broadcast_in_dim.10.gain
  1.0 3.5 %block_state.1 = bf16[512,128]{1,0:T(8,128)(2,1)} custom-call(bf16[512,768]{1,0:T(8,128)(2,1)} %bitcast.17, bf16[3,768,384]{2,1,0:T(8,128)(2,1)} %bitcast.21, f32[1,768]{1,0:T(1,128)S(1)} %broadcast_in_dim.10.gain), custom_call_target="tpu_custom_call" | custom-call | flops 603979776 | bytes 1572864 | tf_op jit(solution)/shard_map/block_state/pallas_call | solution.py:129
  4.5 11.4 %all-to-all-start = ((bf16[32,16,128]{2,1,0:T(8,128)(2,1)}), bf16[32,16,128]{2,1,0:T(8,128)(2,1)S(1)}, u32[]{:S(2)}, u32[]{:S(2)}) async-start(bf16[32,16,128]{2,1,0:T(8,128)(2,1)} %bitcast.2), calls=%async_computation | async-start | bytes 262144 | tf_op jit(solution)/shard_map/all_to_all | solution.py:26
  15.9 0.1 collective-permute-start.2
  16.0 0.5 collective-permute-start.3
  16.5 0.1 collective-permute-start.4
  16.6 0.4 collective-permute-start.1
  17.0 0.0 copy-done.8
  17.0 9.0 %all-to-all-done.pieces = bf16[32,16,128]{2,1,0:T(8,128)(2,1)S(1)} async-done(((bf16[32,16,128]{2,1,0:T(8,128)(2,1)}), bf16[32,16,128]{2,1,0:T(8,128)(2,1)S(1)}, u32[]{:S(2)}, u32[]{:S(2)}) %all-to-all-start) | async-done | bytes 131104 | tf_op jit(solution)/shard_map/all_to_all | solution.py:26
  26.0 0.7 prefix.1
  26.8 5.1 %all-to-all-start.1 = ((bf16[64,16,128]{2,1,0:T(8,128)(2,1)}), bf16[64,16,128]{2,1,0:T(8,128)(2,1)S(1)}, u32[]{:S(2)}, u32[]{:S(2)}) async-start(bf16[64,16,128]{2,1,0:T(8,128)(2,1)} %bitcast.3), calls=%async_computation.1 | async-start | bytes 524288 | tf_op jit(solution)/shard_map/all_to_all | solution.py:26
  31.9 0.0 copy-done.7
  31.9 0.2 convert_reduce_fusion
  32.1 0.0 collective-permute-done.w_other
  32.1 0.0 copy-done.2
  32.1 0.0 copy-done.1
  32.1 5.1 %inside_block.1 = (bf16[256,768]{1,0:T(8,128)(2,1)S(1)}, f32[256,768]{1,0:T(8,128)S(1)}) custom-call(bf16[512,768]{1,0:T(8,128)(2,1)S(1)} %bitcast.19, f32[1,768]{1,0:T(1,128)S(1)} %broadcast_in_dim.10.gain, bf16[3,768,384]{2,1,0:T(8,128)(2,1)S(1)} %bitcast.22, bf16[3,768,384]{2,1,0:T(8,128)(2,1)} %collective-permute-done.w_other), custom_call_target="tpu_custom_call" | custom-call | flops 1912602624 | bytes 3145728 | tf_op jit(solution)/shard_map/inside_block/pallas_call | solution.py:209
  37.3 0.0 copy-start.3
  37.3 0.9 copy-done.3
  38.2 0.0 copy-start.4
  38.2 0.7 copy-done.4
  39.0 0.0 collective-permute-done.1.out_other
  39.0 5.3 %all-to-all-done.1 = bf16[64,16,128]{2,1,0:T(8,128)(2,1)S(1)} async-done(((bf16[64,16,128]{2,1,0:T(8,128)(2,1)}), bf16[64,16,128]{2,1,0:T(8,128)(2,1)S(1)}, u32[]{:S(2)}, u32[]{:S(2)}) %all-to-all-start.1) | async-done | bytes 262176 | tf_op jit(solution)/shard_map/all_to_all | solution.py:26
  44.3 3.4 %mix_heads.1 = (f32[256,768]{1,0:T(8,128)}, bf16[256,768]{1,0:T(8,128)(2,1)}, bf16[512,768]{1,0:T(8,128)(2,1)S(1)}) custom-call(bf16[256,768]{1,0:T(8,128)(2,1)} %copy-done.4, f32[256,768]{1,0:T(8,128)} %copy-done.3, bf16[32,2,16,128]{3,2,1,0:T(8,128)(2,1)S(1)} %bitcast.23, bf16[384,768]{1,0:T(8,128)(2,1)} %out_own.1, ...), custom_call_target="tpu_custom_call" | custom-call | flops 553648128 | bytes 2359296 | tf_op jit(solution)/shard_map/mix_heads/pallas_call | solution.py:306
  47.7 0.2 reshape.63
  47.9 34.6 %all_to_all.20 = bf16[128,4,768]{2,1,0:T(4,128)(2,1)S(1)} all-to-all(bf16[128,4,768]{2,1,0:T(4,128)(2,1)S(1)} %reshape.63), channel_id=1, replica_groups=mesh['seq_0'=8,'seq_1'=4,'head'=2,'dp'=4] {'seq_0','seq_1','dp'}, dimensions={0} | all-to-all | bytes 1572864 | tf_op jit(solution)/shard_map/all_to_all | solution.py:26
  82.5 0.2 reshape.64.refs_0_
  82.7 0.0 collective-permute-done.2.refs_4_
  82.7 0.0 collective-permute-done.3.refs_5_
  82.7 0.0 collective-permute-done.4.refs_6_
  82.7 12.0 %expert_mlp.1 = bf16[512,768]{1,0:T(8,128)(2,1)S(1)} custom-call(bf16[512,768]{1,0:T(8,128)(2,1)S(1)} %reshape.64.refs_0_, bf16[768,1536]{1,0:T(8,128)(2,1)} %bitcast.29, bf16[768,1536]{1,0:T(8,128)(2,1)} %bitcast.31, bf16[1536,768]{1,0:T(8,128)(2,1)} %bitcast.33, bf16[768,1536]{1,0:T(8,128)(2,1)} %collective-permute-done.2.refs_4_, ...), custom_call_target="tpu_custom_call" | custom-call | flops 7247757312 | bytes 14155776 | tf_op jit(solution)/shard_map/expert_mlp/pallas_call | solution.py:74
  94.7 0.0 copy-start.6
  94.7 1.1 reshape.65
  95.8 6.5 %all-to-all-start.3 = ((bf16[128,4,768]{2,1,0:T(4,128)(2,1)}), bf16[128,4,768]{2,1,0:T(4,128)(2,1)S(1)}, u32[]{:S(2)}, u32[]{:S(2)}) async-start(bf16[128,4,768]{2,1,0:T(4,128)(2,1)} %reshape.65), calls=%async_computation.3 | async-start | bytes 1572864 | tf_op jit(solution)/shard_map/all_to_all | solution.py:26
  102.3 0.0 copy-done
  102.3 0.0 copy-done.6
  102.3 0.3 fusion
  102.7 24.4 %all-to-all-done.3 = bf16[128,4,768]{2,1,0:T(4,128)(2,1)S(1)} async-done(((bf16[128,4,768]{2,1,0:T(4,128)(2,1)}), bf16[128,4,768]{2,1,0:T(4,128)(2,1)S(1)}, u32[]{:S(2)}, u32[]{:S(2)}) %all-to-all-start.3) | async-done | bytes 786464 | tf_op jit(solution)/shard_map/all_to_all | solution.py:26
  127.0 0.2 reshape.66
  127.2 0.4 convolution_multiply_fusion
  127.6 0.0 copy-done.5
  127.7 0.8 fusion.1
  (5 shorter events, 0.0 us)
Async XLA Ops:
  0.0 102.3 %copy-start = (bf16[768,128]{1,0:T(8,128)(2,1)S(1)}, bf16[768,128]{1,0:T(8,128)(2,1)}, u32[]{:S(2)}) copy-start(bf16[768,128]{1,0:T(8,128)(2,1)} %param.15) | copy-start | bytes 589828
  0.0 32.1 %copy-start.2 = (bf16[768,3,384]{2,0,1:T(8,128)(2,1)S(1)}, bf16[768,3,384]{2,0,1:T(8,128)(2,1)}, u32[]{:S(2)}) copy-start(bf16[768,3,384]{2,0,1:T(8,128)(2,1)} %param.12) | copy-start | bytes 5308420
  0.0 32.1 %copy-start.1 = (bf16[1,512,768]{2,1,0:T(8,128)(2,1)S(1)}, bf16[1,512,768]{2,1,0:T(8,128)(2,1)}, u32[]{:S(2)}) copy-start(bf16[1,512,768]{2,1,0:T(8,128)(2,1)} %param.10) | copy-start | bytes 2359300
  0.0 17.0 %copy-start.8 = (f32[768]{0:T(1024)S(1)}, f32[768]{0:T(1024)}, u32[]{:S(2)}) copy-start(f32[768]{0:T(1024)} %param.14) | copy-start | bytes 9220
  0.0 31.9 %copy-start.7 = (s32[1,256,1]{1,2,0:T(1,128)S(1)}, s32[1,256,1]{1,2,0:T(1,128)}, u32[]{:S(2)}) copy-start(s32[1,256,1]{1,2,0:T(1,128)} %param.16) | copy-start | bytes 3076
  0.0 32.1 %collective-permute-start = (bf16[3,768,384]{2,1,0:T(8,128)(2,1)}, bf16[3,768,384]{2,1,0:T(8,128)(2,1)}, u32[]{:S(2)}, u32[]{:S(2)}) collective-permute-start(bf16[3,768,384]{2,1,0:T(8,128)(2,1)} %bitcast.20), channel_id=1, source_target_pairs={{0,4},{4,0},{1,5},{5,1},{2,6},{6,2},{3,7},{7,3},{8,12},{12,8},{9,1... | collective-permute-start | bytes 5308424 | tf_op jit(solution)/shard_map/ppermute | solution.py:22
  4.5 21.5 %all-to-all-start = ((bf16[32,16,128]{2,1,0:T(8,128)(2,1)}), bf16[32,16,128]{2,1,0:T(8,128)(2,1)S(1)}, u32[]{:S(2)}, u32[]{:S(2)}) async-start(bf16[32,16,128]{2,1,0:T(8,128)(2,1)} %bitcast.2), calls=%async_computation | async-start | bytes 262144 | tf_op jit(solution)/shard_map/all_to_all | solution.py:26
  15.9 66.8 %collective-permute-start.2 = (bf16[768,1536]{1,0:T(8,128)(2,1)}, bf16[768,1536]{1,0:T(8,128)(2,1)}, u32[]{:S(2)}, u32[]{:S(2)}) collective-permute-start(bf16[768,1536]{1,0:T(8,128)(2,1)} %bitcast.28), channel_id=1, source_target_pairs={{0,4},{4,0},{1,5},{5,1},{2,6},{6,2},{3,7},{7,3},{8,12},{12,8},{9,1... | collective-permute-start | bytes 7077896 | tf_op jit(solution)/shard_map/ppermute | solution.py:22
  16.0 66.7 %collective-permute-start.3 = (bf16[768,1536]{1,0:T(8,128)(2,1)}, bf16[768,1536]{1,0:T(8,128)(2,1)}, u32[]{:S(2)}, u32[]{:S(2)}) collective-permute-start(bf16[768,1536]{1,0:T(8,128)(2,1)} %bitcast.30), channel_id=1, source_target_pairs={{0,4},{4,0},{1,5},{5,1},{2,6},{6,2},{3,7},{7,3},{8,12},{12,8},{9,1... | collective-permute-start | bytes 7077896 | tf_op jit(solution)/shard_map/ppermute | solution.py:22
  16.5 66.2 %collective-permute-start.4 = (bf16[1536,768]{1,0:T(8,128)(2,1)}, bf16[1536,768]{1,0:T(8,128)(2,1)}, u32[]{:S(2)}, u32[]{:S(2)}) collective-permute-start(bf16[1536,768]{1,0:T(8,128)(2,1)} %bitcast.32), channel_id=1, source_target_pairs={{0,4},{4,0},{1,5},{5,1},{2,6},{6,2},{3,7},{7,3},{8,12},{12,8},{9,1... | collective-permute-start | bytes 7077896 | tf_op jit(solution)/shard_map/ppermute | solution.py:22
  16.6 22.4 %collective-permute-start.1 = (bf16[384,768]{1,0:T(8,128)(2,1)}, bf16[384,768]{1,0:T(8,128)(2,1)}, u32[]{:S(2)}, u32[]{:S(2)}) collective-permute-start(bf16[384,768]{1,0:T(8,128)(2,1)} %out_own.1), channel_id=1, source_target_pairs={{0,4},{4,0},{1,5},{5,1},{2,6},{6,2},{3,7},{7,3},{8,12},{12,8},{9,1... | collective-permute-start | bytes 1769480 | tf_op jit(solution)/shard_map/ppermute | solution.py:22
  26.8 17.5 %all-to-all-start.1 = ((bf16[64,16,128]{2,1,0:T(8,128)(2,1)}), bf16[64,16,128]{2,1,0:T(8,128)(2,1)S(1)}, u32[]{:S(2)}, u32[]{:S(2)}) async-start(bf16[64,16,128]{2,1,0:T(8,128)(2,1)} %bitcast.3), calls=%async_computation.1 | async-start | bytes 524288 | tf_op jit(solution)/shard_map/all_to_all | solution.py:26
  37.3 1.0 copy-start.3
  38.2 0.7 copy-start.4
  94.7 7.7 %copy-start.6 = (bf16[256,768]{1,0:T(8,128)(2,1)S(1)}, bf16[256,768]{1,0:T(8,128)(2,1)}, u32[]{:S(2)}) copy-start(bf16[256,768]{1,0:T(8,128)(2,1)} %get-tuple-element.13) | copy-start | bytes 1179652
  95.8 31.9 %copy-start.5 = (f32[256,768]{1,0:T(8,128)S(1)}, f32[256,768]{1,0:T(8,128)}, u32[]{:S(2)}) copy-start(f32[256,768]{1,0:T(8,128)} %get-tuple-element.12) | copy-start | bytes 2359300
  95.8 31.3 %all-to-all-start.3 = ((bf16[128,4,768]{2,1,0:T(4,128)(2,1)}), bf16[128,4,768]{2,1,0:T(4,128)(2,1)S(1)}, u32[]{:S(2)}, u32[]{:S(2)}) async-start(bf16[128,4,768]{2,1,0:T(4,128)(2,1)} %reshape.65), calls=%async_computation.3 | async-start | bytes 1572864 | tf_op jit(solution)/shard_map/all_to_all | solution.py:26

commit v3 on v2

--- a/solution.py
+++ b/solution.py
@@ -8,8 +8,8 @@
 from jax.sharding import Mesh
 from jax.sharding import PartitionSpec as P
 
+
 HD = 128
-BLOCK = 512
 SEQ = ("seq_0", "seq_1")
 SEQ_DP = ("seq_0", "seq_1", "dp")
 SEQ_HEAD = ("seq_0", "seq_1", "head")
@@ -97,7 +97,7 @@
 def normed_rows(rows, gain):
     x = rows.astype(jnp.float32)
     mean = jnp.sum(x * x, axis=-1, keepdims=True) * (1.0 / x.shape[1])
-    return x * lax.rsqrt(mean + NORM_EPS) * gain
+    return x * lax.rsqrt(mean + NORM_EPS) * gain.reshape(1, -1)
 
 
 def state_kernel(series, weight, gain, state_out, rows, table, sems):
@@ -152,8 +152,7 @@
     total = jnp.zeros(pieces.shape[1:], jnp.float32)
     for k in range(pieces.shape[0]):
         rounded = total.astype(jnp.bfloat16)
-        out[k, 0] = rounded
-        out[k, 1] = rounded
+        out[k] = rounded
         total = total + pieces[k].astype(jnp.float32)
 
 
@@ -163,7 +162,7 @@
         prefix_kernel,
         in_specs=[pl.BlockSpec(memory_space=pltpu.VMEM)],
         out_specs=pl.BlockSpec(memory_space=pltpu.VMEM),
-        out_shape=jax.ShapeDtypeStruct((count, 2, lines, lanes), jnp.bfloat16),
+        out_shape=jax.ShapeDtypeStruct((count, lines, lanes), jnp.bfloat16),
         compiler_params=pltpu.CompilerParams(vmem_limit_bytes=4 * MIB),
         cost_estimate=pl.CostEstimate(
             flops=count * lines * lanes, bytes_accessed=6 * count * lines * lanes, transcendentals=0
@@ -172,9 +171,11 @@
     )(pieces)
 
 
-def inside_kernel(series, gain, w_own, w_other, queries_out, inside_out):
+def inside_kernel(
+    series, gain, w_own, w_other, queries_out, inside_out, queries_held, inside_held, sems
+):
     count, _ = series.shape
-    own_rows = queries_out.shape[0]
+    own_rows = queries_held.shape[0]
     half = w_own.shape[2]
     heads = half // HD
     first_row = pl.multiple_of(lax.axis_index("head") * own_rows, own_rows)
@@ -187,7 +188,7 @@
             jnp.dot(rows, weight[k], preferred_element_type=jnp.float32).astype(jnp.bfloat16)
             for k, rows in ((0, mine), (1, normed), (2, normed))
         )
-        queries_out[:, part * half : (part + 1) * half] = queries
+        queries_held[:, part * half : (part + 1) * half] = queries
         for n in range(heads):
             at = slice(n * HD, (n + 1) * HD)
             scores = lax.dot_general(
@@ -198,9 +199,15 @@
             )
             scores = jnp.where(causal, scores, 0.0).astype(jnp.bfloat16)
             lanes = slice(part * half + n * HD, part * half + (n + 1) * HD)
-            inside_out[:, lanes] = jnp.dot(
+            inside_held[:, lanes] = jnp.dot(
                 scores, values[:, at], preferred_element_type=jnp.float32
             )
+    keep_queries = pltpu.make_async_copy(queries_held, queries_out, sems.at[0])
+    keep_inside = pltpu.make_async_copy(inside_held, inside_out, sems.at[1])
+    keep_queries.start()
+    keep_inside.start()
+    keep_queries.wait()
+    keep_inside.wait()
 
 
 def inside_block(series, gain, w_own, w_other, own_rows):
@@ -209,10 +216,15 @@
     return pl.pallas_call(
         inside_kernel,
         in_specs=[pl.BlockSpec(memory_space=pltpu.VMEM)] * 4,
-        out_specs=[pl.BlockSpec(memory_space=pltpu.VMEM)] * 2,
+        out_specs=[pl.BlockSpec(memory_space=pl.ANY)] * 2,
         out_shape=[
-            jax.ShapeDtypeStruct((own_rows, 2 * half), jnp.bfloat16),
-            jax.ShapeDtypeStruct((own_rows, 2 * half), jnp.float32),
+            pltpu.HBM((own_rows, 2 * half), jnp.bfloat16),
+            pltpu.HBM((own_rows, 2 * half), jnp.float32),
+        ],
+        scratch_shapes=[
+            pltpu.VMEM((own_rows, 2 * half), jnp.bfloat16),
+            pltpu.VMEM((own_rows, 2 * half), jnp.float32),
+            pltpu.SemaphoreType.DMA((2,)),
         ],
         compiler_params=pltpu.CompilerParams(vmem_limit_bytes=24 * MIB),
         cost_estimate=pl.CostEstimate(
@@ -227,7 +239,8 @@
 def mix_kernel(
     queries,
     inside,
-    states,
+    state_own,
+    state_other,
     out_own,
     out_other,
     series,
@@ -238,23 +251,17 @@
     send_out,
     queries_in,
     inside_in,
-    weights_in,
-    rows_in,
     residual_held,
     normed_held,
     sems,
 ):
-    own_rows, width = rows_in.shape
+    own_rows, _ = queries_in.shape
     half = out_own.shape[0]
     heads = half // HD
-    head_rank = lax.axis_index("head")
-    first_row = pl.multiple_of(head_rank * own_rows, own_rows)
+    first_row = pl.multiple_of(lax.axis_index("head") * own_rows, own_rows)
     fetches = [
         pltpu.make_async_copy(queries, queries_in, sems.at[0]),
         pltpu.make_async_copy(inside, inside_in, sems.at[1]),
-        pltpu.make_async_copy(out_own, weights_in.at[0], sems.at[2]),
-        pltpu.make_async_copy(out_other, weights_in.at[1], sems.at[3]),
-        pltpu.make_async_copy(series.at[pl.ds(first_row, own_rows)], rows_in, sems.at[4]),
     ]
     for fetch in fetches:
         fetch.start()
@@ -263,33 +270,26 @@
     unit = 1.0 / (position.astype(jnp.float32) * math.sqrt(HD))
     slot = lax.broadcasted_iota(jnp.int32, (send_out.shape[0], own_rows), 0)
     chosen = jnp.where(slot == slots[...], 1.0, 0.0).astype(jnp.bfloat16)
-    per_head = HD // states.shape[2]
     fetches[0].wait()
     fetches[1].wait()
     mixed = []
-    for part in range(2):
-        rank = head_rank if part == 0 else 1 - head_rank
+    for part, state in ((0, state_own), (1, state_other)):
         for n in range(heads):
             lanes = slice(part * half + n * HD, part * half + (n + 1) * HD)
-            start = states[n * per_head : (n + 1) * per_head, rank].reshape(HD, HD)
+            start = state[n * HD : (n + 1) * HD, :]
             carried = jnp.dot(queries_in[:, lanes], start, preferred_element_type=jnp.float32)
             mixed.append(((inside_in[:, lanes] + carried) * unit).astype(jnp.bfloat16))
-    fetches[2].wait()
-    total = jnp.dot(
-        jnp.concatenate(mixed[:heads], axis=1), weights_in[0], preferred_element_type=jnp.float32
-    )
-    fetches[3].wait()
-    total += jnp.dot(
-        jnp.concatenate(mixed[heads:], axis=1), weights_in[1], preferred_element_type=jnp.float32
-    )
-    fetches[4].wait()
-    total += rows_in[...].astype(jnp.float32)
+    total = series[pl.ds(first_row, own_rows), :].astype(jnp.float32)
+    for mine, weight in ((mixed[:heads], out_own), (mixed[heads:], out_other)):
+        total += jnp.dot(
+            jnp.concatenate(mine, axis=1), weight[...], preferred_element_type=jnp.float32
+        )
     residual_held[...] = total
-    keep_residual = pltpu.make_async_copy(residual_held, residual_out, sems.at[5])
+    keep_residual = pltpu.make_async_copy(residual_held, residual_out, sems.at[2])
     keep_residual.start()
     normed = normed_rows(total, gain[...]).astype(jnp.bfloat16)
     normed_held[...] = normed
-    keep_normed = pltpu.make_async_copy(normed_held, normed_out, sems.at[6])
+    keep_normed = pltpu.make_async_copy(normed_held, normed_out, sems.at[3])
     keep_normed.start()
     send_out[...] = jnp.dot(chosen, normed, preferred_element_type=jnp.float32).astype(
         jnp.bfloat16
@@ -298,14 +298,15 @@
     keep_normed.wait()
 
 
-def mix_heads(queries, inside, states, out_own, out_other, series, gain, slots, slot_count):
+def mix_heads(
+    queries, inside, state_own, state_other, out_own, out_other, series, gain, slots, slot_count
+):
     own_rows, width = queries.shape
-    half = out_own.shape[0]
     anywhere = pl.BlockSpec(memory_space=pl.ANY)
     local = pl.BlockSpec(memory_space=pltpu.VMEM)
     return pl.pallas_call(
         mix_kernel,
-        in_specs=[anywhere, anywhere, local, anywhere, anywhere, anywhere, local, local],
+        in_specs=[anywhere] * 2 + [local] * 7,
         out_specs=[anywhere, anywhere, local],
         out_shape=[
             pltpu.HBM((own_rows, width), jnp.float32),
@@ -315,11 +316,9 @@
         scratch_shapes=[
             pltpu.VMEM((own_rows, width), jnp.bfloat16),
             pltpu.VMEM((own_rows, width), jnp.float32),
-            pltpu.VMEM((2, half, width), jnp.bfloat16),
-            pltpu.VMEM((own_rows, width), jnp.bfloat16),
             pltpu.VMEM((own_rows, width), jnp.float32),
             pltpu.VMEM((own_rows, width), jnp.bfloat16),
-            pltpu.SemaphoreType.DMA((7,)),
+            pltpu.SemaphoreType.DMA((4,)),
         ],
         compiler_params=pltpu.CompilerParams(vmem_limit_bytes=24 * MIB),
         cost_estimate=pl.CostEstimate(
@@ -331,10 +330,11 @@
     )(
         in_hbm(queries),
         in_hbm(inside),
-        states,
-        in_hbm(out_own),
-        in_hbm(out_other),
-        in_hbm(series),
+        state_own,
+        state_other,
+        out_own,
+        out_other,
+        series,
         gain,
         slots,
     )
@@ -363,11 +363,11 @@
     own_expert = (gate_weight[0], up_weight[0], down_weight[0])
     other_expert = tuple(from_partner(w) for w in own_expert)
 
-    state = block_state(series[0], qkv_own, norm_attn[None])
+    state = block_state(series[0], qkv_own, norm_attn)
     pieces = exchange(state.reshape(seq_size, state.shape[0] // seq_size, HD), SEQ)
-    before = prefix(pieces)
-    states = exchange(before.reshape(seq_size * head_count, *before.shape[2:]), SEQ_HEAD)
-    queries, inside = inside_block(series[0], norm_attn[None], qkv_own, qkv_other, own_rows)
+    state_own = exchange(prefix(pieces), SEQ)
+    state_other = from_partner(state_own)
+    queries, inside = inside_block(series[0], norm_attn, qkv_own, qkv_other, own_rows)
 
     route_ids = expert_ids[0, :, 0]
     expert_count = router_weight.shape[1]
@@ -380,11 +380,12 @@
     residual, normed_moe, send_buffer = mix_heads(
         queries,
         inside,
-        states.reshape(before.shape),
+        state_own.reshape(state.shape),
+        state_other.reshape(state.shape),
         out_weight,
         out_other,
         series[0],
-        norm_moe[None],
+        norm_moe,
         slot_index[None, :],
         expert_count * capacity,
     )
@@ -426,6 +427,7 @@
         P(SEQ_DP, None, "head"),
         P(SEQ_DP, "head", None),
     )
+
     return jax.shard_map(
         on_device, mesh=split, in_specs=placed, out_specs=P("dp", SEQ_HEAD, None), check_vma=False
     )

time: 129 us -> 133 us (1.031)
  waiting for transfers between devices: 38.7 us -> 42.9 us
  local copies, waits for them, and re-layouts: 4.18 us -> 2.48 us
  Pallas kernels: 24.7 us -> 26.4 us
    all_to_all x3, waiting for transfers between devices: 38.7 us -> 42.9 us  [exchange(): return lax.all_to_all(pieces, axes, split_axis=0, concat_axis=0, tiled=True)]
  transfers between devices with their start and end apart: 8 -> 9, of which waited for: 3 -> 3; matrix products, arithmetic and copies ran while one was open for 1% -> 1% of each run, Pallas kernels for 10% -> 11%
where the time goes in v3:
time: 133 us; the launch traced here: 132 us
  waiting for transfers between devices  42.9 us (32%)
  blocking collectives  34.4 us (26%)
  Pallas kernels  26.4 us (20%)
  starting transfers between devices  23.7 us (18%)
  local copies, waits for them, and re-layouts  2.48 us (2%)
    all_to_all x3, waiting for transfers between devices, exchange(): return lax.all_to_all(pieces, axes, split_axis=0, concat_axis=0, tiled=True)  42.9 us
    all_to_all x1, blocking collectives, exchange(): return lax.all_to_all(pieces, axes, split_axis=0, concat_axis=0, tiled=True)  34.4 us
    all_to_all x3, starting transfers between devices, exchange(): return lax.all_to_all(pieces, axes, split_axis=0, concat_axis=0, tiled=True)  22.5 us
    pallas_call x1, Pallas kernels, expert_of(): pl.pallas_call(lambda *refs: expert_kernel(blocks, *refs), grid=(2 * bloc...  12 us
    pallas_call x1, Pallas kernels, inside_block(): pl.pallas_call(inside_kernel, in_specs=[pl.BlockSpec(memory_space=pltpu.V...  6.05 us
    pallas_call x1, Pallas kernels, mix_heads(): pl.pallas_call(mix_kernel, in_specs=[anywhere] * 2 + [local] * 7, out_spe...  4.21 us
    pallas_call x1, Pallas kernels, block_state(): pl.pallas_call(state_kernel, in_specs=[pl.BlockSpec(memory_space=pl.ANY),...  3.51 us
  transfers between devices with their start and end apart: 9, of which 3 were waited for; matrix products, arithmetic and copies ran while one was open for 1% of the time, Pallas kernels for 11%

profile of v3, /device:TPU:32, one launch (start us, length us, event | category | flops | bytes accessed | tf_op | source)
XLA Modules:
  0.0 132.0 jit_solution(11105064895563373566)
XLA Ops:
  0.0 0.0 copy-start
  0.0 0.0 copy-start.2
  0.0 0.1 collective-permute-start
  0.1 0.0 copy-start.4
  0.1 0.8 copy-done.4
  1.0 3.5 %block_state.1 = bf16[512,128]{1,0:T(8,128)(2,1)} custom-call(bf16[512,768]{1,0:T(8,128)(2,1)} %bitcast.17, bf16[3,768,384]{2,1,0:T(8,128)(2,1)} %bitcast.21, f32[768]{0:T(1024)S(1)} %copy-done.4), custom_call_target="tpu_custom_call" | custom-call | flops 603979776 | bytes 1572864 | tf_op jit(solution)/shard_map/block_state/pallas_call | solution.py:129
  4.5 11.4 %all-to-all-start = ((bf16[32,16,128]{2,1,0:T(8,128)(2,1)}), bf16[32,16,128]{2,1,0:T(8,128)(2,1)S(1)}, u32[]{:S(2)}, u32[]{:S(2)}) async-start(bf16[32,16,128]{2,1,0:T(8,128)(2,1)} %bitcast.2), calls=%async_computation | async-start | bytes 262144 | tf_op jit(solution)/shard_map/all_to_all | solution.py:26
  15.9 0.1 collective-permute-start.3
  16.0 0.5 collective-permute-start.4
  16.4 0.1 collective-permute-start.5
  16.6 0.4 collective-permute-start.2
  17.0 9.0 %all-to-all-done.pieces = bf16[32,16,128]{2,1,0:T(8,128)(2,1)S(1)} async-done(((bf16[32,16,128]{2,1,0:T(8,128)(2,1)}), bf16[32,16,128]{2,1,0:T(8,128)(2,1)S(1)}, u32[]{:S(2)}, u32[]{:S(2)}) %all-to-all-start) | async-done | bytes 131104 | tf_op jit(solution)/shard_map/all_to_all | solution.py:26
  26.0 0.7 prefix.1
  26.7 4.6 %all-to-all-start.1 = ((bf16[32,16,128]{2,1,0:T(8,128)(2,1)}), bf16[32,16,128]{2,1,0:T(8,128)(2,1)S(1)}, u32[]{:S(2)}, u32[]{:S(2)}) async-start(bf16[32,16,128]{2,1,0:T(8,128)(2,1)} %prefix.1), calls=%async_computation.1 | async-start | bytes 262144 | tf_op jit(solution)/shard_map/all_to_all | solution.py:26
  31.3 0.0 copy-done.9
  31.3 0.2 convert_reduce_fusion
  31.5 0.0 copy-start.3
  31.5 0.0 copy-start.6
  31.5 9.4 %all-to-all-done.1 = bf16[32,16,128]{2,1,0:T(8,128)(2,1)S(1)} async-done(((bf16[32,16,128]{2,1,0:T(8,128)(2,1)}), bf16[32,16,128]{2,1,0:T(8,128)(2,1)S(1)}, u32[]{:S(2)}, u32[]{:S(2)}) %all-to-all-start.1) | async-done | bytes 131104 | tf_op jit(solution)/shard_map/all_to_all | solution.py:26
  40.9 0.0 collective-permute-done.w_other
  40.9 0.0 collective-permute-start.1
  40.9 0.0 copy-done.2
  40.9 0.0 copy-done.1
  40.9 0.0 copy-done.5
  41.0 6.0 %inside_block.1 = (bf16[256,768]{1,0:T(8,128)(2,1)}, f32[256,768]{1,0:T(8,128)}) custom-call(bf16[512,768]{1,0:T(8,128)(2,1)S(1)} %bitcast.18, f32[768]{0:T(1024)S(1)} %copy-done.5, bf16[3,768,384]{2,1,0:T(8,128)(2,1)S(1)} %bitcast.22, bf16[3,768,384]{2,1,0:T(8,128)(2,1)} %collective-permute-done.w_other), custom_call_target="tpu_custom_call" | custom-call | flops 1912602624 | bytes 3145728 | tf_op jit(solution)/shard_map/inside_block/pallas_call | solution.py:216
  47.0 0.0 collective-permute-done.2.out_other
  47.0 0.0 collective-permute-done.1
  47.0 0.0 copy-done.3
  47.0 0.0 copy-done.6
  47.1 4.2 %mix_heads.1 = (f32[256,768]{1,0:T(8,128)}, bf16[256,768]{1,0:T(8,128)(2,1)}, bf16[512,768]{1,0:T(8,128)(2,1)S(1)}) custom-call(bf16[256,768]{1,0:T(8,128)(2,1)} %get-tuple-element.10.queries, f32[256,768]{1,0:T(8,128)} %get-tuple-element.11.inside, bf16[512,128]{1,0:T(8,128)(2,1)S(1)} %bitcast.23, bf16[512,128]{1,0:T(8,128)(2,1)S(1)} %bitcast.24, ...), custom_call_target="tpu_custom_call" | custom-call | flops 553648128 | bytes 2359296 | tf_op jit(solution)/shard_map/mix_heads/pallas_call | solution.py:307
  51.3 0.2 reshape.63
  51.5 34.4 %all_to_all.20 = bf16[128,4,768]{2,1,0:T(4,128)(2,1)S(1)} all-to-all(bf16[128,4,768]{2,1,0:T(4,128)(2,1)S(1)} %reshape.63), channel_id=1, replica_groups=mesh['seq_0'=8,'seq_1'=4,'head'=2,'dp'=4] {'seq_0','seq_1','dp'}, dimensions={0} | all-to-all | bytes 1572864 | tf_op jit(solution)/shard_map/all_to_all | solution.py:26
  85.9 0.2 reshape.64.refs_0_
  86.1 0.0 collective-permute-done.3.refs_4_
  86.1 0.0 collective-permute-done.4.refs_5_
  86.1 0.0 collective-permute-done.5.refs_6_
  86.1 12.0 %expert_mlp.1 = bf16[512,768]{1,0:T(8,128)(2,1)S(1)} custom-call(bf16[512,768]{1,0:T(8,128)(2,1)S(1)} %reshape.64.refs_0_, bf16[768,1536]{1,0:T(8,128)(2,1)} %bitcast.30, bf16[768,1536]{1,0:T(8,128)(2,1)} %bitcast.32, bf16[1536,768]{1,0:T(8,128)(2,1)} %bitcast.34, bf16[768,1536]{1,0:T(8,128)(2,1)} %collective-permute-done.3.refs_4_, ...), custom_call_target="tpu_custom_call" | custom-call | flops 7247757312 | bytes 14155776 | tf_op jit(solution)/shard_map/expert_mlp/pallas_call | solution.py:74
  98.1 0.0 copy-start.8
  98.1 1.1 reshape.65
  99.1 6.5 %all-to-all-start.3 = ((bf16[128,4,768]{2,1,0:T(4,128)(2,1)}), bf16[128,4,768]{2,1,0:T(4,128)(2,1)S(1)}, u32[]{:S(2)}, u32[]{:S(2)}) async-start(bf16[128,4,768]{2,1,0:T(4,128)(2,1)} %reshape.65), calls=%async_computation.3 | async-start | bytes 1572864 | tf_op jit(solution)/shard_map/all_to_all | solution.py:26
  105.7 0.0 copy-done
  105.7 0.0 copy-done.8
  105.7 0.3 fusion
  106.1 24.5 %all-to-all-done.3 = bf16[128,4,768]{2,1,0:T(4,128)(2,1)S(1)} async-done(((bf16[128,4,768]{2,1,0:T(4,128)(2,1)}), bf16[128,4,768]{2,1,0:T(4,128)(2,1)S(1)}, u32[]{:S(2)}, u32[]{:S(2)}) %all-to-all-start.3) | async-done | bytes 786464 | tf_op jit(solution)/shard_map/all_to_all | solution.py:26
  130.5 0.2 reshape.66
  130.7 0.4 convolution_multiply_fusion
  131.1 0.0 copy-done.7
  131.1 0.8 fusion.1
  (7 shorter events, 0.0 us)
Async XLA Ops:
  0.0 105.7 %copy-start = (bf16[768,128]{1,0:T(8,128)(2,1)S(1)}, bf16[768,128]{1,0:T(8,128)(2,1)}, u32[]{:S(2)}) copy-start(bf16[768,128]{1,0:T(8,128)(2,1)} %param.15) | copy-start | bytes 589828
  0.0 40.9 %copy-start.2 = (bf16[768,3,384]{2,0,1:T(8,128)(2,1)S(1)}, bf16[768,3,384]{2,0,1:T(8,128)(2,1)}, u32[]{:S(2)}) copy-start(bf16[768,3,384]{2,0,1:T(8,128)(2,1)} %param.12) | copy-start | bytes 5308420
  0.0 40.9 %copy-start.1 = (bf16[1,512,768]{2,1,0:T(8,128)(2,1)S(1)}, bf16[1,512,768]{2,1,0:T(8,128)(2,1)}, u32[]{:S(2)}) copy-start(bf16[1,512,768]{2,1,0:T(8,128)(2,1)} %param.10) | copy-start | bytes 2359300
  0.0 40.9 %collective-permute-start = (bf16[3,768,384]{2,1,0:T(8,128)(2,1)}, bf16[3,768,384]{2,1,0:T(8,128)(2,1)}, u32[]{:S(2)}, u32[]{:S(2)}) collective-permute-start(bf16[3,768,384]{2,1,0:T(8,128)(2,1)} %bitcast.20), channel_id=1, source_target_pairs={{0,4},{4,0},{1,5},{5,1},{2,6},{6,2},{3,7},{7,3},{8,12},{12,8},{9,1... | collective-permute-start | bytes 5308424 | tf_op jit(solution)/shard_map/ppermute | solution.py:22
  0.1 0.8 copy-start.4
  1.0 30.3 %copy-start.9 = (s32[1,256,1]{1,2,0:T(1,128)S(1)}, s32[1,256,1]{1,2,0:T(1,128)}, u32[]{:S(2)}) copy-start(s32[1,256,1]{1,2,0:T(1,128)} %param.16) | copy-start | bytes 3076
  1.0 40.0 %copy-start.5 = (f32[768]{0:T(1024)S(1)}, f32[768]{0:T(1024)}, u32[]{:S(2)}) copy-start(f32[768]{0:T(1024)} %gain.4) | copy-start | bytes 9220
  4.5 21.5 %all-to-all-start = ((bf16[32,16,128]{2,1,0:T(8,128)(2,1)}), bf16[32,16,128]{2,1,0:T(8,128)(2,1)S(1)}, u32[]{:S(2)}, u32[]{:S(2)}) async-start(bf16[32,16,128]{2,1,0:T(8,128)(2,1)} %bitcast.2), calls=%async_computation | async-start | bytes 262144 | tf_op jit(solution)/shard_map/all_to_all | solution.py:26
  15.9 70.2 %collective-permute-start.3 = (bf16[768,1536]{1,0:T(8,128)(2,1)}, bf16[768,1536]{1,0:T(8,128)(2,1)}, u32[]{:S(2)}, u32[]{:S(2)}) collective-permute-start(bf16[768,1536]{1,0:T(8,128)(2,1)} %bitcast.29), channel_id=1, source_target_pairs={{0,4},{4,0},{1,5},{5,1},{2,6},{6,2},{3,7},{7,3},{8,12},{12,8},{9,1... | collective-permute-start | bytes 7077896 | tf_op jit(solution)/shard_map/ppermute | solution.py:22
  16.0 70.1 %collective-permute-start.4 = (bf16[768,1536]{1,0:T(8,128)(2,1)}, bf16[768,1536]{1,0:T(8,128)(2,1)}, u32[]{:S(2)}, u32[]{:S(2)}) collective-permute-start(bf16[768,1536]{1,0:T(8,128)(2,1)} %bitcast.31), channel_id=1, source_target_pairs={{0,4},{4,0},{1,5},{5,1},{2,6},{6,2},{3,7},{7,3},{8,12},{12,8},{9,1... | collective-permute-start | bytes 7077896 | tf_op jit(solution)/shard_map/ppermute | solution.py:22
  16.4 69.6 %collective-permute-start.5 = (bf16[1536,768]{1,0:T(8,128)(2,1)}, bf16[1536,768]{1,0:T(8,128)(2,1)}, u32[]{:S(2)}, u32[]{:S(2)}) collective-permute-start(bf16[1536,768]{1,0:T(8,128)(2,1)} %bitcast.33), channel_id=1, source_target_pairs={{0,4},{4,0},{1,5},{5,1},{2,6},{6,2},{3,7},{7,3},{8,12},{12,8},{9,1... | collective-permute-start | bytes 7077896 | tf_op jit(solution)/shard_map/ppermute | solution.py:22
  16.6 30.5 %collective-permute-start.2 = (bf16[384,768]{1,0:T(8,128)(2,1)}, bf16[384,768]{1,0:T(8,128)(2,1)}, u32[]{:S(2)}, u32[]{:S(2)}) collective-permute-start(bf16[384,768]{1,0:T(8,128)(2,1)} %out_own.1), channel_id=1, source_target_pairs={{0,4},{4,0},{1,5},{5,1},{2,6},{6,2},{3,7},{7,3},{8,12},{12,8},{9,1... | collective-permute-start | bytes 1769480 | tf_op jit(solution)/shard_map/ppermute | solution.py:22
  26.7 14.2 %all-to-all-start.1 = ((bf16[32,16,128]{2,1,0:T(8,128)(2,1)}), bf16[32,16,128]{2,1,0:T(8,128)(2,1)S(1)}, u32[]{:S(2)}, u32[]{:S(2)}) async-start(bf16[32,16,128]{2,1,0:T(8,128)(2,1)} %prefix.1), calls=%async_computation.1 | async-start | bytes 262144 | tf_op jit(solution)/shard_map/all_to_all | solution.py:26
  31.5 15.5 %copy-start.3 = (bf16[384,768]{1,0:T(8,128)(2,1)S(1)}, bf16[384,768]{1,0:T(8,128)(2,1)}, u32[]{:S(2)}) copy-start(bf16[384,768]{1,0:T(8,128)(2,1)} %out_own.1) | copy-start | bytes 1769476
  31.5 15.5 %copy-start.6 = (f32[768]{0:T(1024)S(1)}, f32[768]{0:T(1024)}, u32[]{:S(2)}) copy-start(f32[768]{0:T(1024)} %gain.5) | copy-start | bytes 9220
  40.9 6.1 %collective-permute-start.1 = (bf16[32,16,128]{2,1,0:T(8,128)(2,1)S(1)}, bf16[32,16,128]{2,1,0:T(8,128)(2,1)S(1)}, u32[]{:S(2)}, u32[]{:S(2)}) collective-permute-start(bf16[32,16,128]{2,1,0:T(8,128)(2,1)S(1)} %all-to-all-done.1), channel_id=1, source_target_pairs={{0,4},{4,0},{1,5},{5,1},{2,6},{6,2},{3,7},{7,3},{8,12},{12,8},{9,1... | collective-permute-start | bytes 393224 | tf_op jit(solution)/shard_map/ppermute | solution.py:22
  98.1 7.6 %copy-start.8 = (bf16[256,768]{1,0:T(8,128)(2,1)S(1)}, bf16[256,768]{1,0:T(8,128)(2,1)}, u32[]{:S(2)}) copy-start(bf16[256,768]{1,0:T(8,128)(2,1)} %get-tuple-element.13) | copy-start | bytes 1179652
  99.1 32.0 %copy-start.7 = (f32[256,768]{1,0:T(8,128)S(1)}, f32[256,768]{1,0:T(8,128)}, u32[]{:S(2)}) copy-start(f32[256,768]{1,0:T(8,128)} %get-tuple-element.12) | copy-start | bytes 2359300
  99.1 31.4 %all-to-all-start.3 = ((bf16[128,4,768]{2,1,0:T(4,128)(2,1)}), bf16[128,4,768]{2,1,0:T(4,128)(2,1)S(1)}, u32[]{:S(2)}, u32[]{:S(2)}) async-start(bf16[128,4,768]{2,1,0:T(4,128)(2,1)} %reshape.65), calls=%async_computation.3 | async-start | bytes 1572864 | tf_op jit(solution)/shard_map/all_to_all | solution.py:26

commit v4 on v3

--- a/solution.py
+++ b/solution.py
@@ -26,61 +26,71 @@
     return lax.all_to_all(pieces, axes, split_axis=0, concat_axis=0, tiled=True)
 
 
-def expert_kernel(blocks, rows, gate_a, up_a, down_a, gate_b, up_b, down_b, out, total):
-    step = pl.program_id(0)
-
-    def add_part(gate, up, down):
+def expert_kernel(rows, gate_a, up_a, down_a, gate_b, up_b, down_b, out, gate, up, down, total, sems):
+    blocks = gate.shape[0]
+    own_blocks = blocks // 2
+    first = FF_BLOCK // 2
+
+    def copies(k):
+        gates, ups, downs = (gate_a, up_a, down_a) if k < own_blocks else (gate_b, up_b, down_b)
+        base = (k % own_blocks) * FF_BLOCK
+        spans = ((0, first), (first, first)) if k == 0 else ((0, FF_BLOCK),)
+        for n, (at, size) in enumerate(spans):
+            row = 0 if k == 0 and n == 0 else k + 1
+            to, source = pl.ds(at, size), pl.ds(base + at, size)
+            yield pltpu.make_async_copy(gates.at[:, source], gate.at[k, :, to], sems.at[row, 0])
+            yield pltpu.make_async_copy(ups.at[:, source], up.at[k, :, to], sems.at[row, 1])
+            yield pltpu.make_async_copy(downs.at[source, :], down.at[k, to, :], sems.at[row, 2])
+
+    started = [list(copies(k)) for k in range(blocks)]
+    for some in started:
+        for copy in some:
+            copy.start()
+
+    def part(gates, ups, downs):
         x = rows[...]
-        g = jnp.dot(x, gate[...], preferred_element_type=jnp.float32)
-        u = jnp.dot(x, up[...], preferred_element_type=jnp.float32)
+        g = jnp.dot(x, gates, preferred_element_type=jnp.float32)
+        u = jnp.dot(x, ups, preferred_element_type=jnp.float32)
         hidden = (g * (0.5 + 0.5 * jnp.tanh(0.5 * g)) * u).astype(jnp.bfloat16)
-        return jnp.dot(hidden, down[...], preferred_element_type=jnp.float32)
-
-    @pl.when(step == 0)
-    def _():
-        total[...] = add_part(gate_a, up_a, down_a)
-
-    @pl.when(jnp.logical_and(step > 0, step < blocks))
-    def _():
-        total[...] += add_part(gate_a, up_a, down_a)
-
-    @pl.when(step >= blocks)
-    def _():
-        total[...] += add_part(gate_b, up_b, down_b)
-
-    @pl.when(step == 2 * blocks - 1)
-    def _():
-        out[...] = total[...].astype(out.dtype)
+        return jnp.dot(hidden, downs, preferred_element_type=jnp.float32)
+
+    for copy in started[0][:3]:
+        copy.wait()
+    total[...] = part(gate[0, :, :first], up[0, :, :first], down[0, :first, :])
+    for copy in started[0][3:]:
+        copy.wait()
+    total[...] += part(gate[0, :, first:], up[0, :, first:], down[0, first:, :])
+
+    def step(k, carry):
+        whole = pl.ds(0, FF_BLOCK)
+        pltpu.make_async_copy(gate_a.at[:, whole], gate.at[k], sems.at[k + 1, 0]).wait()
+        pltpu.make_async_copy(up_a.at[:, whole], up.at[k], sems.at[k + 1, 1]).wait()
+        pltpu.make_async_copy(down_a.at[whole, :], down.at[k], sems.at[k + 1, 2]).wait()
+        total[...] += part(gate[k], up[k], down[k])
+        return carry
+
+    lax.fori_loop(1, blocks, step, 0)
+    out[...] = total[...].astype(out.dtype)
 
 
 def expert_of(rows, own, partner):
     count, width = rows.shape
     units = own[0].shape[1]
-    blocks = units // FF_BLOCK
-
-    def first(step):
-        return jnp.minimum(step, blocks - 1)
-
-    def second(step):
-        return jnp.maximum(step - blocks, 0)
-
-    def specs(place):
-        return [
-            pl.BlockSpec((width, FF_BLOCK), lambda i: (0, place(i))),
-            pl.BlockSpec((width, FF_BLOCK), lambda i: (0, place(i))),
-            pl.BlockSpec((FF_BLOCK, width), lambda i: (place(i), 0)),
-        ]
-
+    blocks = 2 * units // FF_BLOCK
+    local = pl.BlockSpec(memory_space=pltpu.VMEM)
     return pl.pallas_call(
-        lambda *refs: expert_kernel(blocks, *refs),
-        grid=(2 * blocks,),
-        in_specs=[pl.BlockSpec((count, width), lambda i: (0, 0))] + specs(first) + specs(second),
-        out_specs=pl.BlockSpec((count, width), lambda i: (0, 0)),
+        expert_kernel,
+        in_specs=[local] + [pl.BlockSpec(memory_space=pl.ANY)] * 6,
+        out_specs=local,
         out_shape=jax.ShapeDtypeStruct((count, width), jnp.bfloat16),
-        scratch_shapes=[pltpu.VMEM((count, width), jnp.float32)],
-        compiler_params=pltpu.CompilerParams(
-            dimension_semantics=("arbitrary",), vmem_limit_bytes=32 * MIB
-        ),
+        scratch_shapes=[
+            pltpu.VMEM((blocks, width, FF_BLOCK), jnp.bfloat16),
+            pltpu.VMEM((blocks, width, FF_BLOCK), jnp.bfloat16),
+            pltpu.VMEM((blocks, FF_BLOCK, width), jnp.bfloat16),
+            pltpu.VMEM((count, width), jnp.float32),
+            pltpu.SemaphoreType.DMA((blocks + 1, 3)),
+        ],
+        compiler_params=pltpu.CompilerParams(vmem_limit_bytes=36 * MIB),
         cost_estimate=pl.CostEstimate(
             flops=2 * count * width * units * 6,
             bytes_accessed=12 * width * units,
@@ -90,6 +100,16 @@
     )(rows, *(in_hbm(w) for w in own), *(in_hbm(w) for w in partner))
 
 
+def in_parts(source, target, sems, parts):
+    size = source.shape[0] // parts
+    return [
+        pltpu.make_async_copy(
+            source.at[pl.ds(k * size, size)], target.at[pl.ds(k * size, size)], sems.at[k]
+        )
+        for k in range(parts)
+    ]
+
+
 def in_hbm(array):
     return pltpu.with_memory_space_constraint(array, pltpu.HBM)
 
@@ -102,17 +122,22 @@
 
 def state_kernel(series, weight, gain, state_out, rows, table, sems):
     half = table.shape[2]
-    fetch_rows = pltpu.make_async_copy(series, rows, sems.at[0])
-    fetch_keys = pltpu.make_async_copy(weight.at[1], table.at[0], sems.at[1])
-    fetch_values = pltpu.make_async_copy(weight.at[2], table.at[1], sems.at[2])
-    fetch_rows.start()
-    fetch_keys.start()
-    fetch_values.start()
-    fetch_rows.wait()
+    fetches = [
+        in_parts(series, rows, sems.at[0], 4),
+        in_parts(weight.at[1], table.at[0], sems.at[1], 4),
+        in_parts(weight.at[2], table.at[1], sems.at[2], 4),
+    ]
+    for some in fetches:
+        for fetch in some:
+            fetch.start()
+    for fetch in fetches[0]:
+        fetch.wait()
     normed = normed_rows(rows[...], gain[...]).astype(jnp.bfloat16)
-    fetch_keys.wait()
+    for fetch in fetches[1]:
+        fetch.wait()
     keys = jnp.dot(normed, table[0], preferred_element_type=jnp.float32).astype(jnp.bfloat16)
-    fetch_values.wait()
+    for fetch in fetches[2]:
+        fetch.wait()
     values = jnp.dot(normed, table[1], preferred_element_type=jnp.float32).astype(jnp.bfloat16)
     heads = half // HD
     for n in range(heads):
@@ -138,7 +163,7 @@
         scratch_shapes=[
             pltpu.VMEM((count, width), jnp.bfloat16),
             pltpu.VMEM((2, width, half), jnp.bfloat16),
-            pltpu.SemaphoreType.DMA((3,)),
+            pltpu.SemaphoreType.DMA((3, 4)),
         ],
         compiler_params=pltpu.CompilerParams(vmem_limit_bytes=24 * MIB),
         cost_estimate=pl.CostEstimate(
@@ -246,83 +271,125 @@
     series,
     gain,
     slots,
+    ids,
+    router,
     residual_out,
-    normed_out,
+    gate_out,
     send_out,
     queries_in,
     inside_in,
+    weights_in,
+    rows_in,
     residual_held,
-    normed_held,
+    gate_held,
     sems,
 ):
-    own_rows, _ = queries_in.shape
+    own_rows, _ = rows_in.shape
     half = out_own.shape[0]
     heads = half // HD
     first_row = pl.multiple_of(lax.axis_index("head") * own_rows, own_rows)
     fetches = [
-        pltpu.make_async_copy(queries, queries_in, sems.at[0]),
-        pltpu.make_async_copy(inside, inside_in, sems.at[1]),
+        in_parts(queries, queries_in, sems.at[0], 2),
+        in_parts(inside, inside_in, sems.at[1], 4),
+        in_parts(out_own, weights_in.at[0], sems.at[2], 2),
+        in_parts(out_other, weights_in.at[1], sems.at[3], 2),
+        in_parts(series.at[pl.ds(first_row, own_rows)], rows_in, sems.at[4], 2),
     ]
-    for fetch in fetches:
-        fetch.start()
+    for some in fetches:
+        for fetch in some:
+            fetch.start()
+
+    def arrived(k):
+        for fetch in fetches[k]:
+            fetch.wait()
+
     base = lax.axis_index(SEQ) * series.shape[0] + first_row + 1
     position = lax.broadcasted_iota(jnp.int32, (own_rows, HD), 0) + base
     unit = 1.0 / (position.astype(jnp.float32) * math.sqrt(HD))
     slot = lax.broadcasted_iota(jnp.int32, (send_out.shape[0], own_rows), 0)
     chosen = jnp.where(slot == slots[...], 1.0, 0.0).astype(jnp.bfloat16)
-    fetches[0].wait()
-    fetches[1].wait()
-    mixed = []
+    arrived(0)
+    carried = []
     for part, state in ((0, state_own), (1, state_other)):
         for n in range(heads):
             lanes = slice(part * half + n * HD, part * half + (n + 1) * HD)
             start = state[n * HD : (n + 1) * HD, :]
-            carried = jnp.dot(queries_in[:, lanes], start, preferred_element_type=jnp.float32)
-            mixed.append(((inside_in[:, lanes] + carried) * unit).astype(jnp.bfloat16))
-    total = series[pl.ds(first_row, own_rows), :].astype(jnp.float32)
-    for mine, weight in ((mixed[:heads], out_own), (mixed[heads:], out_other)):
-        total += jnp.dot(
-            jnp.concatenate(mine, axis=1), weight[...], preferred_element_type=jnp.float32
-        )
+            carried.append(
+                jnp.dot(queries_in[:, lanes], start, preferred_element_type=jnp.float32)
+            )
+    arrived(1)
+    mixed = [
+        ((inside_in[:, k * HD : (k + 1) * HD] + carried[k]) * unit).astype(jnp.bfloat16)
+        for k in range(2 * heads)
+    ]
+    arrived(2)
+    total = jnp.dot(
+        jnp.concatenate(mixed[:heads], axis=1), weights_in[0], preferred_element_type=jnp.float32
+    )
+    arrived(3)
+    total += jnp.dot(
+        jnp.concatenate(mixed[heads:], axis=1), weights_in[1], preferred_element_type=jnp.float32
+    )
+    arrived(4)
+    total += rows_in[...].astype(jnp.float32)
     residual_held[...] = total
-    keep_residual = pltpu.make_async_copy(residual_held, residual_out, sems.at[2])
-    keep_residual.start()
+    keep_residual = in_parts(residual_held, residual_out, sems.at[5], 4)
+    for keep in keep_residual:
+        keep.start()
     normed = normed_rows(total, gain[...]).astype(jnp.bfloat16)
-    normed_held[...] = normed
-    keep_normed = pltpu.make_async_copy(normed_held, normed_out, sems.at[3])
-    keep_normed.start()
+    logits = jnp.dot(normed, router[...], preferred_element_type=jnp.float32)
+    expert = lax.broadcasted_iota(jnp.int32, logits.shape, 1)
+    logit = jnp.sum(jnp.where(expert == ids[...], logits, 0.0), axis=1, keepdims=True)
+    gate_held[...] = jnp.broadcast_to(jax.nn.sigmoid(logit), gate_held.shape)
+    keep_gate = pltpu.make_async_copy(gate_held, gate_out, sems.at[6, 0])
+    keep_gate.start()
     send_out[...] = jnp.dot(chosen, normed, preferred_element_type=jnp.float32).astype(
         jnp.bfloat16
     )
-    keep_residual.wait()
-    keep_normed.wait()
+    for keep in keep_residual:
+        keep.wait()
+    keep_gate.wait()
 
 
 def mix_heads(
-    queries, inside, state_own, state_other, out_own, out_other, series, gain, slots, slot_count
+    queries,
+    inside,
+    state_own,
+    state_other,
+    out_own,
+    out_other,
+    series,
+    gain,
+    slots,
+    ids,
+    router,
+    slot_count,
 ):
     own_rows, width = queries.shape
+    half = out_own.shape[0]
     anywhere = pl.BlockSpec(memory_space=pl.ANY)
     local = pl.BlockSpec(memory_space=pltpu.VMEM)
     return pl.pallas_call(
         mix_kernel,
-        in_specs=[anywhere] * 2 + [local] * 7,
+        in_specs=[anywhere] * 2 + [local] * 2 + [anywhere] * 3 + [local] * 4,
         out_specs=[anywhere, anywhere, local],
         out_shape=[
             pltpu.HBM((own_rows, width), jnp.float32),
-            pltpu.HBM((own_rows, width), jnp.bfloat16),
+            pltpu.HBM((own_rows, HD), jnp.float32),
             jax.ShapeDtypeStruct((slot_count, width), jnp.bfloat16),
         ],
         scratch_shapes=[
             pltpu.VMEM((own_rows, width), jnp.bfloat16),
             pltpu.VMEM((own_rows, width), jnp.float32),
+            pltpu.VMEM((2, half, width), jnp.bfloat16),
+            pltpu.VMEM((own_rows, width), jnp.bfloat16),
             pltpu.VMEM((own_rows, width), jnp.float32),
-            pltpu.VMEM((own_rows, width), jnp.bfloat16),
-            pltpu.SemaphoreType.DMA((4,)),
+            pltpu.VMEM((own_rows, HD), jnp.float32),
+            pltpu.SemaphoreType.DMA((7, 4)),
         ],
         compiler_params=pltpu.CompilerParams(vmem_limit_bytes=24 * MIB),
         cost_estimate=pl.CostEstimate(
-            flops=2 * own_rows * width * (width + HD + slot_count),
+            flops=2 * own_rows * width * (width + 2 * HD + slot_count),
             bytes_accessed=12 * own_rows * width,
             transcendentals=own_rows,
         ),
@@ -332,12 +399,63 @@
         in_hbm(inside),
         state_own,
         state_other,
-        out_own,
-        out_other,
-        series,
+        in_hbm(out_own),
+        in_hbm(out_other),
+        in_hbm(series),
         gain,
         slots,
-    )
+        ids,
+        router,
+    )
+
+
+def combine_kernel(returned, residual, gate, slots, out, residual_in, gate_in, held, sems):
+    own_rows, width = residual_in.shape
+    fetches = in_parts(residual, residual_in, sems.at[0], 4)
+    fetch_gate = pltpu.make_async_copy(gate, gate_in, sems.at[1, 0])
+    for fetch in fetches:
+        fetch.start()
+    fetch_gate.start()
+    slot = lax.broadcasted_iota(jnp.int32, (returned.shape[0], own_rows), 0)
+    chosen = jnp.where(slot == slots[...], 1.0, 0.0).astype(jnp.bfloat16)
+    routed = lax.dot_general(
+        chosen, returned[...], (((0,), (0,)), ((), ())), preferred_element_type=jnp.float32
+    )
+    fetch_gate.wait()
+    for fetch in fetches:
+        fetch.wait()
+    weight = jnp.concatenate([gate_in[...]] * (width // HD), axis=1)
+    held[...] = (residual_in[...] + weight * routed).astype(jnp.bfloat16)
+    leave = in_parts(held, out, sems.at[2], 4)
+    for copy in leave:
+        copy.start()
+    for copy in leave:
+        copy.wait()
+
+
+def combine(returned, residual, gate, slots):
+    own_rows, width = residual.shape
+    anywhere = pl.BlockSpec(memory_space=pl.ANY)
+    local = pl.BlockSpec(memory_space=pltpu.VMEM)
+    return pl.pallas_call(
+        combine_kernel,
+        in_specs=[local, anywhere, anywhere, local],
+        out_specs=anywhere,
+        out_shape=pltpu.HBM((own_rows, width), jnp.bfloat16),
+        scratch_shapes=[
+            pltpu.VMEM((own_rows, width), jnp.float32),
+            pltpu.VMEM((own_rows, HD), jnp.float32),
+            pltpu.VMEM((own_rows, width), jnp.bfloat16),
+            pltpu.SemaphoreType.DMA((3, 4)),
+        ],
+        compiler_params=pltpu.CompilerParams(vmem_limit_bytes=24 * MIB),
+        cost_estimate=pl.CostEstimate(
+            flops=2 * own_rows * width * returned.shape[0],
+            bytes_accessed=10 * own_rows * width,
+            transcendentals=0,
+        ),
+        name="combine",
+    )(returned, in_hbm(residual), in_hbm(gate), slots)
 
 
 def on_device(
@@ -377,7 +495,8 @@
     slot_rank = jnp.sum(jnp.logical_and(same_expert, earlier_row), axis=1)
     slot_index = route_ids * capacity + slot_rank
 
-    residual, normed_moe, send_buffer = mix_heads(
+    slots = slot_index[None, :]
+    residual, gate, send_buffer = mix_heads(
         queries,
         inside,
         state_own.reshape(state.shape),
@@ -386,27 +505,16 @@
         out_other,
         series[0],
         norm_moe,
-        slot_index[None, :],
+        slots,
+        route_ids[:, None],
+        router_weight,
         expert_count * capacity,
     )
     received = exchange(send_buffer.reshape(expert_count, capacity, width), SEQ_DP)
 
-    logits = jnp.dot(normed_moe, router_weight, preferred_element_type=jnp.float32)
-    picked_expert = route_ids[:, None] == jnp.arange(expert_count, dtype=jnp.int32)[None, :]
-    gate_value = jax.nn.sigmoid(
-        jnp.sum(jnp.where(picked_expert, logits, 0.0), axis=1, keepdims=True)
-    )
     expert_out = expert_of(received.reshape(-1, width), own_expert, other_expert)
     returned = exchange(expert_out.reshape(received.shape), SEQ_DP)
-    routing = (
-        slot_index[:, None] == jnp.arange(expert_count * capacity, dtype=jnp.int32)[None, :]
-    ).astype(jnp.bfloat16)
-    routed = jnp.dot(
-        routing,
-        returned.reshape(expert_count * capacity, width),
-        preferred_element_type=jnp.float32,
-    )
-    layer_out = (residual + gate_value * routed).astype(jnp.bfloat16)
+    layer_out = combine(returned.reshape(send_buffer.shape), residual, gate, slots)
     return layer_out[None]
 
 

time: 133 us -> 131 us (0.985)
  blocking collectives: 34.4 us -> 65.5 us
  waiting for transfers between devices: 42.9 us -> 18.4 us
  starting transfers between devices: 23.7 us -> 17 us
    all_to_all x1 -> x2, blocking collectives: 34.4 us -> 65.5 us  [exchange(): return lax.all_to_all(pieces, axes, split_axis=0, concat_axis=0, tiled=True)]
    all_to_all x3 -> x2, waiting for transfers between devices: 42.9 us -> 18.4 us  [exchange(): return lax.all_to_all(pieces, axes, split_axis=0, concat_axis=0, tiled=True)]
    all_to_all x3 -> x2, starting transfers between devices: 22.5 us -> 15.9 us  [exchange(): return lax.all_to_all(pieces, axes, split_axis=0, concat_axis=0, tiled=True)]
    pallas_call x2 -> x3, Pallas kernels: 16.2 us -> 17.1 us  [the longest x1 10.9 us: expert_of(): pl.pallas_call(expert_kernel, in_specs=[local] + [pl.BlockSpec(memory_spa...]
  transfers between devices with their start and end apart: 9 -> 8, of which waited for: 3 -> 2; matrix products, arithmetic and copies ran while one was open for 1% -> 1% of each run, Pallas kernels for 11% -> 11%
where the time goes in v4:
time: 131 us
  blocking collectives  65.5 us (50%)
  Pallas kernels  27.5 us (21%)
  waiting for transfers between devices  18.4 us (14%)
  starting transfers between devices  17 us (13%)
  local copies, waits for them, and re-layouts  1.72 us (1%)
    all_to_all x2, blocking collectives, exchange(): return lax.all_to_all(pieces, axes, split_axis=0, concat_axis=0, tiled=True)  65.5 us
    all_to_all x2, waiting for transfers between devices, exchange(): return lax.all_to_all(pieces, axes, split_axis=0, concat_axis=0, tiled=True)  18.4 us
    all_to_all x2, starting transfers between devices, exchange(): return lax.all_to_all(pieces, axes, split_axis=0, concat_axis=0, tiled=True)  15.9 us
    pallas_call x1, Pallas kernels, expert_of(): pl.pallas_call(expert_kernel, in_specs=[local] + [pl.BlockSpec(memory_spa...  10.9 us
    pallas_call x1, Pallas kernels, inside_block(): pl.pallas_call(inside_kernel, in_specs=[pl.BlockSpec(memory_space=pltpu.V...  6.01 us
    pallas_call x1, Pallas kernels, mix_heads(): pl.pallas_call(mix_kernel, in_specs=[anywhere] * 2 + [local] * 2 + [anywh...  3.86 us
    pallas_call x1, Pallas kernels, block_state(): pl.pallas_call(state_kernel, in_specs=[pl.BlockSpec(memory_space=pl.ANY),...  3.68 us
  transfers between devices with their start and end apart: 8, of which 2 were waited for; matrix products, arithmetic and copies ran while one was open for 1% of the time, Pallas kernels for 11%

profile of v4, /device:TPU:32, one launch (start us, length us, event | category | flops | bytes accessed | tf_op | source)
XLA Modules:
  0.0 130.7 jit_solution(15436806593456914726)
XLA Ops:
  0.0 0.0 copy-start.1
  0.0 0.0 copy-start
  0.0 0.0 collective-permute-start
  0.0 0.0 copy-start.3
  0.0 0.8 copy-done.3
  0.9 0.0 copy-start.6
  0.9 0.0 copy-start.4
  0.9 3.7 %block_state.1 = bf16[512,128]{1,0:T(8,128)(2,1)} custom-call(bf16[512,768]{1,0:T(8,128)(2,1)} %bitcast.14, bf16[3,768,384]{2,1,0:T(8,128)(2,1)} %bitcast.18, f32[768]{0:T(1024)S(1)} %copy-done.3), custom_call_target="tpu_custom_call" | custom-call | flops 603979776 | bytes 1572864 | tf_op jit(solution)/shard_map/block_state/pallas_call | solution.py:154
  4.5 11.4 %all-to-all-start = ((bf16[32,16,128]{2,1,0:T(8,128)(2,1)}), bf16[32,16,128]{2,1,0:T(8,128)(2,1)S(1)}, u32[]{:S(2)}, u32[]{:S(2)}) async-start(bf16[32,16,128]{2,1,0:T(8,128)(2,1)} %bitcast.2), calls=%async_computation | async-start | bytes 262144 | tf_op jit(solution)/shard_map/all_to_all | solution.py:26
  15.9 0.1 collective-permute-start.3
  16.0 0.5 collective-permute-start.4
  16.5 0.1 collective-permute-start.5
  16.6 0.4 collective-permute-start.2
  17.0 9.1 %all-to-all-done.pieces = bf16[32,16,128]{2,1,0:T(8,128)(2,1)S(1)} async-done(((bf16[32,16,128]{2,1,0:T(8,128)(2,1)}), bf16[32,16,128]{2,1,0:T(8,128)(2,1)S(1)}, u32[]{:S(2)}, u32[]{:S(2)}) %all-to-all-start) | async-done | bytes 131104 | tf_op jit(solution)/shard_map/all_to_all | solution.py:26
  26.1 0.7 prefix.1
  26.8 4.6 %all-to-all-start.1 = ((bf16[32,16,128]{2,1,0:T(8,128)(2,1)}), bf16[32,16,128]{2,1,0:T(8,128)(2,1)S(1)}, u32[]{:S(2)}, u32[]{:S(2)}) async-start(bf16[32,16,128]{2,1,0:T(8,128)(2,1)} %prefix.1), calls=%async_computation.1 | async-start | bytes 262144 | tf_op jit(solution)/shard_map/all_to_all | solution.py:26
  31.4 0.0 copy-done.6
  31.4 0.2 convert_reduce_fusion
  31.6 0.1 copy.12.ids
  31.7 0.0 copy-start.2
  31.7 0.0 copy-start.5
  31.8 9.3 %all-to-all-done.1 = bf16[32,16,128]{2,1,0:T(8,128)(2,1)S(1)} async-done(((bf16[32,16,128]{2,1,0:T(8,128)(2,1)}), bf16[32,16,128]{2,1,0:T(8,128)(2,1)S(1)}, u32[]{:S(2)}, u32[]{:S(2)}) %all-to-all-start.1) | async-done | bytes 131104 | tf_op jit(solution)/shard_map/all_to_all | solution.py:26
  41.0 0.0 collective-permute-done.w_other
  41.0 0.0 collective-permute-start.1
  41.0 0.0 copy-done.1
  41.0 0.0 copy-done
  41.0 0.0 copy-done.4
  41.0 6.0 %inside_block.1 = (bf16[256,768]{1,0:T(8,128)(2,1)}, f32[256,768]{1,0:T(8,128)}) custom-call(bf16[512,768]{1,0:T(8,128)(2,1)S(1)} %bitcast.16, f32[768]{0:T(1024)S(1)} %copy-done.4, bf16[3,768,384]{2,1,0:T(8,128)(2,1)S(1)} %bitcast.19, bf16[3,768,384]{2,1,0:T(8,128)(2,1)} %collective-permute-done.w_other), custom_call_target="tpu_custom_call" | custom-call | flops 1912602624 | bytes 3145728 | tf_op jit(solution)/shard_map/inside_block/pallas_call | solution.py:241
  47.1 0.0 collective-permute-done.2.out_other
  47.1 0.0 collective-permute-done.1
  47.1 0.0 copy-done.2
  47.1 0.0 copy-done.5
  47.1 3.9 %mix_heads.1 = (f32[256,768]{1,0:T(8,128)}, f32[256,128]{1,0:T(8,128)}, bf16[512,768]{1,0:T(8,128)(2,1)S(1)}) custom-call(bf16[256,768]{1,0:T(8,128)(2,1)} %get-tuple-element.10.queries, f32[256,768]{1,0:T(8,128)} %get-tuple-element.11.inside, bf16[512,128]{1,0:T(8,128)(2,1)S(1)} %bitcast.20, bf16[512,128]{1,0:T(8,128)(2,1)S(1)} %bitcast.21, ...), custom_call_target="tpu_custom_call" | custom-call | flops 603979776 | bytes 2359296 | tf_op jit(solution)/shard_map/mix_heads/pallas_call | solution.py:372
  51.0 0.2 reshape.45
  51.2 34.4 %all_to_all.20 = bf16[128,4,768]{2,1,0:T(4,128)(2,1)S(1)} all-to-all(bf16[128,4,768]{2,1,0:T(4,128)(2,1)S(1)} %reshape.45), channel_id=1, replica_groups=mesh['seq_0'=8,'seq_1'=4,'head'=2,'dp'=4] {'seq_0','seq_1','dp'}, dimensions={0} | all-to-all | bytes 1572864 | tf_op jit(solution)/shard_map/all_to_all | solution.py:26
  85.6 0.2 reshape.46.rows
  85.8 0.0 collective-permute-done.3.gate_b
  85.8 0.0 collective-permute-done.4.up_b
  85.8 0.0 collective-permute-done.5.down_b
  85.8 10.9 %expert_mlp.1 = bf16[512,768]{1,0:T(8,128)(2,1)S(1)} custom-call(bf16[512,768]{1,0:T(8,128)(2,1)S(1)} %reshape.46.rows, bf16[768,1536]{1,0:T(8,128)(2,1)} %bitcast.26, bf16[768,1536]{1,0:T(8,128)(2,1)} %bitcast.28, bf16[1536,768]{1,0:T(8,128)(2,1)} %bitcast.30, bf16[768,1536]{1,0:T(8,128)(2,1)} %collective-permute-done.3.gate_b, ...), custom_call_target="tpu_custom_call" | custom-call | flops 7247757312 | bytes 14155776 | tf_op jit(solution)/shard_map/expert_mlp/pallas_call | solution.py:81
  96.7 0.2 reshape.47
  96.9 31.0 %all_to_all.21 = bf16[128,4,768]{2,1,0:T(4,128)(2,1)S(1)} all-to-all(bf16[128,4,768]{2,1,0:T(4,128)(2,1)S(1)} %reshape.47), channel_id=1, replica_groups=mesh['seq_0'=8,'seq_1'=4,'head'=2,'dp'=4] {'seq_0','seq_1','dp'}, dimensions={0} | all-to-all | bytes 1572864 | tf_op jit(solution)/shard_map/all_to_all | solution.py:26
  128.0 0.2 reshape.48.returned
  128.1 2.4 %combine.1 = bf16[256,768]{1,0:T(8,128)(2,1)} custom-call(bf16[512,768]{1,0:T(8,128)(2,1)S(1)} %reshape.48.returned, f32[256,768]{1,0:T(8,128)} %get-tuple-element.13.residual, f32[256,128]{1,0:T(8,128)} %get-tuple-element.14.gate, s32[1,256]{1,0:T(1,128)S(1)} %bitcast_add_fusion.slots), custom_call_target="tpu_custom_call" | custom-call | flops 201326592 | bytes 1966080 | tf_op jit(solution)/shard_map/combine/pallas_call | solution.py:440
  (1 shorter events, 0.0 us)
Async XLA Ops:
  0.0 41.0 %copy-start.1 = (bf16[768,3,384]{2,0,1:T(8,128)(2,1)S(1)}, bf16[768,3,384]{2,0,1:T(8,128)(2,1)}, u32[]{:S(2)}) copy-start(bf16[768,3,384]{2,0,1:T(8,128)(2,1)} %param.12) | copy-start | bytes 5308420
  0.0 41.0 %copy-start = (bf16[1,512,768]{2,1,0:T(8,128)(2,1)S(1)}, bf16[1,512,768]{2,1,0:T(8,128)(2,1)}, u32[]{:S(2)}) copy-start(bf16[1,512,768]{2,1,0:T(8,128)(2,1)} %param.10) | copy-start | bytes 2359300
  0.0 41.0 %collective-permute-start = (bf16[3,768,384]{2,1,0:T(8,128)(2,1)}, bf16[3,768,384]{2,1,0:T(8,128)(2,1)}, u32[]{:S(2)}, u32[]{:S(2)}) collective-permute-start(bf16[3,768,384]{2,1,0:T(8,128)(2,1)} %bitcast.17), channel_id=1, source_target_pairs={{0,4},{4,0},{1,5},{5,1},{2,6},{6,2},{3,7},{7,3},{8,12},{12,8},{9,1... | collective-permute-start | bytes 5308424 | tf_op jit(solution)/shard_map/ppermute | solution.py:22
  0.0 0.8 copy-start.3
  0.9 30.5 %copy-start.6 = (s32[1,256,1]{1,2,0:T(1,128)S(1)}, s32[1,256,1]{1,2,0:T(1,128)}, u32[]{:S(2)}) copy-start(s32[1,256,1]{1,2,0:T(1,128)} %param.16) | copy-start | bytes 3076
  0.9 40.2 %copy-start.4 = (f32[768]{0:T(1024)S(1)}, f32[768]{0:T(1024)}, u32[]{:S(2)}) copy-start(f32[768]{0:T(1024)} %gain.4) | copy-start | bytes 9220
  4.5 21.6 %all-to-all-start = ((bf16[32,16,128]{2,1,0:T(8,128)(2,1)}), bf16[32,16,128]{2,1,0:T(8,128)(2,1)S(1)}, u32[]{:S(2)}, u32[]{:S(2)}) async-start(bf16[32,16,128]{2,1,0:T(8,128)(2,1)} %bitcast.2), calls=%async_computation | async-start | bytes 262144 | tf_op jit(solution)/shard_map/all_to_all | solution.py:26
  15.9 69.9 %collective-permute-start.3 = (bf16[768,1536]{1,0:T(8,128)(2,1)}, bf16[768,1536]{1,0:T(8,128)(2,1)}, u32[]{:S(2)}, u32[]{:S(2)}) collective-permute-start(bf16[768,1536]{1,0:T(8,128)(2,1)} %bitcast.25), channel_id=1, source_target_pairs={{0,4},{4,0},{1,5},{5,1},{2,6},{6,2},{3,7},{7,3},{8,12},{12,8},{9,1... | collective-permute-start | bytes 7077896 | tf_op jit(solution)/shard_map/ppermute | solution.py:22
  16.0 69.8 %collective-permute-start.4 = (bf16[768,1536]{1,0:T(8,128)(2,1)}, bf16[768,1536]{1,0:T(8,128)(2,1)}, u32[]{:S(2)}, u32[]{:S(2)}) collective-permute-start(bf16[768,1536]{1,0:T(8,128)(2,1)} %bitcast.27), channel_id=1, source_target_pairs={{0,4},{4,0},{1,5},{5,1},{2,6},{6,2},{3,7},{7,3},{8,12},{12,8},{9,1... | collective-permute-start | bytes 7077896 | tf_op jit(solution)/shard_map/ppermute | solution.py:22
  16.5 69.3 %collective-permute-start.5 = (bf16[1536,768]{1,0:T(8,128)(2,1)}, bf16[1536,768]{1,0:T(8,128)(2,1)}, u32[]{:S(2)}, u32[]{:S(2)}) collective-permute-start(bf16[1536,768]{1,0:T(8,128)(2,1)} %bitcast.29), channel_id=1, source_target_pairs={{0,4},{4,0},{1,5},{5,1},{2,6},{6,2},{3,7},{7,3},{8,12},{12,8},{9,1... | collective-permute-start | bytes 7077896 | tf_op jit(solution)/shard_map/ppermute | solution.py:22
  16.6 30.4 %collective-permute-start.2 = (bf16[384,768]{1,0:T(8,128)(2,1)}, bf16[384,768]{1,0:T(8,128)(2,1)}, u32[]{:S(2)}, u32[]{:S(2)}) collective-permute-start(bf16[384,768]{1,0:T(8,128)(2,1)} %out_own.1), channel_id=1, source_target_pairs={{0,4},{4,0},{1,5},{5,1},{2,6},{6,2},{3,7},{7,3},{8,12},{12,8},{9,1... | collective-permute-start | bytes 1769480 | tf_op jit(solution)/shard_map/ppermute | solution.py:22
  26.8 14.2 %all-to-all-start.1 = ((bf16[32,16,128]{2,1,0:T(8,128)(2,1)}), bf16[32,16,128]{2,1,0:T(8,128)(2,1)S(1)}, u32[]{:S(2)}, u32[]{:S(2)}) async-start(bf16[32,16,128]{2,1,0:T(8,128)(2,1)} %prefix.1), calls=%async_computation.1 | async-start | bytes 262144 | tf_op jit(solution)/shard_map/all_to_all | solution.py:26
  31.7 15.4 %copy-start.2 = (bf16[768,128]{1,0:T(8,128)(2,1)S(1)}, bf16[768,128]{1,0:T(8,128)(2,1)}, u32[]{:S(2)}) copy-start(bf16[768,128]{1,0:T(8,128)(2,1)} %router.1) | copy-start | bytes 589828
  31.7 15.4 %copy-start.5 = (f32[768]{0:T(1024)S(1)}, f32[768]{0:T(1024)}, u32[]{:S(2)}) copy-start(f32[768]{0:T(1024)} %gain.5) | copy-start | bytes 9220
  41.0 6.1 %collective-permute-start.1 = (bf16[32,16,128]{2,1,0:T(8,128)(2,1)S(1)}, bf16[32,16,128]{2,1,0:T(8,128)(2,1)S(1)}, u32[]{:S(2)}, u32[]{:S(2)}) collective-permute-start(bf16[32,16,128]{2,1,0:T(8,128)(2,1)S(1)} %all-to-all-done.1), channel_id=1, source_target_pairs={{0,4},{4,0},{1,5},{5,1},{2,6},{6,2},{3,7},{7,3},{8,12},{12,8},{9,1... | collective-permute-start | bytes 393224 | tf_op jit(solution)/shard_map/ppermute | solution.py:22

commit v5 on v4

--- a/solution.py
+++ b/solution.py
@@ -120,19 +120,24 @@
     return x * lax.rsqrt(mean + NORM_EPS) * gain.reshape(1, -1)
 
 
-def state_kernel(series, weight, gain, state_out, rows, table, sems):
+def state_kernel(series, weight, gain, state_out, rows, table, gain_in, sems):
     half = table.shape[2]
     fetches = [
         in_parts(series, rows, sems.at[0], 4),
         in_parts(weight.at[1], table.at[0], sems.at[1], 4),
         in_parts(weight.at[2], table.at[1], sems.at[2], 4),
     ]
-    for some in fetches:
+    fetch_gain = pltpu.make_async_copy(gain, gain_in, sems.at[3, 0])
+    for fetch in fetches[0]:
+        fetch.start()
+    fetch_gain.start()
+    for some in fetches[1:]:
         for fetch in some:
             fetch.start()
     for fetch in fetches[0]:
         fetch.wait()
-    normed = normed_rows(rows[...], gain[...]).astype(jnp.bfloat16)
+    fetch_gain.wait()
+    normed = normed_rows(rows[...], gain_in[...]).astype(jnp.bfloat16)
     for fetch in fetches[1]:
         fetch.wait()
     keys = jnp.dot(normed, table[0], preferred_element_type=jnp.float32).astype(jnp.bfloat16)
@@ -156,21 +161,22 @@
         in_specs=[
             pl.BlockSpec(memory_space=pl.ANY),
             pl.BlockSpec(memory_space=pl.ANY),
-            pl.BlockSpec(memory_space=pltpu.VMEM),
+            pl.BlockSpec(memory_space=pl.ANY),
         ],
         out_specs=pl.BlockSpec(memory_space=pltpu.VMEM),
         out_shape=jax.ShapeDtypeStruct((half + HD, HD), jnp.bfloat16),
         scratch_shapes=[
             pltpu.VMEM((count, width), jnp.bfloat16),
             pltpu.VMEM((2, width, half), jnp.bfloat16),
-            pltpu.SemaphoreType.DMA((3, 4)),
+            pltpu.VMEM((width,), jnp.float32),
+            pltpu.SemaphoreType.DMA((4, 4)),
         ],
         compiler_params=pltpu.CompilerParams(vmem_limit_bytes=24 * MIB),
         cost_estimate=pl.CostEstimate(
             flops=4 * count * width * half, bytes_accessed=4 * count * width, transcendentals=count
         ),
         name="block_state",
-    )(in_hbm(series), in_hbm(weight), gain)
+    )(in_hbm(series), in_hbm(weight), in_hbm(gain))
 
 
 def prefix_kernel(pieces, out):
@@ -196,74 +202,69 @@
     )(pieces)
 
 
-def inside_kernel(
-    series, gain, w_own, w_other, queries_out, inside_out, queries_held, inside_held, sems
-):
+def inside_kernel(series, gain, weight, queries_out, inside_out, queries_held, inside_held, sems):
     count, _ = series.shape
-    own_rows = queries_held.shape[0]
-    half = w_own.shape[2]
+    own_rows, half = queries_held.shape
     heads = half // HD
     first_row = pl.multiple_of(lax.axis_index("head") * own_rows, own_rows)
     mine = normed_rows(series[pl.ds(first_row, own_rows), :], gain[...]).astype(jnp.bfloat16)
     normed = normed_rows(series[...], gain[...]).astype(jnp.bfloat16)
     row = lax.broadcasted_iota(jnp.int32, (own_rows, count), 0) + first_row
     causal = row >= lax.broadcasted_iota(jnp.int32, (own_rows, count), 1)
-    for part, weight in ((0, w_own), (1, w_other)):
-        queries, keys, values = (
-            jnp.dot(rows, weight[k], preferred_element_type=jnp.float32).astype(jnp.bfloat16)
-            for k, rows in ((0, mine), (1, normed), (2, normed))
+    queries, keys, values = (
+        jnp.dot(rows, weight[k], preferred_element_type=jnp.float32).astype(jnp.bfloat16)
+        for k, rows in ((0, mine), (1, normed), (2, normed))
+    )
+    queries_held[...] = queries
+    keep_queries = pltpu.make_async_copy(queries_held, queries_out, sems.at[0])
+    keep_queries.start()
+    for n in range(heads):
+        at = slice(n * HD, (n + 1) * HD)
+        scores = lax.dot_general(
+            queries[:, at],
+            keys[:, at],
+            (((1,), (1,)), ((), ())),
+            preferred_element_type=jnp.float32,
         )
-        queries_held[:, part * half : (part + 1) * half] = queries
-        for n in range(heads):
-            at = slice(n * HD, (n + 1) * HD)
-            scores = lax.dot_general(
-                queries[:, at],
-                keys[:, at],
-                (((1,), (1,)), ((), ())),
-                preferred_element_type=jnp.float32,
-            )
-            scores = jnp.where(causal, scores, 0.0).astype(jnp.bfloat16)
-            lanes = slice(part * half + n * HD, part * half + (n + 1) * HD)
-            inside_held[:, lanes] = jnp.dot(
-                scores, values[:, at], preferred_element_type=jnp.float32
-            )
-    keep_queries = pltpu.make_async_copy(queries_held, queries_out, sems.at[0])
+        scores = jnp.where(causal, scores, 0.0).astype(jnp.bfloat16)
+        inside_held[:, at] = jnp.dot(scores, values[:, at], preferred_element_type=jnp.float32)
     keep_inside = pltpu.make_async_copy(inside_held, inside_out, sems.at[1])
-    keep_queries.start()
     keep_inside.start()
     keep_queries.wait()
     keep_inside.wait()
 
 
-def inside_block(series, gain, w_own, w_other, own_rows):
+def inside_block(series, gain, weight, own_rows):
     count, width = series.shape
-    half = w_own.shape[2]
+    half = weight.shape[2]
     return pl.pallas_call(
         inside_kernel,
-        in_specs=[pl.BlockSpec(memory_space=pltpu.VMEM)] * 4,
+        in_specs=[pl.BlockSpec(memory_space=pltpu.VMEM)] * 3,
         out_specs=[pl.BlockSpec(memory_space=pl.ANY)] * 2,
         out_shape=[
-            pltpu.HBM((own_rows, 2 * half), jnp.bfloat16),
-            pltpu.HBM((own_rows, 2 * half), jnp.float32),
+            pltpu.HBM((own_rows, half), jnp.bfloat16),
+            pltpu.HBM((own_rows, half), jnp.float32),
         ],
         scratch_shapes=[
-            pltpu.VMEM((own_rows, 2 * half), jnp.bfloat16),
-            pltpu.VMEM((own_rows, 2 * half), jnp.float32),
+            pltpu.VMEM((own_rows, half), jnp.bfloat16),
+            pltpu.VMEM((own_rows, half), jnp.float32),
             pltpu.SemaphoreType.DMA((2,)),
         ],
         compiler_params=pltpu.CompilerParams(vmem_limit_bytes=24 * MIB),
         cost_estimate=pl.CostEstimate(
-            flops=10 * count * width * half + 8 * own_rows * count * half,
-            bytes_accessed=8 * count * width,
+            flops=5 * count * width * half + 4 * own_rows * count * half,
+            bytes_accessed=4 * count * width,
             transcendentals=0,
         ),
         name="inside_block",
-    )(series, gain, w_own, w_other)
+    )(in_hbm(series), gain, in_hbm(weight))
 
 
 def mix_kernel(
-    queries,
-    inside,
+    queries_own,
+    inside_own,
+    queries_other,
+    inside_other,
     state_own,
     state_other,
     out_own,
@@ -273,6 +274,7 @@
     slots,
     ids,
     router,
+    slot_column,
     residual_out,
     gate_out,
     send_out,
@@ -289,11 +291,13 @@
     heads = half // HD
     first_row = pl.multiple_of(lax.axis_index("head") * own_rows, own_rows)
     fetches = [
-        in_parts(queries, queries_in, sems.at[0], 2),
-        in_parts(inside, inside_in, sems.at[1], 4),
+        in_parts(queries_own, queries_in.at[0], sems.at[0], 2),
+        in_parts(inside_own, inside_in.at[0], sems.at[1], 2),
         in_parts(out_own, weights_in.at[0], sems.at[2], 2),
-        in_parts(out_other, weights_in.at[1], sems.at[3], 2),
-        in_parts(series.at[pl.ds(first_row, own_rows)], rows_in, sems.at[4], 2),
+        in_parts(queries_other, queries_in.at[1], sems.at[3], 2),
+        in_parts(inside_other, inside_in.at[1], sems.at[4], 2),
+        in_parts(out_other, weights_in.at[1], sems.at[5], 2),
+        in_parts(series.at[pl.ds(first_row, own_rows)], rows_in, sems.at[6], 2),
     ]
     for some in fetches:
         for fetch in some:
@@ -308,32 +312,31 @@
     unit = 1.0 / (position.astype(jnp.float32) * math.sqrt(HD))
     slot = lax.broadcasted_iota(jnp.int32, (send_out.shape[0], own_rows), 0)
     chosen = jnp.where(slot == slots[...], 1.0, 0.0).astype(jnp.bfloat16)
-    arrived(0)
-    carried = []
+    total = None
     for part, state in ((0, state_own), (1, state_other)):
-        for n in range(heads):
-            lanes = slice(part * half + n * HD, part * half + (n + 1) * HD)
-            start = state[n * HD : (n + 1) * HD, :]
-            carried.append(
-                jnp.dot(queries_in[:, lanes], start, preferred_element_type=jnp.float32)
+        arrived(3 * part)
+        carried = [
+            jnp.dot(
+                queries_in[part, :, n * HD : (n + 1) * HD],
+                state[n * HD : (n + 1) * HD, :],
+                preferred_element_type=jnp.float32,
             )
-    arrived(1)
-    mixed = [
-        ((inside_in[:, k * HD : (k + 1) * HD] + carried[k]) * unit).astype(jnp.bfloat16)
-        for k in range(2 * heads)
-    ]
-    arrived(2)
-    total = jnp.dot(
-        jnp.concatenate(mixed[:heads], axis=1), weights_in[0], preferred_element_type=jnp.float32
-    )
-    arrived(3)
-    total += jnp.dot(
-        jnp.concatenate(mixed[heads:], axis=1), weights_in[1], preferred_element_type=jnp.float32
-    )
-    arrived(4)
+            for n in range(heads)
+        ]
+        arrived(3 * part + 1)
+        mixed = [
+            ((inside_in[part, :, n * HD : (n + 1) * HD] + carried[n]) * unit).astype(jnp.bfloat16)
+            for n in range(heads)
+        ]
+        arrived(3 * part + 2)
+        added = jnp.dot(
+            jnp.concatenate(mixed, axis=1), weights_in[part], preferred_element_type=jnp.float32
+        )
+        total = added if total is None else total + added
+    arrived(6)
     total += rows_in[...].astype(jnp.float32)
     residual_held[...] = total
-    keep_residual = in_parts(residual_held, residual_out, sems.at[5], 4)
+    keep_residual = in_parts(residual_held, residual_out, sems.at[7], 4)
     for keep in keep_residual:
         keep.start()
     normed = normed_rows(total, gain[...]).astype(jnp.bfloat16)
@@ -341,19 +344,23 @@
     expert = lax.broadcasted_iota(jnp.int32, logits.shape, 1)
     logit = jnp.sum(jnp.where(expert == ids[...], logits, 0.0), axis=1, keepdims=True)
     gate_held[...] = jnp.broadcast_to(jax.nn.sigmoid(logit), gate_held.shape)
-    keep_gate = pltpu.make_async_copy(gate_held, gate_out, sems.at[6, 0])
+    middle = send_out.shape[0] // 2
+    send_out[:middle, :] = jnp.dot(
+        chosen[:middle], normed, preferred_element_type=jnp.float32
+    ).astype(jnp.bfloat16)
+    keep_gate = pltpu.make_async_copy(gate_held, gate_out, sems.at[8, 0])
     keep_gate.start()
-    send_out[...] = jnp.dot(chosen, normed, preferred_element_type=jnp.float32).astype(
-        jnp.bfloat16
-    )
+    send_out[middle:, :] = jnp.dot(
+        chosen[middle:], normed, preferred_element_type=jnp.float32
+    ).astype(jnp.bfloat16)
     for keep in keep_residual:
         keep.wait()
     keep_gate.wait()
 
 
 def mix_heads(
-    queries,
-    inside,
+    part_own,
+    part_other,
     state_own,
     state_other,
     out_own,
@@ -363,15 +370,17 @@
     slots,
     ids,
     router,
+    slot_column,
     slot_count,
 ):
-    own_rows, width = queries.shape
+    own_rows = slots.shape[1]
+    width = series.shape[1]
     half = out_own.shape[0]
     anywhere = pl.BlockSpec(memory_space=pl.ANY)
     local = pl.BlockSpec(memory_space=pltpu.VMEM)
     return pl.pallas_call(
         mix_kernel,
-        in_specs=[anywhere] * 2 + [local] * 2 + [anywhere] * 3 + [local] * 4,
+        in_specs=[anywhere] * 4 + [local] * 2 + [anywhere] * 3 + [local] * 4 + [anywhere],
         out_specs=[anywhere, anywhere, local],
         out_shape=[
             pltpu.HBM((own_rows, width), jnp.float32),
@@ -379,13 +388,13 @@
             jax.ShapeDtypeStruct((slot_count, width), jnp.bfloat16),
         ],
         scratch_shapes=[
-            pltpu.VMEM((own_rows, width), jnp.bfloat16),
-            pltpu.VMEM((own_rows, width), jnp.float32),
+            pltpu.VMEM((2, own_rows, half), jnp.bfloat16),
+            pltpu.VMEM((2, own_rows, half), jnp.float32),
             pltpu.VMEM((2, half, width), jnp.bfloat16),
             pltpu.VMEM((own_rows, width), jnp.bfloat16),
             pltpu.VMEM((own_rows, width), jnp.float32),
             pltpu.VMEM((own_rows, HD), jnp.float32),
-            pltpu.SemaphoreType.DMA((7, 4)),
+            pltpu.SemaphoreType.DMA((9, 4)),
         ],
         compiler_params=pltpu.CompilerParams(vmem_limit_bytes=24 * MIB),
         cost_estimate=pl.CostEstimate(
@@ -395,8 +404,7 @@
         ),
         name="mix_heads",
     )(
-        in_hbm(queries),
-        in_hbm(inside),
+        *(in_hbm(array) for array in (*part_own, *part_other)),
         state_own,
         state_other,
         in_hbm(out_own),
@@ -406,29 +414,30 @@
         slots,
         ids,
         router,
+        slot_column,
     )
 
 
 def combine_kernel(returned, residual, gate, slots, out, residual_in, gate_in, held, sems):
     own_rows, width = residual_in.shape
-    fetches = in_parts(residual, residual_in, sems.at[0], 4)
+    parts = 4
+    fetches = in_parts(residual, residual_in, sems.at[0], parts)
     fetch_gate = pltpu.make_async_copy(gate, gate_in, sems.at[1, 0])
+    fetch_gate.start()
     for fetch in fetches:
         fetch.start()
-    fetch_gate.start()
-    slot = lax.broadcasted_iota(jnp.int32, (returned.shape[0], own_rows), 0)
+    leave = in_parts(held, out, sems.at[2], parts)
+    slot = lax.broadcasted_iota(jnp.int32, (own_rows, returned.shape[0]), 1)
     chosen = jnp.where(slot == slots[...], 1.0, 0.0).astype(jnp.bfloat16)
-    routed = lax.dot_general(
-        chosen, returned[...], (((0,), (0,)), ((), ())), preferred_element_type=jnp.float32
-    )
+    routed = jnp.dot(chosen, returned[...], preferred_element_type=jnp.float32)
     fetch_gate.wait()
-    for fetch in fetches:
-        fetch.wait()
-    weight = jnp.concatenate([gate_in[...]] * (width // HD), axis=1)
-    held[...] = (residual_in[...] + weight * routed).astype(jnp.bfloat16)
-    leave = in_parts(held, out, sems.at[2], 4)
-    for copy in leave:
-        copy.start()
+    size = own_rows // parts
+    for k in range(parts):
+        at = slice(k * size, (k + 1) * size)
+        weight = jnp.concatenate([gate_in[at, :]] * (width // HD), axis=1)
+        fetches[k].wait()
+        held[at, :] = (residual_in[at, :] + weight * routed[at]).astype(jnp.bfloat16)
+        leave[k].start()
     for copy in leave:
         copy.wait()
 
@@ -476,16 +485,17 @@
     own_rows = series.shape[1] // head_count
 
     qkv_own = jnp.moveaxis(qkv_weight, 1, 0)
+    own_expert = (gate_weight[0], up_weight[0], down_weight[0])
     qkv_other = from_partner(qkv_own)
     out_other = from_partner(out_weight)
-    own_expert = (gate_weight[0], up_weight[0], down_weight[0])
     other_expert = tuple(from_partner(w) for w in own_expert)
 
     state = block_state(series[0], qkv_own, norm_attn)
     pieces = exchange(state.reshape(seq_size, state.shape[0] // seq_size, HD), SEQ)
     state_own = exchange(prefix(pieces), SEQ)
     state_other = from_partner(state_own)
-    queries, inside = inside_block(series[0], norm_attn, qkv_own, qkv_other, own_rows)
+    part_own = inside_block(series[0], norm_attn, qkv_own, own_rows)
+    part_other = inside_block(series[0], norm_attn, qkv_other, own_rows)
 
     route_ids = expert_ids[0, :, 0]
     expert_count = router_weight.shape[1]
@@ -496,9 +506,10 @@
     slot_index = route_ids * capacity + slot_rank
 
     slots = slot_index[None, :]
+    slot_column = slot_index[:, None]
     residual, gate, send_buffer = mix_heads(
-        queries,
-        inside,
+        part_own,
+        part_other,
         state_own.reshape(state.shape),
         state_other.reshape(state.shape),
         out_weight,
@@ -508,13 +519,14 @@
         slots,
         route_ids[:, None],
         router_weight,
+        slot_column,
         expert_count * capacity,
     )
     received = exchange(send_buffer.reshape(expert_count, capacity, width), SEQ_DP)
 
     expert_out = expert_of(received.reshape(-1, width), own_expert, other_expert)
     returned = exchange(expert_out.reshape(received.shape), SEQ_DP)
-    layer_out = combine(returned.reshape(send_buffer.shape), residual, gate, slots)
+    layer_out = combine(returned.reshape(send_buffer.shape), residual, gate, slot_column)
     return layer_out[None]
 
 

time: 131 us -> 134 us (1.023)
  Pallas kernels: 27.5 us -> 31.1 us
    pallas_call x1 -> x2, Pallas kernels: 6.01 us -> 9.56 us  [inside_block(): pl.pallas_call(inside_kernel, in_specs=[pl.BlockSpec(memory_space=pltpu.V...]
  transfers between devices with their start and end apart: 8 -> 8, of which waited for: 2 -> 2; matrix products, arithmetic and copies ran while one was open for 1% -> 1% of each run, Pallas kernels for 11% -> 13%
where the time goes in v5:
time: 134 us
  blocking collectives  64.7 us (48%)
  Pallas kernels  31.1 us (23%)
  waiting for transfers between devices  18.2 us (14%)
  starting transfers between devices  17.1 us (13%)
  local copies, waits for them, and re-layouts  1.88 us (1%)
    all_to_all x2, blocking collectives, exchange(): return lax.all_to_all(pieces, axes, split_axis=0, concat_axis=0, tiled=True)  64.7 us
    all_to_all x2, waiting for transfers between devices, exchange(): return lax.all_to_all(pieces, axes, split_axis=0, concat_axis=0, tiled=True)  18.2 us
    all_to_all x2, starting transfers between devices, exchange(): return lax.all_to_all(pieces, axes, split_axis=0, concat_axis=0, tiled=True)  15.9 us
    pallas_call x1, Pallas kernels, expert_of(): pl.pallas_call(expert_kernel, in_specs=[local] + [pl.BlockSpec(memory_spa...  10.9 us
    pallas_call x2, Pallas kernels, inside_block(): pl.pallas_call(inside_kernel, in_specs=[pl.BlockSpec(memory_space=pltpu.V...  9.56 us
    pallas_call x1, Pallas kernels, mix_heads(): pl.pallas_call(mix_kernel, in_specs=[anywhere] * 4 + [local] * 2 + [anywh...  3.94 us
    pallas_call x1, Pallas kernels, block_state(): pl.pallas_call(state_kernel, in_specs=[pl.BlockSpec(memory_space=pl.ANY),...  3.78 us
  transfers between devices with their start and end apart: 8, of which 2 were waited for; matrix products, arithmetic and copies ran while one was open for 1% of the time, Pallas kernels for 13%

profile of v5, /device:TPU:32, one launch (start us, length us, event | category | flops | bytes accessed | tf_op | source)
XLA Modules:
  0.0 133.6 jit_solution(15493132509044532064)
XLA Ops:
  0.0 0.0 copy-start.1
  0.0 0.0 copy-start.3
  0.0 0.0 copy-start.5
  0.0 0.1 collective-permute-start
  0.1 3.8 %block_state.1 = bf16[512,128]{1,0:T(8,128)(2,1)} custom-call(bf16[512,768]{1,0:T(8,128)(2,1)} %bitcast.17, bf16[3,768,384]{2,1,0:T(8,128)(2,1)} %bitcast.22, f32[768]{0:T(1024)} %gain.6), custom_call_target="tpu_custom_call" | custom-call | flops 603979776 | bytes 1572864 | tf_op jit(solution)/shard_map/block_state/pallas_call | solution.py:159
  3.9 11.4 %all-to-all-start = ((bf16[32,16,128]{2,1,0:T(8,128)(2,1)}), bf16[32,16,128]{2,1,0:T(8,128)(2,1)S(1)}, u32[]{:S(2)}, u32[]{:S(2)}) async-start(bf16[32,16,128]{2,1,0:T(8,128)(2,1)} %bitcast.2), calls=%async_computation | async-start | bytes 262144 | tf_op jit(solution)/shard_map/all_to_all | solution.py:26
  15.3 0.0 copy-done.3
  15.3 0.1 collective-permute-start.2
  15.4 0.5 collective-permute-start.3
  15.9 0.1 collective-permute-start.4
  16.0 0.4 collective-permute-start.5
  16.4 0.0 copy-done.5
  16.4 0.2 convert_reduce_fusion
  16.6 8.9 %all-to-all-done.pieces = bf16[32,16,128]{2,1,0:T(8,128)(2,1)S(1)} async-done(((bf16[32,16,128]{2,1,0:T(8,128)(2,1)}), bf16[32,16,128]{2,1,0:T(8,128)(2,1)S(1)}, u32[]{:S(2)}, u32[]{:S(2)}) %all-to-all-start) | async-done | bytes 131104 | tf_op jit(solution)/shard_map/all_to_all | solution.py:26
  25.5 0.7 prefix.1
  26.2 4.6 %all-to-all-start.1 = ((bf16[32,16,128]{2,1,0:T(8,128)(2,1)}), bf16[32,16,128]{2,1,0:T(8,128)(2,1)S(1)}, u32[]{:S(2)}, u32[]{:S(2)}) async-start(bf16[32,16,128]{2,1,0:T(8,128)(2,1)} %prefix.1), calls=%async_computation.1 | async-start | bytes 262144 | tf_op jit(solution)/shard_map/all_to_all | solution.py:26
  30.7 0.1 copy.20.ids
  30.9 0.1 copy.19
  31.1 9.3 %all-to-all-done.1 = bf16[32,16,128]{2,1,0:T(8,128)(2,1)S(1)} async-done(((bf16[32,16,128]{2,1,0:T(8,128)(2,1)}), bf16[32,16,128]{2,1,0:T(8,128)(2,1)S(1)}, u32[]{:S(2)}, u32[]{:S(2)}) %all-to-all-start.1) | async-done | bytes 131104 | tf_op jit(solution)/shard_map/all_to_all | solution.py:26
  40.4 0.0 collective-permute-done.weight
  40.4 0.0 copy-start.6
  40.4 0.0 collective-permute-start.1
  40.4 0.0 copy-done.1
  40.4 5.1 %inside_block.2 = (bf16[256,384]{1,0:T(8,128)(2,1)}, f32[256,384]{1,0:T(8,128)}) custom-call(bf16[512,768]{1,0:T(8,128)(2,1)} %bitcast.18, f32[768]{0:T(1024)S(1)} %copy-done.1, bf16[3,768,384]{2,1,0:T(8,128)(2,1)} %bitcast.23), custom_call_target="tpu_custom_call" | custom-call | flops 956301312 | bytes 1572864 | tf_op jit(solution)/shard_map/inside_block/pallas_call | solution.py:240
  45.5 0.0 copy-done.6
  45.5 0.0 copy-start
  45.5 0.0 copy-start.2
  45.5 4.5 %inside_block.3 = (bf16[256,384]{1,0:T(8,128)(2,1)}, f32[256,384]{1,0:T(8,128)}) custom-call(bf16[512,768]{1,0:T(8,128)(2,1)} %bitcast.19, f32[768]{0:T(1024)S(1)} %copy-done.1, bf16[3,768,384]{2,1,0:T(8,128)(2,1)} %copy-done.6), custom_call_target="tpu_custom_call" | custom-call | flops 956301312 | bytes 1572864 | tf_op jit(solution)/shard_map/inside_block/pallas_call | solution.py:240
  50.0 0.0 collective-permute-done.2.out_other
  50.0 0.0 copy-start.4
  50.0 0.0 collective-permute-done.1
  50.0 0.9 copy-done.4
  50.9 0.0 copy-done
  50.9 0.0 copy-done.2
  50.9 3.9 %mix_heads.1 = (f32[256,768]{1,0:T(8,128)}, f32[256,128]{1,0:T(8,128)}, bf16[512,768]{1,0:T(8,128)(2,1)S(1)}) custom-call(bf16[256,384]{1,0:T(8,128)(2,1)} %get-tuple-element.12.queries_own, f32[256,384]{1,0:T(8,128)} %get-tuple-element.13.inside_own, bf16[256,384]{1,0:T(8,128)(2,1)} %get-tuple-element.14.queries_other, ...), custom_call_target="tpu_custom_call" | custom-call | flops 603979776 | bytes 2359296 | tf_op jit(solution)/shard_map/mix_heads/pallas_call | solution.py:381
  54.8 0.2 reshape.62
  55.0 33.8 %all_to_all.20 = bf16[128,4,768]{2,1,0:T(4,128)(2,1)S(1)} all-to-all(bf16[128,4,768]{2,1,0:T(4,128)(2,1)S(1)} %reshape.62), channel_id=1, replica_groups=mesh['seq_0'=8,'seq_1'=4,'head'=2,'dp'=4] {'seq_0','seq_1','dp'}, dimensions={0} | all-to-all | bytes 1572864 | tf_op jit(solution)/shard_map/all_to_all | solution.py:26
  88.8 0.2 reshape.63.rows
  89.0 0.0 collective-permute-done.3.gate_b
  89.0 0.0 collective-permute-done.4.up_b
  89.0 0.0 collective-permute-done.5.down_b
  89.0 10.9 %expert_mlp.1 = bf16[512,768]{1,0:T(8,128)(2,1)S(1)} custom-call(bf16[512,768]{1,0:T(8,128)(2,1)S(1)} %reshape.63.rows, bf16[768,1536]{1,0:T(8,128)(2,1)} %bitcast.29, bf16[768,1536]{1,0:T(8,128)(2,1)} %bitcast.31, bf16[1536,768]{1,0:T(8,128)(2,1)} %bitcast.33, bf16[768,1536]{1,0:T(8,128)(2,1)} %collective-permute-done.3.gate_b, ...), custom_call_target="tpu_custom_call" | custom-call | flops 7247757312 | bytes 14155776 | tf_op jit(solution)/shard_map/expert_mlp/pallas_call | solution.py:81
  99.9 0.2 reshape.64
  100.1 30.9 %all_to_all.21 = bf16[128,4,768]{2,1,0:T(4,128)(2,1)S(1)} all-to-all(bf16[128,4,768]{2,1,0:T(4,128)(2,1)S(1)} %reshape.64), channel_id=1, replica_groups=mesh['seq_0'=8,'seq_1'=4,'head'=2,'dp'=4] {'seq_0','seq_1','dp'}, dimensions={0} | all-to-all | bytes 1572864 | tf_op jit(solution)/shard_map/all_to_all | solution.py:26
  131.0 0.2 reshape.65.returned
  131.2 2.2 %combine.1 = bf16[256,768]{1,0:T(8,128)(2,1)} custom-call(bf16[512,768]{1,0:T(8,128)(2,1)S(1)} %reshape.65.returned, f32[256,768]{1,0:T(8,128)} %get-tuple-element.17.residual, f32[256,128]{1,0:T(8,128)} %get-tuple-element.18.gate, s32[256,1]{1,0:T(8,128)S(1)} %multiply_add_fusion.slot_column.slots), custom_call_target="tpu_custom_call" | custom-call | flops 201326592 | bytes 1966080 | tf_op jit(solution)/shard_map/combine/pallas_call | solution.py:449
  (2 shorter events, 0.0 us)
Async XLA Ops:
  0.0 40.4 %copy-start.1 = (f32[768]{0:T(1024)S(1)}, f32[768]{0:T(1024)}, u32[]{:S(2)}) copy-start(f32[768]{0:T(1024)} %gain.6) | copy-start | bytes 9220
  0.0 15.3 %copy-start.3 = (bf16[384,768]{1,0:T(8,128)(2,1)S(1)}, bf16[384,768]{1,0:T(8,128)(2,1)}, u32[]{:S(2)}) copy-start(bf16[384,768]{1,0:T(8,128)(2,1)} %out_own.1) | copy-start | bytes 1769476
  0.0 16.4 %copy-start.5 = (s32[1,256,1]{1,2,0:T(1,128)S(1)}, s32[1,256,1]{1,2,0:T(1,128)}, u32[]{:S(2)}) copy-start(s32[1,256,1]{1,2,0:T(1,128)} %param.16) | copy-start | bytes 3076
  0.0 40.4 %collective-permute-start = (bf16[3,768,384]{2,1,0:T(8,128)(2,1)}, bf16[3,768,384]{2,1,0:T(8,128)(2,1)S(1)}, u32[]{:S(2)}, u32[]{:S(2)}) collective-permute-start(bf16[3,768,384]{2,1,0:T(8,128)(2,1)} %bitcast.21), channel_id=1, source_target_pairs={{0,4},{4,0},{1,5},{5,1},{2,6},{6,2},{3,7},{7,3},{8,12},{12,8},{9,1... | collective-permute-start | bytes 5308424 | tf_op jit(solution)/shard_map/ppermute | solution.py:22
  3.9 21.6 %all-to-all-start = ((bf16[32,16,128]{2,1,0:T(8,128)(2,1)}), bf16[32,16,128]{2,1,0:T(8,128)(2,1)S(1)}, u32[]{:S(2)}, u32[]{:S(2)}) async-start(bf16[32,16,128]{2,1,0:T(8,128)(2,1)} %bitcast.2), calls=%async_computation | async-start | bytes 262144 | tf_op jit(solution)/shard_map/all_to_all | solution.py:26
  15.3 34.7 %collective-permute-start.2 = (bf16[384,768]{1,0:T(8,128)(2,1)S(1)}, bf16[384,768]{1,0:T(8,128)(2,1)S(1)}, u32[]{:S(2)}, u32[]{:S(2)}) collective-permute-start(bf16[384,768]{1,0:T(8,128)(2,1)S(1)} %copy-done.3), channel_id=1, source_target_pairs={{0,4},{4,0},{1,5},{5,1},{2,6},{6,2},{3,7},{7,3},{8,12},{12,8},{9,1... | collective-permute-start | bytes 1769480 | tf_op jit(solution)/shard_map/ppermute | solution.py:22
  15.4 73.6 %collective-permute-start.3 = (bf16[768,1536]{1,0:T(8,128)(2,1)}, bf16[768,1536]{1,0:T(8,128)(2,1)}, u32[]{:S(2)}, u32[]{:S(2)}) collective-permute-start(bf16[768,1536]{1,0:T(8,128)(2,1)} %bitcast.28), channel_id=1, source_target_pairs={{0,4},{4,0},{1,5},{5,1},{2,6},{6,2},{3,7},{7,3},{8,12},{12,8},{9,1... | collective-permute-start | bytes 7077896 | tf_op jit(solution)/shard_map/ppermute | solution.py:22
  15.9 73.1 %collective-permute-start.4 = (bf16[768,1536]{1,0:T(8,128)(2,1)}, bf16[768,1536]{1,0:T(8,128)(2,1)}, u32[]{:S(2)}, u32[]{:S(2)}) collective-permute-start(bf16[768,1536]{1,0:T(8,128)(2,1)} %bitcast.30), channel_id=1, source_target_pairs={{0,4},{4,0},{1,5},{5,1},{2,6},{6,2},{3,7},{7,3},{8,12},{12,8},{9,1... | collective-permute-start | bytes 7077896 | tf_op jit(solution)/shard_map/ppermute | solution.py:22
  16.0 73.0 %collective-permute-start.5 = (bf16[1536,768]{1,0:T(8,128)(2,1)}, bf16[1536,768]{1,0:T(8,128)(2,1)}, u32[]{:S(2)}, u32[]{:S(2)}) collective-permute-start(bf16[1536,768]{1,0:T(8,128)(2,1)} %bitcast.32), channel_id=1, source_target_pairs={{0,4},{4,0},{1,5},{5,1},{2,6},{6,2},{3,7},{7,3},{8,12},{12,8},{9,1... | collective-permute-start | bytes 7077896 | tf_op jit(solution)/shard_map/ppermute | solution.py:22
  26.2 14.2 %all-to-all-start.1 = ((bf16[32,16,128]{2,1,0:T(8,128)(2,1)}), bf16[32,16,128]{2,1,0:T(8,128)(2,1)S(1)}, u32[]{:S(2)}, u32[]{:S(2)}) async-start(bf16[32,16,128]{2,1,0:T(8,128)(2,1)} %prefix.1), calls=%async_computation.1 | async-start | bytes 262144 | tf_op jit(solution)/shard_map/all_to_all | solution.py:26
  40.4 5.1 %copy-start.6 = (bf16[3,768,384]{2,1,0:T(8,128)(2,1)}, bf16[3,768,384]{2,1,0:T(8,128)(2,1)S(1)}, u32[]{:S(2)}) copy-start(bf16[3,768,384]{2,1,0:T(8,128)(2,1)S(1)} %collective-permute-done.weight) | copy-start | bytes 5308420
  40.4 9.6 %collective-permute-start.1 = (bf16[32,16,128]{2,1,0:T(8,128)(2,1)S(1)}, bf16[32,16,128]{2,1,0:T(8,128)(2,1)S(1)}, u32[]{:S(2)}, u32[]{:S(2)}) collective-permute-start(bf16[32,16,128]{2,1,0:T(8,128)(2,1)S(1)} %all-to-all-done.1), channel_id=1, source_target_pairs={{0,4},{4,0},{1,5},{5,1},{2,6},{6,2},{3,7},{7,3},{8,12},{12,8},{9,1... | collective-permute-start | bytes 393224 | tf_op jit(solution)/shard_map/ppermute | solution.py:22
  45.5 5.4 %copy-start = (bf16[768,128]{1,0:T(8,128)(2,1)S(1)}, bf16[768,128]{1,0:T(8,128)(2,1)}, u32[]{:S(2)}) copy-start(bf16[768,128]{1,0:T(8,128)(2,1)} %router.1) | copy-start | bytes 589828
  45.5 5.4 %copy-start.2 = (f32[768]{0:T(1024)S(1)}, f32[768]{0:T(1024)}, u32[]{:S(2)}) copy-start(f32[768]{0:T(1024)} %gain.7) | copy-start | bytes 9220
  50.0 0.9 copy-start.4

commit v6 on v5

--- a/solution.py
+++ b/solution.py
@@ -114,13 +114,19 @@
     return pltpu.with_memory_space_constraint(array, pltpu.HBM)
 
 
+def in_vmem(array):
+    return pltpu.with_memory_space_constraint(array, pltpu.VMEM)
+
+
 def normed_rows(rows, gain):
     x = rows.astype(jnp.float32)
     mean = jnp.sum(x * x, axis=-1, keepdims=True) * (1.0 / x.shape[1])
     return x * lax.rsqrt(mean + NORM_EPS) * gain.reshape(1, -1)
 
 
-def state_kernel(series, weight, gain, state_out, rows, table, gain_in, sems):
+def state_kernel(
+    series, weight, gain, state_out, normed_out, rows, table, gain_in, sems
+):
     half = table.shape[2]
     fetches = [
         in_parts(series, rows, sems.at[0], 4),
@@ -138,6 +144,7 @@
         fetch.wait()
     fetch_gain.wait()
     normed = normed_rows(rows[...], gain_in[...]).astype(jnp.bfloat16)
+    normed_out[...] = normed
     for fetch in fetches[1]:
         fetch.wait()
     keys = jnp.dot(normed, table[0], preferred_element_type=jnp.float32).astype(jnp.bfloat16)
@@ -163,8 +170,11 @@
             pl.BlockSpec(memory_space=pl.ANY),
             pl.BlockSpec(memory_space=pl.ANY),
         ],
-        out_specs=pl.BlockSpec(memory_space=pltpu.VMEM),
-        out_shape=jax.ShapeDtypeStruct((half + HD, HD), jnp.bfloat16),
+        out_specs=[pl.BlockSpec(memory_space=pltpu.VMEM)] * 2,
+        out_shape=[
+            jax.ShapeDtypeStruct((half + HD, HD), jnp.bfloat16),
+            pltpu.VMEM((count, width), jnp.bfloat16),
+        ],
         scratch_shapes=[
             pltpu.VMEM((count, width), jnp.bfloat16),
             pltpu.VMEM((2, width, half), jnp.bfloat16),
@@ -202,22 +212,26 @@
     )(pieces)
 
 
-def inside_kernel(series, gain, weight, queries_out, inside_out, queries_held, inside_held, sems):
-    count, _ = series.shape
-    own_rows, half = queries_held.shape
+def inside_kernel(normed, weight, queries_out, inside_out, table, sems):
+    count, _ = normed.shape
+    own_rows, half = queries_out.shape
     heads = half // HD
+    fetches = [in_parts(weight.at[k], table.at[k], sems.at[k], 2) for k in range(3)]
+    for k in (1, 2, 0):
+        for fetch in fetches[k]:
+            fetch.start()
     first_row = pl.multiple_of(lax.axis_index("head") * own_rows, own_rows)
-    mine = normed_rows(series[pl.ds(first_row, own_rows), :], gain[...]).astype(jnp.bfloat16)
-    normed = normed_rows(series[...], gain[...]).astype(jnp.bfloat16)
     row = lax.broadcasted_iota(jnp.int32, (own_rows, count), 0) + first_row
     causal = row >= lax.broadcasted_iota(jnp.int32, (own_rows, count), 1)
-    queries, keys, values = (
-        jnp.dot(rows, weight[k], preferred_element_type=jnp.float32).astype(jnp.bfloat16)
-        for k, rows in ((0, mine), (1, normed), (2, normed))
-    )
-    queries_held[...] = queries
-    keep_queries = pltpu.make_async_copy(queries_held, queries_out, sems.at[0])
-    keep_queries.start()
+
+    def project(source, k):
+        for fetch in fetches[k]:
+            fetch.wait()
+        return jnp.dot(source, table[k], preferred_element_type=jnp.float32).astype(jnp.bfloat16)
+
+    keys, values = project(normed[...], 1), project(normed[...], 2)
+    queries = project(normed[pl.ds(first_row, own_rows), :], 0)
+    queries_out[...] = queries
     for n in range(heads):
         at = slice(n * HD, (n + 1) * HD)
         scores = lax.dot_general(
@@ -227,28 +241,24 @@
             preferred_element_type=jnp.float32,
         )
         scores = jnp.where(causal, scores, 0.0).astype(jnp.bfloat16)
-        inside_held[:, at] = jnp.dot(scores, values[:, at], preferred_element_type=jnp.float32)
-    keep_inside = pltpu.make_async_copy(inside_held, inside_out, sems.at[1])
-    keep_inside.start()
-    keep_queries.wait()
-    keep_inside.wait()
-
-
-def inside_block(series, gain, weight, own_rows):
-    count, width = series.shape
+        inside_out[:, at] = jnp.dot(scores, values[:, at], preferred_element_type=jnp.float32)
+
+
+def inside_block(normed, weight, own_rows):
+    count, width = normed.shape
     half = weight.shape[2]
+    local = pl.BlockSpec(memory_space=pltpu.VMEM)
     return pl.pallas_call(
         inside_kernel,
-        in_specs=[pl.BlockSpec(memory_space=pltpu.VMEM)] * 3,
-        out_specs=[pl.BlockSpec(memory_space=pl.ANY)] * 2,
+        in_specs=[local, pl.BlockSpec(memory_space=pl.ANY)],
+        out_specs=[local] * 2,
         out_shape=[
-            pltpu.HBM((own_rows, half), jnp.bfloat16),
-            pltpu.HBM((own_rows, half), jnp.float32),
-        ],
-        scratch_shapes=[
             pltpu.VMEM((own_rows, half), jnp.bfloat16),
             pltpu.VMEM((own_rows, half), jnp.float32),
-            pltpu.SemaphoreType.DMA((2,)),
+        ],
+        scratch_shapes=[
+            pltpu.VMEM((3, width, half), jnp.bfloat16),
+            pltpu.SemaphoreType.DMA((3, 2)),
         ],
         compiler_params=pltpu.CompilerParams(vmem_limit_bytes=24 * MIB),
         cost_estimate=pl.CostEstimate(
@@ -257,7 +267,7 @@
             transcendentals=0,
         ),
         name="inside_block",
-    )(in_hbm(series), gain, in_hbm(weight))
+    )(in_vmem(normed), in_hbm(weight))
 
 
 def mix_kernel(
@@ -276,28 +286,21 @@
     router,
     slot_column,
     residual_out,
-    gate_out,
     send_out,
-    queries_in,
-    inside_in,
     weights_in,
     rows_in,
-    residual_held,
-    gate_held,
+    router_in,
     sems,
 ):
-    own_rows, _ = rows_in.shape
+    own_rows, width = rows_in.shape
     half = out_own.shape[0]
     heads = half // HD
     first_row = pl.multiple_of(lax.axis_index("head") * own_rows, own_rows)
     fetches = [
-        in_parts(queries_own, queries_in.at[0], sems.at[0], 2),
-        in_parts(inside_own, inside_in.at[0], sems.at[1], 2),
-        in_parts(out_own, weights_in.at[0], sems.at[2], 2),
-        in_parts(queries_other, queries_in.at[1], sems.at[3], 2),
-        in_parts(inside_other, inside_in.at[1], sems.at[4], 2),
-        in_parts(out_other, weights_in.at[1], sems.at[5], 2),
-        in_parts(series.at[pl.ds(first_row, own_rows)], rows_in, sems.at[6], 2),
+        in_parts(out_own, weights_in.at[0], sems.at[0], 2),
+        in_parts(out_other, weights_in.at[1], sems.at[1], 2),
+        in_parts(series.at[pl.ds(first_row, own_rows)], rows_in, sems.at[2], 2),
+        in_parts(router, router_in, sems.at[3], 1),
     ]
     for some in fetches:
         for fetch in some:
@@ -313,49 +316,32 @@
     slot = lax.broadcasted_iota(jnp.int32, (send_out.shape[0], own_rows), 0)
     chosen = jnp.where(slot == slots[...], 1.0, 0.0).astype(jnp.bfloat16)
     total = None
-    for part, state in ((0, state_own), (1, state_other)):
-        arrived(3 * part)
-        carried = [
-            jnp.dot(
-                queries_in[part, :, n * HD : (n + 1) * HD],
-                state[n * HD : (n + 1) * HD, :],
-                preferred_element_type=jnp.float32,
-            )
-            for n in range(heads)
-        ]
-        arrived(3 * part + 1)
-        mixed = [
-            ((inside_in[part, :, n * HD : (n + 1) * HD] + carried[n]) * unit).astype(jnp.bfloat16)
-            for n in range(heads)
-        ]
-        arrived(3 * part + 2)
+    for part, queries, inside, state in (
+        (0, queries_own, inside_own, state_own),
+        (1, queries_other, inside_other, state_other),
+    ):
+        mixed = []
+        for n in range(heads):
+            at = slice(n * HD, (n + 1) * HD)
+            carried = jnp.dot(queries[:, at], state[at, :], preferred_element_type=jnp.float32)
+            mixed.append(((inside[:, at] + carried) * unit).astype(jnp.bfloat16))
+        arrived(part)
         added = jnp.dot(
             jnp.concatenate(mixed, axis=1), weights_in[part], preferred_element_type=jnp.float32
         )
         total = added if total is None else total + added
-    arrived(6)
+    arrived(2)
     total += rows_in[...].astype(jnp.float32)
-    residual_held[...] = total
-    keep_residual = in_parts(residual_held, residual_out, sems.at[7], 4)
-    for keep in keep_residual:
-        keep.start()
+    residual_out[:, :width] = total
     normed = normed_rows(total, gain[...]).astype(jnp.bfloat16)
-    logits = jnp.dot(normed, router[...], preferred_element_type=jnp.float32)
+    send_out[...] = jnp.dot(chosen, normed, preferred_element_type=jnp.float32).astype(
+        jnp.bfloat16
+    )
+    arrived(3)
+    logits = jnp.dot(normed, router_in[...], preferred_element_type=jnp.float32)
     expert = lax.broadcasted_iota(jnp.int32, logits.shape, 1)
     logit = jnp.sum(jnp.where(expert == ids[...], logits, 0.0), axis=1, keepdims=True)
-    gate_held[...] = jnp.broadcast_to(jax.nn.sigmoid(logit), gate_held.shape)
-    middle = send_out.shape[0] // 2
-    send_out[:middle, :] = jnp.dot(
-        chosen[:middle], normed, preferred_element_type=jnp.float32
-    ).astype(jnp.bfloat16)
-    keep_gate = pltpu.make_async_copy(gate_held, gate_out, sems.at[8, 0])
-    keep_gate.start()
-    send_out[middle:, :] = jnp.dot(
-        chosen[middle:], normed, preferred_element_type=jnp.float32
-    ).astype(jnp.bfloat16)
-    for keep in keep_residual:
-        keep.wait()
-    keep_gate.wait()
+    residual_out[:, width:] = jnp.broadcast_to(jax.nn.sigmoid(logit), (own_rows, HD))
 
 
 def mix_heads(
@@ -380,21 +366,17 @@
     local = pl.BlockSpec(memory_space=pltpu.VMEM)
     return pl.pallas_call(
         mix_kernel,
-        in_specs=[anywhere] * 4 + [local] * 2 + [anywhere] * 3 + [local] * 4 + [anywhere],
-        out_specs=[anywhere, anywhere, local],
+        in_specs=[local] * 6 + [anywhere] * 3 + [local] * 3 + [anywhere] * 2,
+        out_specs=[local] * 2,
         out_shape=[
-            pltpu.HBM((own_rows, width), jnp.float32),
-            pltpu.HBM((own_rows, HD), jnp.float32),
+            pltpu.VMEM((own_rows, width + HD), jnp.float32),
             jax.ShapeDtypeStruct((slot_count, width), jnp.bfloat16),
         ],
         scratch_shapes=[
-            pltpu.VMEM((2, own_rows, half), jnp.bfloat16),
-            pltpu.VMEM((2, own_rows, half), jnp.float32),
             pltpu.VMEM((2, half, width), jnp.bfloat16),
             pltpu.VMEM((own_rows, width), jnp.bfloat16),
-            pltpu.VMEM((own_rows, width), jnp.float32),
-            pltpu.VMEM((own_rows, HD), jnp.float32),
-            pltpu.SemaphoreType.DMA((9, 4)),
+            pltpu.VMEM(router.shape, jnp.bfloat16),
+            pltpu.SemaphoreType.DMA((4, 2)),
         ],
         compiler_params=pltpu.CompilerParams(vmem_limit_bytes=24 * MIB),
         cost_estimate=pl.CostEstimate(
@@ -404,7 +386,7 @@
         ),
         name="mix_heads",
     )(
-        *(in_hbm(array) for array in (*part_own, *part_other)),
+        *(in_vmem(array) for array in (*part_own, *part_other)),
         state_own,
         state_other,
         in_hbm(out_own),
@@ -413,49 +395,40 @@
         gain,
         slots,
         ids,
-        router,
+        in_hbm(router),
         slot_column,
     )
 
 
-def combine_kernel(returned, residual, gate, slots, out, residual_in, gate_in, held, sems):
-    own_rows, width = residual_in.shape
+def combine_kernel(returned, residual, slots, out, held, sems):
+    own_rows, width = held.shape
     parts = 4
-    fetches = in_parts(residual, residual_in, sems.at[0], parts)
-    fetch_gate = pltpu.make_async_copy(gate, gate_in, sems.at[1, 0])
-    fetch_gate.start()
-    for fetch in fetches:
-        fetch.start()
-    leave = in_parts(held, out, sems.at[2], parts)
+    leave = in_parts(held, out, sems, parts)
     slot = lax.broadcasted_iota(jnp.int32, (own_rows, returned.shape[0]), 1)
     chosen = jnp.where(slot == slots[...], 1.0, 0.0).astype(jnp.bfloat16)
-    routed = jnp.dot(chosen, returned[...], preferred_element_type=jnp.float32)
-    fetch_gate.wait()
     size = own_rows // parts
     for k in range(parts):
         at = slice(k * size, (k + 1) * size)
-        weight = jnp.concatenate([gate_in[at, :]] * (width // HD), axis=1)
-        fetches[k].wait()
-        held[at, :] = (residual_in[at, :] + weight * routed[at]).astype(jnp.bfloat16)
+        routed = jnp.dot(chosen[at], returned[...], preferred_element_type=jnp.float32)
+        weight = jnp.concatenate([residual[at, width:]] * (width // HD), axis=1)
+        held[at, :] = (residual[at, :width] + weight * routed).astype(jnp.bfloat16)
         leave[k].start()
     for copy in leave:
         copy.wait()
 
 
-def combine(returned, residual, gate, slots):
-    own_rows, width = residual.shape
+def combine(returned, residual, slots):
+    own_rows, width = residual.shape[0], returned.shape[1]
     anywhere = pl.BlockSpec(memory_space=pl.ANY)
     local = pl.BlockSpec(memory_space=pltpu.VMEM)
     return pl.pallas_call(
         combine_kernel,
-        in_specs=[local, anywhere, anywhere, local],
+        in_specs=[local] * 3,
         out_specs=anywhere,
         out_shape=pltpu.HBM((own_rows, width), jnp.bfloat16),
         scratch_shapes=[
-            pltpu.VMEM((own_rows, width), jnp.float32),
-            pltpu.VMEM((own_rows, HD), jnp.float32),
             pltpu.VMEM((own_rows, width), jnp.bfloat16),
-            pltpu.SemaphoreType.DMA((3, 4)),
+            pltpu.SemaphoreType.DMA((4,)),
         ],
         compiler_params=pltpu.CompilerParams(vmem_limit_bytes=24 * MIB),
         cost_estimate=pl.CostEstimate(
@@ -464,7 +437,7 @@
             transcendentals=0,
         ),
         name="combine",
-    )(returned, in_hbm(residual), in_hbm(gate), slots)
+    )(returned, in_vmem(residual), slots)
 
 
 def on_device(
@@ -490,12 +463,12 @@
     out_other = from_partner(out_weight)
     other_expert = tuple(from_partner(w) for w in own_expert)
 
-    state = block_state(series[0], qkv_own, norm_attn)
+    state, normed_in = block_state(series[0], qkv_own, norm_attn)
     pieces = exchange(state.reshape(seq_size, state.shape[0] // seq_size, HD), SEQ)
     state_own = exchange(prefix(pieces), SEQ)
     state_other = from_partner(state_own)
-    part_own = inside_block(series[0], norm_attn, qkv_own, own_rows)
-    part_other = inside_block(series[0], norm_attn, qkv_other, own_rows)
+    part_own = inside_block(normed_in, qkv_own, own_rows)
+    part_other = inside_block(normed_in, qkv_other, own_rows)
 
     route_ids = expert_ids[0, :, 0]
     expert_count = router_weight.shape[1]
@@ -507,7 +480,7 @@
 
     slots = slot_index[None, :]
     slot_column = slot_index[:, None]
-    residual, gate, send_buffer = mix_heads(
+    residual, send_buffer = mix_heads(
         part_own,
         part_other,
         state_own.reshape(state.shape),
@@ -526,7 +499,7 @@
 
     expert_out = expert_of(received.reshape(-1, width), own_expert, other_expert)
     returned = exchange(expert_out.reshape(received.shape), SEQ_DP)
-    layer_out = combine(returned.reshape(send_buffer.shape), residual, gate, slot_column)
+    layer_out = combine(returned.reshape(send_buffer.shape), residual, slot_column)
     return layer_out[None]
 
 

time: 134 us -> 130 us (0.970)
  Pallas kernels: 31.1 us -> 26.7 us
    pallas_call x4, Pallas kernels: 15.7 us -> 11.3 us  [the longest x2 6.78 us: inside_block(): pl.pallas_call(inside_kernel, in_specs=[local, pl.BlockSpec(memory_space=...]
  transfers between devices with their start and end apart: 8 -> 8, of which waited for: 2 -> 2; matrix products, arithmetic and copies ran while one was open for 1% -> 1% of each run, Pallas kernels for 13% -> 11%
where the time goes in v6:
time: 130 us
  blocking collectives  65.5 us (50%)
  Pallas kernels  26.7 us (21%)
  waiting for transfers between devices  18.2 us (14%)
  starting transfers between devices  17 us (13%)
  local copies, waits for them, and re-layouts  1.79 us (1%)
    all_to_all x2, blocking collectives, exchange(): return lax.all_to_all(pieces, axes, split_axis=0, concat_axis=0, tiled=True)  65.5 us
    all_to_all x2, waiting for transfers between devices, exchange(): return lax.all_to_all(pieces, axes, split_axis=0, concat_axis=0, tiled=True)  18.2 us
    all_to_all x2, starting transfers between devices, exchange(): return lax.all_to_all(pieces, axes, split_axis=0, concat_axis=0, tiled=True)  15.9 us
    pallas_call x1, Pallas kernels, expert_of(): pl.pallas_call(expert_kernel, in_specs=[local] + [pl.BlockSpec(memory_spa...  10.9 us
    pallas_call x2, Pallas kernels, inside_block(): pl.pallas_call(inside_kernel, in_specs=[local, pl.BlockSpec(memory_space=...  6.78 us
    pallas_call x1, Pallas kernels, block_state(): pl.pallas_call(state_kernel, in_specs=[pl.BlockSpec(memory_space=pl.ANY),...  3.79 us
    pallas_call x1, Pallas kernels, mix_heads(): pl.pallas_call(mix_kernel, in_specs=[local] * 6 + [anywhere] * 3 + [local...  3.15 us
  transfers between devices with their start and end apart: 8, of which 2 were waited for; matrix products, arithmetic and copies ran while one was open for 1% of the time, Pallas kernels for 11%

profile of v6, /device:TPU:32, one launch (start us, length us, event | category | flops | bytes accessed | tf_op | source)
XLA Modules:
  0.0 129.8 jit_solution(2686931302126964130)
XLA Ops:
  0.0 0.0 copy-start.1
  0.0 0.0 copy-start.3
  0.0 0.0 collective-permute-start
  0.0 3.8 %block_state.1 = (bf16[512,128]{1,0:T(8,128)(2,1)}, bf16[512,768]{1,0:T(8,128)(2,1)S(1)}) custom-call(bf16[512,768]{1,0:T(8,128)(2,1)} %bitcast.17, bf16[3,768,384]{2,1,0:T(8,128)(2,1)} %bitcast.20, f32[768]{0:T(1024)} %gain.2), custom_call_target="tpu_custom_call" | custom-call | flops 603979776 | bytes 1572864 | tf_op jit(solution)/shard_map/block_state/pallas_call | solution.py:166
  3.8 11.4 %all-to-all-start = ((bf16[32,16,128]{2,1,0:T(8,128)(2,1)}), bf16[32,16,128]{2,1,0:T(8,128)(2,1)S(1)}, u32[]{:S(2)}, u32[]{:S(2)}) async-start(bf16[32,16,128]{2,1,0:T(8,128)(2,1)} %bitcast.2), calls=%async_computation | async-start | bytes 262144 | tf_op jit(solution)/shard_map/all_to_all | solution.py:26
  15.2 0.0 copy-done.1
  15.2 0.1 collective-permute-start.2
  15.3 0.5 collective-permute-start.3
  15.8 0.1 collective-permute-start.4
  15.9 0.4 collective-permute-start.5
  16.3 0.0 copy-done.3
  16.3 0.2 convert_reduce_fusion
  16.5 8.9 %all-to-all-done.pieces = bf16[32,16,128]{2,1,0:T(8,128)(2,1)S(1)} async-done(((bf16[32,16,128]{2,1,0:T(8,128)(2,1)}), bf16[32,16,128]{2,1,0:T(8,128)(2,1)S(1)}, u32[]{:S(2)}, u32[]{:S(2)}) %all-to-all-start) | async-done | bytes 131104 | tf_op jit(solution)/shard_map/all_to_all | solution.py:26
  25.4 0.7 prefix.1
  26.1 4.6 %all-to-all-start.1 = ((bf16[32,16,128]{2,1,0:T(8,128)(2,1)}), bf16[32,16,128]{2,1,0:T(8,128)(2,1)S(1)}, u32[]{:S(2)}, u32[]{:S(2)}) async-start(bf16[32,16,128]{2,1,0:T(8,128)(2,1)} %prefix.1), calls=%async_computation.1 | async-start | bytes 262144 | tf_op jit(solution)/shard_map/all_to_all | solution.py:26
  30.7 0.1 copy.20.ids
  30.8 0.1 copy.19
  31.0 9.3 %all-to-all-done.1 = bf16[32,16,128]{2,1,0:T(8,128)(2,1)S(1)} async-done(((bf16[32,16,128]{2,1,0:T(8,128)(2,1)}), bf16[32,16,128]{2,1,0:T(8,128)(2,1)S(1)}, u32[]{:S(2)}, u32[]{:S(2)}) %all-to-all-start.1) | async-done | bytes 131104 | tf_op jit(solution)/shard_map/all_to_all | solution.py:26
  40.3 0.0 collective-permute-done.weight
  40.3 0.0 collective-permute-start.1
  40.3 3.4 %inside_block.2 = (bf16[256,384]{1,0:T(8,128)(2,1)S(1)}, f32[256,384]{1,0:T(8,128)S(1)}) custom-call(bf16[512,768]{1,0:T(8,128)(2,1)S(1)} %get-tuple-element.13.normed, bf16[3,768,384]{2,1,0:T(8,128)(2,1)} %bitcast.21), custom_call_target="tpu_custom_call" | custom-call | flops 956301312 | bytes 1572864 | tf_op jit(solution)/shard_map/inside_block/pallas_call | solution.py:251
  43.7 0.0 copy-start
  43.7 3.4 %inside_block.3 = (bf16[256,384]{1,0:T(8,128)(2,1)S(1)}, f32[256,384]{1,0:T(8,128)S(1)}) custom-call(bf16[512,768]{1,0:T(8,128)(2,1)S(1)} %get-tuple-element.13.normed, bf16[3,768,384]{2,1,0:T(8,128)(2,1)} %collective-permute-done.weight), custom_call_target="tpu_custom_call" | custom-call | flops 956301312 | bytes 1572864 | tf_op jit(solution)/shard_map/inside_block/pallas_call | solution.py:251
  47.1 0.0 collective-permute-done.2.out_other
  47.1 0.0 copy-start.2
  47.1 0.0 collective-permute-done.1
  47.1 0.8 copy-done.2
  47.9 0.0 copy-done
  47.9 3.1 %mix_heads.1 = (f32[256,896]{1,0:T(8,128)S(1)}, bf16[512,768]{1,0:T(8,128)(2,1)S(1)}) custom-call(bf16[256,384]{1,0:T(8,128)(2,1)S(1)} %get-tuple-element.14.queries_own, f32[256,384]{1,0:T(8,128)S(1)} %get-tuple-element.15.inside_own, bf16[256,384]{1,0:T(8,128)(2,1)S(1)} %get-tuple-element.16.queries_other, f32[256,384]{1,0:T(8,128)S(1)} %get-tuple-element.17.inside_other, ...), custom_call_target="tpu_custom_call" | custom-call | flops 603979776 | bytes 2359296 | tf_op jit(solution)/shard_map/mix_heads/pallas_call | solution.py:367
  51.1 0.2 reshape.62
  51.3 34.4 %all_to_all.20 = bf16[128,4,768]{2,1,0:T(4,128)(2,1)S(1)} all-to-all(bf16[128,4,768]{2,1,0:T(4,128)(2,1)S(1)} %reshape.62), channel_id=1, replica_groups=mesh['seq_0'=8,'seq_1'=4,'head'=2,'dp'=4] {'seq_0','seq_1','dp'}, dimensions={0} | all-to-all | bytes 1572864 | tf_op jit(solution)/shard_map/all_to_all | solution.py:26
  85.7 0.2 reshape.63.rows
  85.9 0.0 collective-permute-done.3.gate_b
  85.9 0.0 collective-permute-done.4.up_b
  85.9 0.0 collective-permute-done.5.down_b
  85.9 10.9 %expert_mlp.1 = bf16[512,768]{1,0:T(8,128)(2,1)S(1)} custom-call(bf16[512,768]{1,0:T(8,128)(2,1)S(1)} %reshape.63.rows, bf16[768,1536]{1,0:T(8,128)(2,1)} %bitcast.27, bf16[768,1536]{1,0:T(8,128)(2,1)} %bitcast.29, bf16[1536,768]{1,0:T(8,128)(2,1)} %bitcast.31, bf16[768,1536]{1,0:T(8,128)(2,1)} %collective-permute-done.3.gate_b, ...), custom_call_target="tpu_custom_call" | custom-call | flops 7247757312 | bytes 14155776 | tf_op jit(solution)/shard_map/expert_mlp/pallas_call | solution.py:81
  96.9 0.2 reshape.64
  97.0 31.0 %all_to_all.21 = bf16[128,4,768]{2,1,0:T(4,128)(2,1)S(1)} all-to-all(bf16[128,4,768]{2,1,0:T(4,128)(2,1)S(1)} %reshape.64), channel_id=1, replica_groups=mesh['seq_0'=8,'seq_1'=4,'head'=2,'dp'=4] {'seq_0','seq_1','dp'}, dimensions={0} | all-to-all | bytes 1572864 | tf_op jit(solution)/shard_map/all_to_all | solution.py:26
  128.1 0.2 reshape.65.returned
  128.3 1.4 %combine.1 = bf16[256,768]{1,0:T(8,128)(2,1)} custom-call(bf16[512,768]{1,0:T(8,128)(2,1)S(1)} %reshape.65.returned, f32[256,896]{1,0:T(8,128)S(1)} %get-tuple-element.20.residual, s32[256,1]{1,0:T(8,128)S(1)} %multiply_add_fusion.slot_column.slots), custom_call_target="tpu_custom_call" | custom-call | flops 201326592 | bytes 1966080 | tf_op jit(solution)/shard_map/combine/pallas_call | solution.py:424
  (2 shorter events, 0.0 us)
Async XLA Ops:
  0.0 15.2 %copy-start.1 = (bf16[384,768]{1,0:T(8,128)(2,1)S(1)}, bf16[384,768]{1,0:T(8,128)(2,1)}, u32[]{:S(2)}) copy-start(bf16[384,768]{1,0:T(8,128)(2,1)} %out_own.1) | copy-start | bytes 1769476
  0.0 16.3 %copy-start.3 = (s32[1,256,1]{1,2,0:T(1,128)S(1)}, s32[1,256,1]{1,2,0:T(1,128)}, u32[]{:S(2)}) copy-start(s32[1,256,1]{1,2,0:T(1,128)} %param.16) | copy-start | bytes 3076
  0.0 40.3 %collective-permute-start = (bf16[3,768,384]{2,1,0:T(8,128)(2,1)}, bf16[3,768,384]{2,1,0:T(8,128)(2,1)}, u32[]{:S(2)}, u32[]{:S(2)}) collective-permute-start(bf16[3,768,384]{2,1,0:T(8,128)(2,1)} %bitcast.19), channel_id=1, source_target_pairs={{0,4},{4,0},{1,5},{5,1},{2,6},{6,2},{3,7},{7,3},{8,12},{12,8},{9,1... | collective-permute-start | bytes 5308424 | tf_op jit(solution)/shard_map/ppermute | solution.py:22
  3.8 21.6 %all-to-all-start = ((bf16[32,16,128]{2,1,0:T(8,128)(2,1)}), bf16[32,16,128]{2,1,0:T(8,128)(2,1)S(1)}, u32[]{:S(2)}, u32[]{:S(2)}) async-start(bf16[32,16,128]{2,1,0:T(8,128)(2,1)} %bitcast.2), calls=%async_computation | async-start | bytes 262144 | tf_op jit(solution)/shard_map/all_to_all | solution.py:26
  15.2 31.9 %collective-permute-start.2 = (bf16[384,768]{1,0:T(8,128)(2,1)S(1)}, bf16[384,768]{1,0:T(8,128)(2,1)S(1)}, u32[]{:S(2)}, u32[]{:S(2)}) collective-permute-start(bf16[384,768]{1,0:T(8,128)(2,1)S(1)} %copy-done.1), channel_id=1, source_target_pairs={{0,4},{4,0},{1,5},{5,1},{2,6},{6,2},{3,7},{7,3},{8,12},{12,8},{9,1... | collective-permute-start | bytes 1769480 | tf_op jit(solution)/shard_map/ppermute | solution.py:22
  15.3 70.6 %collective-permute-start.3 = (bf16[768,1536]{1,0:T(8,128)(2,1)}, bf16[768,1536]{1,0:T(8,128)(2,1)}, u32[]{:S(2)}, u32[]{:S(2)}) collective-permute-start(bf16[768,1536]{1,0:T(8,128)(2,1)} %bitcast.26), channel_id=1, source_target_pairs={{0,4},{4,0},{1,5},{5,1},{2,6},{6,2},{3,7},{7,3},{8,12},{12,8},{9,1... | collective-permute-start | bytes 7077896 | tf_op jit(solution)/shard_map/ppermute | solution.py:22
  15.8 70.1 %collective-permute-start.4 = (bf16[768,1536]{1,0:T(8,128)(2,1)}, bf16[768,1536]{1,0:T(8,128)(2,1)}, u32[]{:S(2)}, u32[]{:S(2)}) collective-permute-start(bf16[768,1536]{1,0:T(8,128)(2,1)} %bitcast.28), channel_id=1, source_target_pairs={{0,4},{4,0},{1,5},{5,1},{2,6},{6,2},{3,7},{7,3},{8,12},{12,8},{9,1... | collective-permute-start | bytes 7077896 | tf_op jit(solution)/shard_map/ppermute | solution.py:22
  15.9 70.0 %collective-permute-start.5 = (bf16[1536,768]{1,0:T(8,128)(2,1)}, bf16[1536,768]{1,0:T(8,128)(2,1)}, u32[]{:S(2)}, u32[]{:S(2)}) collective-permute-start(bf16[1536,768]{1,0:T(8,128)(2,1)} %bitcast.30), channel_id=1, source_target_pairs={{0,4},{4,0},{1,5},{5,1},{2,6},{6,2},{3,7},{7,3},{8,12},{12,8},{9,1... | collective-permute-start | bytes 7077896 | tf_op jit(solution)/shard_map/ppermute | solution.py:22
  26.1 14.2 %all-to-all-start.1 = ((bf16[32,16,128]{2,1,0:T(8,128)(2,1)}), bf16[32,16,128]{2,1,0:T(8,128)(2,1)S(1)}, u32[]{:S(2)}, u32[]{:S(2)}) async-start(bf16[32,16,128]{2,1,0:T(8,128)(2,1)} %prefix.1), calls=%async_computation.1 | async-start | bytes 262144 | tf_op jit(solution)/shard_map/all_to_all | solution.py:26
  40.3 6.8 %collective-permute-start.1 = (bf16[32,16,128]{2,1,0:T(8,128)(2,1)S(1)}, bf16[32,16,128]{2,1,0:T(8,128)(2,1)S(1)}, u32[]{:S(2)}, u32[]{:S(2)}) collective-permute-start(bf16[32,16,128]{2,1,0:T(8,128)(2,1)S(1)} %all-to-all-done.1), channel_id=1, source_target_pairs={{0,4},{4,0},{1,5},{5,1},{2,6},{6,2},{3,7},{7,3},{8,12},{12,8},{9,1... | collective-permute-start | bytes 393224 | tf_op jit(solution)/shard_map/ppermute | solution.py:22
  43.7 4.2 %copy-start = (f32[768]{0:T(1024)S(1)}, f32[768]{0:T(1024)}, u32[]{:S(2)}) copy-start(f32[768]{0:T(1024)} %gain.3) | copy-start | bytes 9220
  47.1 0.8 copy-start.2

commit v7 on v6

--- a/solution.py
+++ b/solution.py
@@ -140,11 +140,13 @@
     for some in fetches[1:]:
         for fetch in some:
             fetch.start()
-    for fetch in fetches[0]:
+    fetch_gain.wait()
+    size = rows.shape[0] // len(fetches[0])
+    for k, fetch in enumerate(fetches[0]):
+        at = slice(k * size, (k + 1) * size)
         fetch.wait()
-    fetch_gain.wait()
-    normed = normed_rows(rows[...], gain_in[...]).astype(jnp.bfloat16)
-    normed_out[...] = normed
+        normed_out[at, :] = normed_rows(rows[at, :], gain_in[...]).astype(jnp.bfloat16)
+    normed = normed_out[...]
     for fetch in fetches[1]:
         fetch.wait()
     keys = jnp.dot(normed, table[0], preferred_element_type=jnp.float32).astype(jnp.bfloat16)
@@ -270,16 +272,74 @@
     )(in_vmem(normed), in_hbm(weight))
 
 
+def heads_through(queries, inside, state, first, weight):
+    own_rows, half = queries.shape
+    position = lax.broadcasted_iota(jnp.int32, (own_rows, HD), 0) + first
+    unit = 1.0 / (position.astype(jnp.float32) * math.sqrt(HD))
+    mixed = []
+    for n in range(half // HD):
+        at = slice(n * HD, (n + 1) * HD)
+        carried = jnp.dot(queries[:, at], state[at, :], preferred_element_type=jnp.float32)
+        mixed.append(((inside[:, at] + carried) * unit).astype(jnp.bfloat16))
+    return lambda: jnp.dot(
+        jnp.concatenate(mixed, axis=1), weight[...], preferred_element_type=jnp.float32
+    )
+
+
+def first_position(own_rows):
+    places = lax.axis_index(SEQ) * lax.axis_size("head") + lax.axis_index("head")
+    return places * own_rows + 1
+
+
+def mix_own_kernel(queries, inside, state, out_weight, series, total, weight_in, rows_in, sems):
+    own_rows = queries.shape[0]
+    first_row = pl.multiple_of(lax.axis_index("head") * own_rows, own_rows)
+    fetches = [
+        in_parts(out_weight, weight_in, sems.at[0], 2),
+        in_parts(series.at[pl.ds(first_row, own_rows)], rows_in, sems.at[1], 2),
+    ]
+    for some in fetches:
+        for fetch in some:
+            fetch.start()
+    through = heads_through(queries, inside, state, first_position(own_rows), weight_in)
+    for some in fetches:
+        for fetch in some:
+            fetch.wait()
+    total[...] = through() + rows_in[...].astype(jnp.float32)
+
+
+def mix_own(part, state, out_weight, series):
+    queries, inside = part
+    own_rows, half = queries.shape
+    width = series.shape[1]
+    anywhere = pl.BlockSpec(memory_space=pl.ANY)
+    local = pl.BlockSpec(memory_space=pltpu.VMEM)
+    return pl.pallas_call(
+        mix_own_kernel,
+        in_specs=[local] * 3 + [anywhere] * 2,
+        out_specs=local,
+        out_shape=pltpu.VMEM((own_rows, width), jnp.float32),
+        scratch_shapes=[
+            pltpu.VMEM((half, width), jnp.bfloat16),
+            pltpu.VMEM((own_rows, width), jnp.bfloat16),
+            pltpu.SemaphoreType.DMA((2, 2)),
+        ],
+        compiler_params=pltpu.CompilerParams(vmem_limit_bytes=16 * MIB),
+        cost_estimate=pl.CostEstimate(
+            flops=2 * own_rows * half * (width + HD),
+            bytes_accessed=8 * own_rows * width,
+            transcendentals=0,
+        ),
+        name="mix_own",
+    )(in_vmem(queries), in_vmem(inside), state, in_hbm(out_weight), in_hbm(series))
+
+
 def mix_kernel(
-    queries_own,
-    inside_own,
-    queries_other,
-    inside_other,
-    state_own,
-    state_other,
-    out_own,
-    out_other,
-    series,
+    queries,
+    inside,
+    state,
+    begun,
+    out_weight,
     gain,
     slots,
     ids,
@@ -287,96 +347,50 @@
     slot_column,
     residual_out,
     send_out,
-    weights_in,
-    rows_in,
+    weight_in,
     router_in,
     sems,
 ):
-    own_rows, width = rows_in.shape
-    half = out_own.shape[0]
-    heads = half // HD
-    first_row = pl.multiple_of(lax.axis_index("head") * own_rows, own_rows)
-    fetches = [
-        in_parts(out_own, weights_in.at[0], sems.at[0], 2),
-        in_parts(out_other, weights_in.at[1], sems.at[1], 2),
-        in_parts(series.at[pl.ds(first_row, own_rows)], rows_in, sems.at[2], 2),
-        in_parts(router, router_in, sems.at[3], 1),
-    ]
-    for some in fetches:
-        for fetch in some:
-            fetch.start()
-
-    def arrived(k):
-        for fetch in fetches[k]:
-            fetch.wait()
-
-    base = lax.axis_index(SEQ) * series.shape[0] + first_row + 1
-    position = lax.broadcasted_iota(jnp.int32, (own_rows, HD), 0) + base
-    unit = 1.0 / (position.astype(jnp.float32) * math.sqrt(HD))
+    own_rows, width = begun.shape
+    fetches = in_parts(out_weight, weight_in, sems.at[0], 2)
+    fetch_router = pltpu.make_async_copy(router, router_in, sems.at[1, 0])
+    for fetch in fetches:
+        fetch.start()
+    fetch_router.start()
     slot = lax.broadcasted_iota(jnp.int32, (send_out.shape[0], own_rows), 0)
     chosen = jnp.where(slot == slots[...], 1.0, 0.0).astype(jnp.bfloat16)
-    total = None
-    for part, queries, inside, state in (
-        (0, queries_own, inside_own, state_own),
-        (1, queries_other, inside_other, state_other),
-    ):
-        mixed = []
-        for n in range(heads):
-            at = slice(n * HD, (n + 1) * HD)
-            carried = jnp.dot(queries[:, at], state[at, :], preferred_element_type=jnp.float32)
-            mixed.append(((inside[:, at] + carried) * unit).astype(jnp.bfloat16))
-        arrived(part)
-        added = jnp.dot(
-            jnp.concatenate(mixed, axis=1), weights_in[part], preferred_element_type=jnp.float32
-        )
-        total = added if total is None else total + added
-    arrived(2)
-    total += rows_in[...].astype(jnp.float32)
+    through = heads_through(queries, inside, state, first_position(own_rows), weight_in)
+    for fetch in fetches:
+        fetch.wait()
+    total = begun[...] + through()
     residual_out[:, :width] = total
     normed = normed_rows(total, gain[...]).astype(jnp.bfloat16)
     send_out[...] = jnp.dot(chosen, normed, preferred_element_type=jnp.float32).astype(
         jnp.bfloat16
     )
-    arrived(3)
+    fetch_router.wait()
     logits = jnp.dot(normed, router_in[...], preferred_element_type=jnp.float32)
     expert = lax.broadcasted_iota(jnp.int32, logits.shape, 1)
     logit = jnp.sum(jnp.where(expert == ids[...], logits, 0.0), axis=1, keepdims=True)
     residual_out[:, width:] = jnp.broadcast_to(jax.nn.sigmoid(logit), (own_rows, HD))
 
 
-def mix_heads(
-    part_own,
-    part_other,
-    state_own,
-    state_other,
-    out_own,
-    out_other,
-    series,
-    gain,
-    slots,
-    ids,
-    router,
-    slot_column,
-    slot_count,
-):
-    own_rows = slots.shape[1]
-    width = series.shape[1]
-    half = out_own.shape[0]
+def mix_heads(part, state, begun, out_weight, gain, slots, ids, router, slot_column, slot_count):
+    own_rows, width = begun.shape
     anywhere = pl.BlockSpec(memory_space=pl.ANY)
     local = pl.BlockSpec(memory_space=pltpu.VMEM)
     return pl.pallas_call(
         mix_kernel,
-        in_specs=[local] * 6 + [anywhere] * 3 + [local] * 3 + [anywhere] * 2,
+        in_specs=[local] * 4 + [anywhere] + [local] * 3 + [anywhere] * 2,
         out_specs=[local] * 2,
         out_shape=[
             pltpu.VMEM((own_rows, width + HD), jnp.float32),
             jax.ShapeDtypeStruct((slot_count, width), jnp.bfloat16),
         ],
         scratch_shapes=[
-            pltpu.VMEM((2, half, width), jnp.bfloat16),
-            pltpu.VMEM((own_rows, width), jnp.bfloat16),
+            pltpu.VMEM(out_weight.shape, jnp.bfloat16),
             pltpu.VMEM(router.shape, jnp.bfloat16),
-            pltpu.SemaphoreType.DMA((4, 2)),
+            pltpu.SemaphoreType.DMA((2, 2)),
         ],
         compiler_params=pltpu.CompilerParams(vmem_limit_bytes=24 * MIB),
         cost_estimate=pl.CostEstimate(
@@ -386,12 +400,10 @@
         ),
         name="mix_heads",
     )(
-        *(in_vmem(array) for array in (*part_own, *part_other)),
-        state_own,
-        state_other,
-        in_hbm(out_own),
-        in_hbm(out_other),
-        in_hbm(series),
+        *(in_vmem(array) for array in part),
+        state,
+        in_vmem(begun),
+        in_hbm(out_weight),
         gain,
         slots,
         ids,
@@ -477,17 +489,15 @@
     same_expert = route_ids[:, None] == route_ids[None, :]
     slot_rank = jnp.sum(jnp.logical_and(same_expert, earlier_row), axis=1)
     slot_index = route_ids * capacity + slot_rank
-
     slots = slot_index[None, :]
     slot_column = slot_index[:, None]
+
+    begun = mix_own(part_own, state_own.reshape(state.shape), out_weight, series[0])
     residual, send_buffer = mix_heads(
-        part_own,
         part_other,
-        state_own.reshape(state.shape),
         state_other.reshape(state.shape),
-        out_weight,
+        begun,
         out_other,
-        series[0],
         norm_moe,
         slots,
         route_ids[:, None],

time: 130 us -> 131 us (level)
    pallas_call x1 -> x2, Pallas kernels: 3.15 us -> 4.1 us  [the longest x1 2.48 us: mix_heads(): pl.pallas_call(mix_kernel, in_specs=[local] * 4 + [anywhere] + [local] *...]
  transfers between devices with their start and end apart: 8 -> 8, of which waited for: 2 -> 2; matrix products, arithmetic and copies ran while one was open for 1% -> 1% of each run, Pallas kernels for 11% -> 12%
where the time goes in v7:
time: 131 us
  blocking collectives  65.5 us (50%)
  Pallas kernels  27.8 us (21%)
  waiting for transfers between devices  18.2 us (14%)
  starting transfers between devices  17 us (13%)
  local copies, waits for them, and re-layouts  1.79 us (1%)
    all_to_all x2, blocking collectives, exchange(): return lax.all_to_all(pieces, axes, split_axis=0, concat_axis=0, tiled=True)  65.5 us
    all_to_all x2, waiting for transfers between devices, exchange(): return lax.all_to_all(pieces, axes, split_axis=0, concat_axis=0, tiled=True)  18.2 us
    all_to_all x2, starting transfers between devices, exchange(): return lax.all_to_all(pieces, axes, split_axis=0, concat_axis=0, tiled=True)  15.9 us
    pallas_call x1, Pallas kernels, expert_of(): pl.pallas_call(expert_kernel, in_specs=[local] + [pl.BlockSpec(memory_spa...  10.9 us
    pallas_call x2, Pallas kernels, inside_block(): pl.pallas_call(inside_kernel, in_specs=[local, pl.BlockSpec(memory_space=...  6.79 us
    pallas_call x1, Pallas kernels, block_state(): pl.pallas_call(state_kernel, in_specs=[pl.BlockSpec(memory_space=pl.ANY),...  3.86 us
  transfers between devices with their start and end apart: 8, of which 2 were waited for; matrix products, arithmetic and copies ran while one was open for 1% of the time, Pallas kernels for 12%

profile of v7, /device:TPU:32, one launch (start us, length us, event | category | flops | bytes accessed | tf_op | source)
XLA Modules:
  0.0 130.8 jit_solution(3159364198858463220)
XLA Ops:
  0.0 0.0 copy-start.1
  0.0 0.0 copy-start.3
  0.0 0.0 collective-permute-start
  0.0 3.9 %block_state.1 = (bf16[512,128]{1,0:T(8,128)(2,1)}, bf16[512,768]{1,0:T(8,128)(2,1)S(1)}) custom-call(bf16[512,768]{1,0:T(8,128)(2,1)} %bitcast.17, bf16[3,768,384]{2,1,0:T(8,128)(2,1)} %bitcast.20, f32[768]{0:T(1024)} %gain.2), custom_call_target="tpu_custom_call" | custom-call | flops 603979776 | bytes 1572864 | tf_op jit(solution)/shard_map/block_state/pallas_call | solution.py:168
  3.9 11.4 %all-to-all-start = ((bf16[32,16,128]{2,1,0:T(8,128)(2,1)}), bf16[32,16,128]{2,1,0:T(8,128)(2,1)S(1)}, u32[]{:S(2)}, u32[]{:S(2)}) async-start(bf16[32,16,128]{2,1,0:T(8,128)(2,1)} %bitcast.2), calls=%async_computation | async-start | bytes 262144 | tf_op jit(solution)/shard_map/all_to_all | solution.py:26
  15.3 0.0 copy-done.1
  15.3 0.1 collective-permute-start.2
  15.4 0.5 collective-permute-start.3
  15.9 0.1 collective-permute-start.4
  16.0 0.4 collective-permute-start.5
  16.4 0.0 copy-done.3
  16.4 0.2 convert_reduce_fusion
  16.6 8.9 %all-to-all-done.pieces = bf16[32,16,128]{2,1,0:T(8,128)(2,1)S(1)} async-done(((bf16[32,16,128]{2,1,0:T(8,128)(2,1)}), bf16[32,16,128]{2,1,0:T(8,128)(2,1)S(1)}, u32[]{:S(2)}, u32[]{:S(2)}) %all-to-all-start) | async-done | bytes 131104 | tf_op jit(solution)/shard_map/all_to_all | solution.py:26
  25.5 0.7 prefix.1
  26.2 4.6 %all-to-all-start.1 = ((bf16[32,16,128]{2,1,0:T(8,128)(2,1)}), bf16[32,16,128]{2,1,0:T(8,128)(2,1)S(1)}, u32[]{:S(2)}, u32[]{:S(2)}) async-start(bf16[32,16,128]{2,1,0:T(8,128)(2,1)} %prefix.1), calls=%async_computation.1 | async-start | bytes 262144 | tf_op jit(solution)/shard_map/all_to_all | solution.py:26
  30.7 0.1 copy.20.ids
  30.9 0.1 copy.19
  31.1 9.3 %all-to-all-done.1 = bf16[32,16,128]{2,1,0:T(8,128)(2,1)S(1)} async-done(((bf16[32,16,128]{2,1,0:T(8,128)(2,1)}), bf16[32,16,128]{2,1,0:T(8,128)(2,1)S(1)}, u32[]{:S(2)}, u32[]{:S(2)}) %all-to-all-start.1) | async-done | bytes 131104 | tf_op jit(solution)/shard_map/all_to_all | solution.py:26
  40.4 0.0 collective-permute-done.weight
  40.4 0.0 collective-permute-start.1
  40.4 3.4 %inside_block.3 = (bf16[256,384]{1,0:T(8,128)(2,1)S(1)}, f32[256,384]{1,0:T(8,128)S(1)}) custom-call(bf16[512,768]{1,0:T(8,128)(2,1)S(1)} %get-tuple-element.13.normed, bf16[3,768,384]{2,1,0:T(8,128)(2,1)} %bitcast.21), custom_call_target="tpu_custom_call" | custom-call | flops 956301312 | bytes 1572864 | tf_op jit(solution)/shard_map/inside_block/pallas_call | solution.py:253
  43.8 1.6 %mix_own.1.begun = f32[256,768]{1,0:T(8,128)S(1)} custom-call(bf16[256,384]{1,0:T(8,128)(2,1)S(1)} %get-tuple-element.17.queries, f32[256,384]{1,0:T(8,128)S(1)} %get-tuple-element.18.inside, bf16[512,128]{1,0:T(8,128)(2,1)S(1)} %bitcast.15, bf16[384,768]{1,0:T(8,128)(2,1)} %out_weight.1, bf16[512,768]{1,0:T(8,128)(2,1)} %bitcast.18), custom_call_target="tpu_custom_call" | custom-call | flops 176160768 | bytes 1572864 | tf_op jit(solution)/shard_map/mix_own/pallas_call | solution.py:317
  45.4 0.0 copy-start
  45.4 3.4 %inside_block.2 = (bf16[256,384]{1,0:T(8,128)(2,1)S(1)}, f32[256,384]{1,0:T(8,128)S(1)}) custom-call(bf16[512,768]{1,0:T(8,128)(2,1)S(1)} %get-tuple-element.13.normed, bf16[3,768,384]{2,1,0:T(8,128)(2,1)} %collective-permute-done.weight), custom_call_target="tpu_custom_call" | custom-call | flops 956301312 | bytes 1572864 | tf_op jit(solution)/shard_map/inside_block/pallas_call | solution.py:253
  48.8 0.0 collective-permute-done.2.out_weight
  48.8 0.0 copy-start.2
  48.8 0.0 collective-permute-done.1
  48.8 0.8 copy-done.2
  49.6 0.0 copy-done
  49.6 2.5 %mix_heads.1 = (f32[256,896]{1,0:T(8,128)S(1)}, bf16[512,768]{1,0:T(8,128)(2,1)S(1)}) custom-call(bf16[256,384]{1,0:T(8,128)(2,1)S(1)} %get-tuple-element.14.queries, f32[256,384]{1,0:T(8,128)S(1)} %get-tuple-element.15.inside, bf16[512,128]{1,0:T(8,128)(2,1)S(1)} %bitcast.16, f32[256,768]{1,0:T(8,128)S(1)} %mix_own.1.begun, bf16[384,768]{1,0:T(8,128)(2,1)} %copy-done.2, ...), custom_call_target="tpu_custom_call" | custom-call | flops 603979776 | bytes 2359296 | tf_op jit(solution)/shard_map/mix_heads/pallas_call | solution.py:382
  52.1 0.2 reshape.62
  52.3 34.4 %all_to_all.20 = bf16[128,4,768]{2,1,0:T(4,128)(2,1)S(1)} all-to-all(bf16[128,4,768]{2,1,0:T(4,128)(2,1)S(1)} %reshape.62), channel_id=1, replica_groups=mesh['seq_0'=8,'seq_1'=4,'head'=2,'dp'=4] {'seq_0','seq_1','dp'}, dimensions={0} | all-to-all | bytes 1572864 | tf_op jit(solution)/shard_map/all_to_all | solution.py:26
  86.7 0.2 reshape.63.rows
  86.9 0.0 collective-permute-done.3.gate_b
  86.9 0.0 collective-permute-done.4.up_b
  86.9 0.0 collective-permute-done.5.down_b
  86.9 10.9 %expert_mlp.1 = bf16[512,768]{1,0:T(8,128)(2,1)S(1)} custom-call(bf16[512,768]{1,0:T(8,128)(2,1)S(1)} %reshape.63.rows, bf16[768,1536]{1,0:T(8,128)(2,1)} %bitcast.27, bf16[768,1536]{1,0:T(8,128)(2,1)} %bitcast.29, bf16[1536,768]{1,0:T(8,128)(2,1)} %bitcast.31, bf16[768,1536]{1,0:T(8,128)(2,1)} %collective-permute-done.3.gate_b, ...), custom_call_target="tpu_custom_call" | custom-call | flops 7247757312 | bytes 14155776 | tf_op jit(solution)/shard_map/expert_mlp/pallas_call | solution.py:81
  97.9 0.2 reshape.64
  98.1 31.0 %all_to_all.21 = bf16[128,4,768]{2,1,0:T(4,128)(2,1)S(1)} all-to-all(bf16[128,4,768]{2,1,0:T(4,128)(2,1)S(1)} %reshape.64), channel_id=1, replica_groups=mesh['seq_0'=8,'seq_1'=4,'head'=2,'dp'=4] {'seq_0','seq_1','dp'}, dimensions={0} | all-to-all | bytes 1572864 | tf_op jit(solution)/shard_map/all_to_all | solution.py:26
  129.1 0.2 reshape.65.returned
  129.3 1.4 %combine.1 = bf16[256,768]{1,0:T(8,128)(2,1)} custom-call(bf16[512,768]{1,0:T(8,128)(2,1)S(1)} %reshape.65.returned, f32[256,896]{1,0:T(8,128)S(1)} %get-tuple-element.20.residual, s32[256,1]{1,0:T(8,128)S(1)} %multiply_add_fusion.slot_column.slots), custom_call_target="tpu_custom_call" | custom-call | flops 201326592 | bytes 1966080 | tf_op jit(solution)/shard_map/combine/pallas_call | solution.py:436
  (2 shorter events, 0.0 us)
Async XLA Ops:
  0.0 15.3 %copy-start.1 = (bf16[384,768]{1,0:T(8,128)(2,1)S(1)}, bf16[384,768]{1,0:T(8,128)(2,1)}, u32[]{:S(2)}) copy-start(bf16[384,768]{1,0:T(8,128)(2,1)} %out_weight.1) | copy-start | bytes 1769476
  0.0 16.4 %copy-start.3 = (s32[1,256,1]{1,2,0:T(1,128)S(1)}, s32[1,256,1]{1,2,0:T(1,128)}, u32[]{:S(2)}) copy-start(s32[1,256,1]{1,2,0:T(1,128)} %param.16) | copy-start | bytes 3076
  0.0 40.4 %collective-permute-start = (bf16[3,768,384]{2,1,0:T(8,128)(2,1)}, bf16[3,768,384]{2,1,0:T(8,128)(2,1)}, u32[]{:S(2)}, u32[]{:S(2)}) collective-permute-start(bf16[3,768,384]{2,1,0:T(8,128)(2,1)} %bitcast.19), channel_id=1, source_target_pairs={{0,4},{4,0},{1,5},{5,1},{2,6},{6,2},{3,7},{7,3},{8,12},{12,8},{9,1... | collective-permute-start | bytes 5308424 | tf_op jit(solution)/shard_map/ppermute | solution.py:22
  3.9 21.6 %all-to-all-start = ((bf16[32,16,128]{2,1,0:T(8,128)(2,1)}), bf16[32,16,128]{2,1,0:T(8,128)(2,1)S(1)}, u32[]{:S(2)}, u32[]{:S(2)}) async-start(bf16[32,16,128]{2,1,0:T(8,128)(2,1)} %bitcast.2), calls=%async_computation | async-start | bytes 262144 | tf_op jit(solution)/shard_map/all_to_all | solution.py:26
  15.3 33.5 %collective-permute-start.2 = (bf16[384,768]{1,0:T(8,128)(2,1)S(1)}, bf16[384,768]{1,0:T(8,128)(2,1)S(1)}, u32[]{:S(2)}, u32[]{:S(2)}) collective-permute-start(bf16[384,768]{1,0:T(8,128)(2,1)S(1)} %copy-done.1), channel_id=1, source_target_pairs={{0,4},{4,0},{1,5},{5,1},{2,6},{6,2},{3,7},{7,3},{8,12},{12,8},{9,1... | collective-permute-start | bytes 1769480 | tf_op jit(solution)/shard_map/ppermute | solution.py:22
  15.4 71.5 %collective-permute-start.3 = (bf16[768,1536]{1,0:T(8,128)(2,1)}, bf16[768,1536]{1,0:T(8,128)(2,1)}, u32[]{:S(2)}, u32[]{:S(2)}) collective-permute-start(bf16[768,1536]{1,0:T(8,128)(2,1)} %bitcast.26), channel_id=1, source_target_pairs={{0,4},{4,0},{1,5},{5,1},{2,6},{6,2},{3,7},{7,3},{8,12},{12,8},{9,1... | collective-permute-start | bytes 7077896 | tf_op jit(solution)/shard_map/ppermute | solution.py:22
  15.9 71.1 %collective-permute-start.4 = (bf16[768,1536]{1,0:T(8,128)(2,1)}, bf16[768,1536]{1,0:T(8,128)(2,1)}, u32[]{:S(2)}, u32[]{:S(2)}) collective-permute-start(bf16[768,1536]{1,0:T(8,128)(2,1)} %bitcast.28), channel_id=1, source_target_pairs={{0,4},{4,0},{1,5},{5,1},{2,6},{6,2},{3,7},{7,3},{8,12},{12,8},{9,1... | collective-permute-start | bytes 7077896 | tf_op jit(solution)/shard_map/ppermute | solution.py:22
  16.0 71.0 %collective-permute-start.5 = (bf16[1536,768]{1,0:T(8,128)(2,1)}, bf16[1536,768]{1,0:T(8,128)(2,1)}, u32[]{:S(2)}, u32[]{:S(2)}) collective-permute-start(bf16[1536,768]{1,0:T(8,128)(2,1)} %bitcast.30), channel_id=1, source_target_pairs={{0,4},{4,0},{1,5},{5,1},{2,6},{6,2},{3,7},{7,3},{8,12},{12,8},{9,1... | collective-permute-start | bytes 7077896 | tf_op jit(solution)/shard_map/ppermute | solution.py:22
  26.2 14.2 %all-to-all-start.1 = ((bf16[32,16,128]{2,1,0:T(8,128)(2,1)}), bf16[32,16,128]{2,1,0:T(8,128)(2,1)S(1)}, u32[]{:S(2)}, u32[]{:S(2)}) async-start(bf16[32,16,128]{2,1,0:T(8,128)(2,1)} %prefix.1), calls=%async_computation.1 | async-start | bytes 262144 | tf_op jit(solution)/shard_map/all_to_all | solution.py:26
  40.4 8.5 %collective-permute-start.1 = (bf16[32,16,128]{2,1,0:T(8,128)(2,1)S(1)}, bf16[32,16,128]{2,1,0:T(8,128)(2,1)S(1)}, u32[]{:S(2)}, u32[]{:S(2)}) collective-permute-start(bf16[32,16,128]{2,1,0:T(8,128)(2,1)S(1)} %all-to-all-done.1), channel_id=1, source_target_pairs={{0,4},{4,0},{1,5},{5,1},{2,6},{6,2},{3,7},{7,3},{8,12},{12,8},{9,1... | collective-permute-start | bytes 393224 | tf_op jit(solution)/shard_map/ppermute | solution.py:22
  45.4 4.2 %copy-start = (f32[768]{0:T(1024)S(1)}, f32[768]{0:T(1024)}, u32[]{:S(2)}) copy-start(f32[768]{0:T(1024)} %gain.3) | copy-start | bytes 9220
  48.8 0.8 copy-start.2
